TPU v7x, 32 devices: a whole 2x2x4 slice. The times are simulated.
32 devices in a mesh: seq: 32 (over z, y, x, core).
Axes of the slice: x: 2, y: 2, z: 4, core: 2. Of those that a mesh axis runs over, the one named last changes fastest.
Arguments:
- tokens: bfloat16 [5120, 2048], P('seq'), may hold values from -6 to 6
- cotangent: bfloat16 [5120, 2048], P('seq'), may hold values from -6 to 6
- gate_codes: int32 [5120, 256], P('seq'), may hold values from 256 to 4096, as said below
- lengths: int32 [4], replicated, may hold values from 1 to 2560, 5120 in all
- mixer_gain: bfloat16 [2048], P('seq'), may hold values from 0.099609375 to 1.8984375
- query_weight: bfloat16 [2048, 2048], P('seq'), may hold values from -0.125 to 0.125
- key_weight: bfloat16 [2048, 2048], P('seq'), may hold values from -0.125 to 0.125
- value_weight: bfloat16 [2048, 2048], P('seq'), may hold values from -0.125 to 0.125
- head_gain: bfloat16 [2048], P('seq'), may hold values from 0.099609375 to 1.8984375
- output_weight: bfloat16 [2048, 2048], P('seq'), may hold values from -0.125 to 0.125
- feed_gain: bfloat16 [2048], P('seq'), may hold values from 0.099609375 to 1.8984375
- gate_weight: bfloat16 [2048, 5632], P('seq'), may hold values from -0.125 to 0.125
- up_weight: bfloat16 [2048, 5632], P('seq'), may hold values from -0.125 to 0.125
- down_weight: bfloat16 [2048, 5632], P('seq'), may hold values from -0.078125 to 0.078125
Outputs:
- block_out: bfloat16 [5120, 2048], P('seq')
- input_grad: float32 [5120, 2048], P('seq')
- mixer_gain_grad: float32 [2048], P('seq')
- query_grad: float32 [2048, 2048], P('seq')
- key_grad: float32 [2048, 2048], P('seq')
- value_grad: float32 [2048, 2048], P('seq')
- head_gain_grad: float32 [2048], P('seq')
- output_weight_grad: float32 [2048, 2048], P('seq')
- feed_gain_grad: float32 [2048], P('seq')
- gate_grad: float32 [2048, 5632], P('seq')
- up_grad: float32 [2048, 5632], P('seq')
- down_grad: float32 [2048, 5632], P('seq')
Inputs may be any that keep to these rules, and one draw needn't show every extreme that they name: `gate_codes`: whole numbers, forget-gate logits of each token and each of the 4 x 64 slots, times 256. The 4 sequences lie one after another along the tokens; the lengths add up to 5120 and the longest is exactly 2560.
All inputs are finite; a program needn't handle non-finite values.
Results may differ from a plain program's by a relative error of at most 0.017.
The roundings to bfloat16 on the way count: a program that leaves them out, or rounds other values in their place, can miss the bound.
Values may be sent and summed in bfloat16 or wider, within the bound.
A program may use at most 504 MiB of HBM per device.

v0:
```python
import jax
import jax.numpy as jnp
from jax import lax
from jax.sharding import PartitionSpec as P

HEADS = 4
SLOTS = 64


epsilon = 1e-06
highest = lax.Precision.HIGHEST
contract_last = (((1,), (1,)), ((), ()))
contract_first = (((0,), (0,)), ((), ()))


def entering(shard, axis, combine, identity):
    devices, index = (lax.axis_size(axis), lax.axis_index(axis))
    everything = jax.tree.map(lambda part: lax.all_gather(part, axis), shard)
    start = jax.tree.map(
        lambda part, zero: jnp.broadcast_to(jnp.asarray(zero, part.dtype), part.shape),
        shard,
        identity,
    )

    def entering_step(k, before):
        reached = k < index
        new = combine(before, jax.tree.map(lambda part: part[k], everything))
        return jax.tree.map(lambda a, b: jnp.where(reached, a, b), new, before)

    return lax.fori_loop(0, devices, entering_step, start)


def carried_in(shard, axis, combine, identity):
    devices, index = (lax.axis_size(axis), lax.axis_index(axis))
    everything = jax.tree.map(
        lambda part, kind: lax.all_gather(part.astype(kind), axis),
        shard,
        (jnp.bfloat16, jnp.bfloat16),
    )
    start = jax.tree.map(
        lambda part, zero: jnp.broadcast_to(jnp.asarray(zero, part.dtype), part.shape),
        shard,
        identity,
    )

    def carried_step(k, before):
        at = devices - 1 - k
        reached = at > index
        new = combine(
            before, jax.tree.map(lambda part, own: part[at].astype(own.dtype), everything, shard)
        )
        return jax.tree.map(lambda a, b: jnp.where(reached, a, b), new, before)

    return lax.fori_loop(0, devices, carried_step, start)


def rms_factor(value_rows):
    return lax.rsqrt(jnp.mean(value_rows * value_rows, axis=-1, keepdims=True) + epsilon)


def precise_result(form, left, right):
    return jnp.einsum(form, left, right, precision=highest, preferred_element_type=jnp.float32)


def plain_result(form, left, right):
    return jnp.einsum(form, left, right, preferred_element_type=jnp.float32)


def chain_join(earlier, later):
    return (earlier[0] * later[0], later[0][..., None] * earlier[1] + later[1])


def block_tables(decay, starts):
    count = jnp.cumsum(starts)
    length = decay.shape[0]
    places = jnp.arange(length)
    before = places[:, None] >= places[None, :]
    same = jnp.where(before & (count[:, None] == count[None, :]), 1.0, 0.0).astype(jnp.float32)
    fresh_state = jnp.where(count == 0, 1.0, 0.0).astype(jnp.float32)
    logsum = jnp.cumsum(decay, axis=0)
    growth_factor = jnp.exp(logsum)
    backward_pass = jnp.exp(-logsum) * -jnp.expm1(decay)
    tail = jnp.where(count == count[-1], 1.0, 0.0).astype(jnp.float32)
    weight_matrix = growth_factor[-1][None] * backward_pass * tail[:, None, None]
    carried_state = fresh_state[-1] * growth_factor[-1]
    return (same, fresh_state, growth_factor, backward_pass, weight_matrix, carried_state)


def local(
    tokens,
    cotangent,
    gate_codes,
    lengths,
    mixer_gain,
    query_weight,
    key_weight,
    value_weight,
    head_gain,
    output_weight,
    feed_gain,
    gate_weight,
    up_weight,
    down_weight,
):
    local_rows = tokens.shape[0]
    width = tokens.shape[1]
    head_size = width // HEADS
    hidden_width = gate_weight.shape[1]
    tokens_f = tokens.astype(jnp.float32)
    factor_one = rms_factor(tokens_f)
    normed_one = tokens_f * factor_one
    position = lax.axis_index("seq") * local_rows + jnp.arange(local_rows, dtype=jnp.int32)
    first_token = jnp.cumsum(lengths) - lengths
    starts = jnp.sum(jnp.where(position[:, None] == first_token[None, :], 1, 0), axis=1).astype(
        jnp.int32
    )
    decay = jax.nn.log_sigmoid(gate_codes.astype(jnp.float32) / 256.0).reshape(
        local_rows, HEADS, SLOTS
    )
    same, fresh_state, growth_factor, backward_pass, weight_matrix, carried_state = block_tables(
        decay, starts
    )
    piece_a = lax.all_gather(mixer_gain, "seq", axis=0, tiled=True)
    piece_b = lax.all_gather(head_gain, "seq", axis=0, tiled=True)
    piece_c = lax.all_gather(feed_gain, "seq", axis=0, tiled=True)
    piece_query = lax.all_gather(query_weight, "seq", axis=0, tiled=True)
    piece_key = lax.all_gather(key_weight, "seq", axis=0, tiled=True)
    piece_value = lax.all_gather(value_weight, "seq", axis=0, tiled=True)
    section = (normed_one * piece_a.astype(jnp.float32)[None, :]).astype(jnp.bfloat16)
    normed_b = section
    query_acc = jnp.dot(section, piece_query, preferred_element_type=jnp.float32)
    key_acc = jnp.dot(section, piece_key, preferred_element_type=jnp.float32)
    value_acc = jnp.dot(section, piece_value, preferred_element_type=jnp.float32)
    heads_shape = (local_rows, HEADS, head_size)
    query_rows = query_acc.astype(jnp.bfloat16).reshape(heads_shape)
    key_rows = key_acc.astype(jnp.bfloat16).reshape(heads_shape)
    value_rows = value_acc.astype(jnp.bfloat16).reshape(heads_shape)
    query_float = query_rows.astype(jnp.float32)
    local_state = jnp.concatenate(
        [
            precise_result("oft,ofi->fti", weight_matrix, key_rows.astype(jnp.float32)),
            precise_result("oft,ofi->fti", weight_matrix, value_rows.astype(jnp.float32)),
        ],
        axis=-1,
    )
    unit = jnp.ones_like(carried_state)
    blank = jnp.zeros_like(local_state)
    gain_in, state_in = entering((carried_state, local_state), "seq", chain_join, (unit, blank))
    running_key_state = state_in[..., :head_size]
    running_value_state = state_in[..., head_size:]
    affinity = plain_result("thd,shd->hts", query_rows, key_rows)
    masked_scores = affinity * same[None]
    score_matrix = growth_factor * precise_result(
        "ynf,fye->nye", masked_scores, backward_pass
    ) + growth_factor * fresh_state[:, None, None] * precise_result(
        "egr,gjr->egj", query_float, running_key_state
    )
    probs = jax.nn.softmax(score_matrix, axis=-1)
    lifted = probs * growth_factor
    mixing_matrix = (precise_result("thm,shm->hts", lifted, backward_pass) * same[None]).astype(
        jnp.bfloat16
    )
    entry_point = lifted * fresh_state[:, None, None]
    slot_output = plain_result("via,avj->ivj", mixing_matrix, value_rows) + precise_result(
        "xfj,fjg->xfg", entry_point, running_value_state
    )
    head_factor = rms_factor(slot_output)
    unit_heads = slot_output * head_factor
    head_gain_f = piece_b.astype(jnp.float32).reshape(HEADS, head_size)
    normed_heads = (unit_heads * head_gain_f).astype(jnp.bfloat16).reshape(local_rows, width)
    mixed = jnp.dot(
        normed_heads,
        lax.all_gather(output_weight, "seq", axis=0, tiled=True),
        preferred_element_type=jnp.float32,
    )
    residual = tokens_f + mixed
    factor_two = rms_factor(residual)
    normed_two = residual * factor_two
    feed_input = (normed_two * piece_c.astype(jnp.float32)).astype(jnp.bfloat16)
    pieces = (
        lax.all_gather(gate_weight, "seq", axis=0, tiled=True),
        lax.all_gather(up_weight, "seq", axis=0, tiled=True),
    )
    section = feed_input
    gate = jnp.dot(section, pieces[0], preferred_element_type=jnp.float32)
    upward = jnp.dot(section, pieces[1], preferred_element_type=jnp.float32)
    sigma = jax.nn.sigmoid(gate)
    active = gate * sigma
    hidden = (active * upward).astype(jnp.bfloat16)
    feed_out = lax.dot_general(
        hidden,
        lax.all_gather(down_weight, "seq", axis=0, tiled=True),
        contract_last,
        preferred_element_type=jnp.float32,
    )
    block_out = (residual + feed_out).astype(jnp.bfloat16)
    cotangent_f = cotangent.astype(jnp.float32)
    hidden_grad = jnp.dot(
        cotangent,
        lax.all_gather(down_weight, "seq", axis=0, tiled=True),
        preferred_element_type=jnp.float32,
    )
    gate_back = (hidden_grad * upward * sigma * (1.0 + gate * (1.0 - sigma))).astype(jnp.bfloat16)
    up_back = (hidden_grad * active).astype(jnp.bfloat16)
    pieces = lax.all_gather((gate_weight, up_weight), "seq", axis=0, tiled=True)
    feed_in_grad = lax.dot_general(
        gate_back, pieces[0], contract_last, preferred_element_type=jnp.float32
    ) + lax.dot_general(up_back, pieces[1], contract_last, preferred_element_type=jnp.float32)
    feed_grads = jnp.concatenate([gate_back, up_back], axis=1)
    feed_sums = lax.psum_scatter(
        jnp.concatenate(
            [
                lax.dot_general(
                    feed_input, feed_grads, contract_first, preferred_element_type=jnp.float32
                ),
                lax.dot_general(
                    cotangent, hidden, contract_first, preferred_element_type=jnp.float32
                ),
            ],
            axis=1,
        ),
        "seq",
        scatter_dimension=0,
        tiled=True,
    )
    feed_gain_part = jnp.sum(normed_two * feed_in_grad, axis=0)
    scaled_two = feed_in_grad * piece_c.astype(jnp.float32)
    residual_grad = cotangent_f + factor_two * (
        scaled_two - normed_two * jnp.mean(normed_two * scaled_two, axis=-1, keepdims=True)
    )
    mixed_grad = residual_grad.astype(jnp.bfloat16)
    heads_grad = lax.dot_general(
        mixed_grad,
        lax.all_gather(output_weight, "seq", axis=0, tiled=True),
        contract_last,
        preferred_element_type=jnp.float32,
    ).reshape(heads_shape)
    head_gain_part = jnp.sum(unit_heads * heads_grad, axis=0).reshape(width)
    scaled_heads = heads_grad * head_gain_f
    out_back = (
        head_factor
        * (scaled_heads - unit_heads * jnp.mean(unit_heads * scaled_heads, axis=-1, keepdims=True))
    ).astype(jnp.bfloat16)
    output_backward_float = out_back.astype(jnp.float32)
    mixing_grad = plain_result("thd,shd->hts", out_back, value_rows)
    local_value = plain_result("hts,thd->shd", mixing_matrix, out_back)
    leading_value = precise_result("ixn,ixb->xnb", entry_point, output_backward_float)
    lifted_grad = growth_factor * precise_result(
        "ynf,fye->nye", mixing_grad * same[None], backward_pass
    ) + growth_factor * fresh_state[:, None, None] * precise_result(
        "egr,gjr->egj", output_backward_float, running_value_state
    )
    score_grad = probs * (lifted_grad - jnp.sum(probs * lifted_grad, axis=-1, keepdims=True))
    inner_grad = growth_factor * score_grad
    state_gradient = inner_grad * fresh_state[:, None, None]
    affinity_grad = (precise_result("thm,shm->hts", inner_grad, backward_pass) * same[None]).astype(
        jnp.bfloat16
    )
    leading_key = precise_result("ixn,ixb->xnb", state_gradient, query_float)
    back_state = jnp.concatenate([leading_key, leading_value], axis=-1)
    gain_out, later_grad = carried_in((carried_state, back_state), "seq", chain_join, (unit, blank))
    subsequent_key = later_grad[..., :head_size]
    subsequent_value = later_grad[..., head_size:]
    query_back = (
        (
            plain_result("via,avj->ivj", affinity_grad, key_rows)
            + precise_result("xfj,fjg->xfg", state_gradient, running_key_state)
        )
        .astype(jnp.bfloat16)
        .reshape(local_rows, width)
    )
    key_back = (
        (
            plain_result("hts,thd->shd", affinity_grad, query_rows)
            + precise_result("pzo,zot->pzt", weight_matrix, subsequent_key)
        )
        .astype(jnp.bfloat16)
        .reshape(local_rows, width)
    )
    value_back = (
        (local_value + precise_result("pzo,zot->pzt", weight_matrix, subsequent_value))
        .astype(jnp.bfloat16)
        .reshape(local_rows, width)
    )
    pieces = lax.all_gather((query_weight, key_weight, value_weight), "seq", axis=0, tiled=True)
    mixer_in_grad = (
        lax.dot_general(query_back, pieces[0], contract_last, preferred_element_type=jnp.float32)
        + lax.dot_general(key_back, pieces[1], contract_last, preferred_element_type=jnp.float32)
        + lax.dot_general(value_back, pieces[2], contract_last, preferred_element_type=jnp.float32)
    )
    mixer_gain_part = jnp.sum(normed_one * mixer_in_grad, axis=0)
    scaled_one = mixer_in_grad * piece_a.astype(jnp.float32)
    input_grad = residual_grad + factor_one * (
        scaled_one - normed_one * jnp.mean(normed_one * scaled_one, axis=-1, keepdims=True)
    )
    projection_grads = jnp.concatenate([query_back, key_back, value_back], axis=1)
    mixer_sums = lax.psum_scatter(
        jnp.concatenate(
            [
                lax.dot_general(
                    normed_b, projection_grads, contract_first, preferred_element_type=jnp.float32
                ),
                lax.dot_general(
                    normed_heads, mixed_grad, contract_first, preferred_element_type=jnp.float32
                ),
            ],
            axis=1,
        ),
        "seq",
        scatter_dimension=0,
        tiled=True,
    )
    gain_sums = (
        lax.psum_scatter(mixer_gain_part, "seq", scatter_dimension=0, tiled=True),
        lax.psum_scatter(head_gain_part, "seq", scatter_dimension=0, tiled=True),
        lax.psum_scatter(feed_gain_part, "seq", scatter_dimension=0, tiled=True),
    )
    return (
        block_out,
        input_grad,
        gain_sums[0],
        mixer_sums[:, :width],
        mixer_sums[:, width : 2 * width],
        mixer_sums[:, 2 * width : 3 * width],
        gain_sums[1],
        mixer_sums[:, 3 * width :],
        gain_sums[2],
        feed_sums[:, :hidden_width],
        feed_sums[:, hidden_width : 2 * hidden_width],
        feed_sums[:, 2 * hidden_width :],
    )


def solution(mesh):
    return jax.shard_map(
        local,
        mesh=mesh,
        in_specs=(
            P("seq", None),
            P("seq", None),
            P("seq", None),
            P(),
            P("seq"),
            P("seq", None),
            P("seq", None),
            P("seq", None),
            P("seq"),
            P("seq", None),
            P("seq"),
            P("seq", None),
            P("seq", None),
            P("seq", None),
        ),
        out_specs=(
            P("seq", None),
            P("seq", None),
            P("seq"),
            P("seq", None),
            P("seq", None),
            P("seq", None),
            P("seq"),
            P("seq", None),
            P("seq"),
            P("seq", None),
            P("seq", None),
            P("seq", None),
        ),
        check_vma=False,
    )
```

profile of v0, /device:TPU:0, one launch (start us, length us, event | category | flops | bytes accessed | tf_op | source)
XLA Modules:
  0.0 3823.7 jit_solution(6796610249351785658)
XLA Ops:
  13.5 2.4 reduce-window.30
  21.5 42.7 %all-reduce.10 = (bf16[2048]{0:T(1024)(128)(2,1)S(1)}, bf16[2048]{0:T(1024)(128)(2,1)S(1)}, bf16[2048]{0:T(1024)(128)(2,1)S(1)}) all-reduce(bf16[2048]{0:T(1024)(128)(2,1)S(1)} %dynamic-update-slice, bf16[2048]{0:T(1024)(128)(2,1)S(1)} %dynamic-update-slice.1, bf16[2048]{0:T(1024)(128)(2,1)S(1)} %dynamic-update-slice.2), channel_id=1, replica_groups=mesh['seq'=32] {'seq'}, use_global_device_ids=true, to_apply=%add.2 | all-reduce | flops 6144 | bytes 24576
  64.4 26.6 all-gather.11.cloned.1.call-done
  91.0 4.9 convolution_convert_fusion.2
  96.4 73.9 %all-gather.15.cloned.1.call-done = bf16[2048,2048]{1,0:T(8,128)(2,1)} async-done(((bf16[64,2048]{1,0:T(8,128)(2,1)}), bf16[2048,2048]{1,0:T(8,128)(2,1)}) %all-gather.15.cloned.1.call-update) | async-done | bytes 8388624 | tf_op jit(solution)/shard_map/all_gather | solution.py:127
  170.3 4.9 convolution_convert_fusion
  179.7 39.6 %all_gather.59 = f32[32,4,64]{2,1,0:T(4,128)S(1)} all-gather(f32[1,4,64]{2,1,0:T(4,128)S(1)} %get-tuple-element.329), channel_id=1, replica_groups=mesh['seq'=32] {'seq'}, dimensions={0}, use_global_device_ids=true | all-gather | bytes 33792 | tf_op jit(solution)/shard_map/all_gather | solution.py:18
  219.4 29.8 all-gather.13.cloned.1.call-done
  249.2 5.0 convolution_convert_fusion.1
  256.1 1.9 copy.161
  258.0 187.9 %all-gather.27.cloned.1.call-done = f32[128,64,1024]{2,1,0:T(8,128)} async-done(((f32[4,64,1024]{2,1,0:T(8,128)}), f32[128,64,1024]{2,1,0:T(8,128)}) %all-gather.27.cloned.1.call-update) | async-done | bytes 33554448 | tf_op jit(solution)/shard_map/all_gather | solution.py:18
  445.9 48.4 %while.30 = (s32[]{:T(128)}, f32[4,64,1024]{2,1,0:T(8,128)S(1)}, s32[]{:T(128)}, f32[32,4,64]{2,1,0:T(4,128)S(1)}, f32[32,4,64,1024]{3,2,1,0:T(8,128)}, /*index=5*/s32[]{:T(128)}, s32[]{:T(128)}) while((s32[]{:T(128)}, f32[4,64,1024]{2,1,0:T(8,128)S(1)}, s32[]{:T(128)}, f32[32,4,64]{2,1,0:T(4,128)S(1)}, ...), condition=%wide.region_8.9_spmd.clone, body=%wide.region_7.8_spmd.clone.sunk | while | flops 1048580 | bytes 3148913 | solution.py:30
  453.7 1.5 fusion.165
  495.8 1.9 copy.167
  497.7 1.9 fusion.102
  502.1 1.7 fusion.36
  507.7 16.5 all-gather.17.cloned.1.call-done
  524.3 5.3 multiply_reduce_fusion.3
  529.8 140.5 %all-gather.19.cloned.1.call-done = bf16[2048,5632]{1,0:T(8,128)(2,1)} async-done(((bf16[64,5632]{1,0:T(8,128)(2,1)}), bf16[2048,5632]{1,0:T(8,128)(2,1)}) %all-gather.19.cloned.1.call-update) | async-done | bytes 23068688 | tf_op jit(solution)/shard_map/all_gather | solution.py:181
  670.3 11.5 fusion.106
  681.7 134.2 %all-gather.21.cloned.1.call-done = bf16[2048,5632]{1,0:T(8,128)(2,1)} async-done(((bf16[64,5632]{1,0:T(8,128)(2,1)}), bf16[2048,5632]{1,0:T(8,128)(2,1)}) %all-gather.21.cloned.1.call-update) | async-done | bytes 23068688 | tf_op jit(solution)/shard_map/all_gather | solution.py:182
  815.9 11.5 fusion.107
  827.5 134.1 %all-gather.23.cloned.1.call-done = bf16[2048,5632]{1,0:T(8,128)(2,1)} async-done(((bf16[64,5632]{1,0:T(8,128)(2,1)}), bf16[2048,5632]{1,0:T(8,128)(2,1)}) %all-gather.23.cloned.1.call-update) | async-done | bytes 23068688 | tf_op jit(solution)/shard_map/all_gather | solution.py:192
  961.6 14.1 multiply_convert_fusion
  975.7 13.7 fusion.108
  989.4 14.3 multiply_reduce_fusion
  1003.8 1.9 multiply_add_fusion
  1005.7 6.8 fusion.84
  1017.8 9.2 broadcast_multiply_fusion
  1029.5 20.3 convolution_bitcast_fusion
  1049.8 33.8 fusion.4
  1083.6 90.8 %pad_maximum_fusion = f32[2048,16896]{1,0:T(8,128)} fusion(f32[2048,5632]{1,0:T(8,128)} %convolution_bitcast_fusion, f32[2048,11264]{1,0:T(8,128)} %fusion.4), kind=kLoop, calls=%fused_computation.8 | loop fusion | flops 34603008 | bytes 276824064 | tf_op jit(solution)/shard_map/concatenate | solution.py:211
  1175.1 39.7 %all_gather.68 = bf16[32,4,64]{2,1,0:T(4,128)(2,1)S(1)} all-gather(bf16[1,4,64]{2,1,0:T(4,128)(2,1)S(1)} %copy-done.50), channel_id=1, replica_groups=mesh['seq'=32] {'seq'}, dimensions={0}, use_global_device_ids=true | all-gather | bytes 16896 | tf_op jit(solution)/shard_map/all_gather | solution.py:36
  1222.6 9.5 fusion.82
  1232.2 44.0 %while.31 = (s32[]{:T(128)}, f32[4,64,1024]{2,1,0:T(8,128)S(1)}, s32[]{:T(128)}, bf16[32,4,64]{2,1,0:T(4,128)(2,1)S(1)}, bf16[32,4,64,1024]{3,2,1,0:T(8,128)(2,1...) while((s32[]{:T(128)}, f32[4,64,1024]{2,1,0:T(8,128)S(1)}, s32[]{:T(128)}, ...), condition=%wide.region_17.18_spmd.clone, body=%wide.region_16.17_spmd.clone.sunk | while | flops 1310984 | bytes 2624175 | solution.py:54
  1276.1 2.6 fusion.33
  1282.9 21.7 fusion.10
  1304.6 46.5 %pad_maximum_fusion.1 = f32[2048,8192]{1,0:T(8,128)} fusion(f32[2048,2048]{1,0:T(8,128)} %fusion.82, f32[2048,6144]{1,0:T(8,128)} %fusion.10), kind=kLoop, calls=%fused_computation.9 | loop fusion | flops 16777216 | bytes 134217728 | tf_op jit(solution)/shard_map/concatenate | solution.py:298
  1351.8 7.5 fusion.110
  1359.3 14.1 fusion.9
  1373.5 7.0 convolution_add_fusion.3
  1380.5 7.6 fusion.29
  1388.1 38.5 %all-reduce.9 = (f32[2048]{0:T(1024)S(1)}, f32[2048]{0:T(1024)S(1)}, f32[2048]{0:T(1024)S(1)}) all-reduce(f32[2048]{0:T(1024)S(1)} %get-tuple-element.300, f32[2048]{0:T(1024)S(1)} %bitcast.223, f32[2048]{0:T(1024)S(1)} %copy-done.48), channel_id=3, replica_groups=mesh['seq'=32] {'seq'}, use_global_device_ids=true, to_apply=%region_20.21.clone | all-reduce | flops 6144 | bytes 49152
  1428.3 2.7 fusion.28
  1431.0 1676.9 %all-reduce.13.cloned.1.call-done = f32[2048,16896]{1,0:T(8,128)} async-done(((f32[2048,16896]{1,0:T(8,128)}), f32[2048,16896]{1,0:T(8,128)}) %all-reduce.13.cloned.1.call-update) | async-done | bytes 138412048
  3107.9 5.1 fusion.100
  3113.0 700.9 %reduce-scatter.2.cloned.1.call-done = f32[64,8192]{1,0:T(8,128)} async-done(((f32[2048,8192]{1,0:T(8,128)}), f32[64,8192]{1,0:T(8,128)}) %reduce-scatter.2.cloned.1.call-update) | async-done | bytes 2097168 | tf_op jit(solution)/shard_map/reduce_scatter | solution.py:297
  3813.9 2.9 fusion.101
  (341 shorter events, 137.4 us)
Async XLA Ops:
  7.2 83.9 %all-gather.11.cloned.1.call-start = ((), (), s32[]{:S(2)}) async-start(), calls=%async_computation.1 | async-start | bytes 8650752 | tf_op jit(solution)/shard_map/all_gather | solution.py:128
  7.9 162.4 %all-gather.15.cloned.1.call-start = ((), (), s32[]{:S(2)}) async-start(), calls=%async_computation.3 | async-start | bytes 8650752 | tf_op jit(solution)/shard_map/all_gather | solution.py:127
  8.7 240.6 %all-gather.13.cloned.1.call-start = ((), (), s32[]{:S(2)}) async-start(), calls=%async_computation.2 | async-start | bytes 8650752 | tf_op jit(solution)/shard_map/all_gather | solution.py:126
  9.4 436.5 %all-gather.27.cloned.1.call-start = ((), (), s32[]{:S(2)}) async-start(), calls=%async_computation.10 | async-start | bytes 34603008 | tf_op jit(solution)/shard_map/all_gather | solution.py:18
  16.6 4.0 copy-start.26
  18.1 2.7 copy-start.51
  18.1 3.0 copy-start.52
  18.1 3.2 copy-start.53
  18.1 46.1 %copy-start.8 = (bf16[160,2048]{1,0:T(8,128)(2,1)S(1)}, bf16[160,2048]{1,0:T(8,128)(2,1)}, u32[]{:S(2)}) copy-start(bf16[160,2048]{1,0:T(8,128)(2,1)} %param.18) | copy-start | bytes 1966084
  20.7 154.5 %copy-start.16 = (f32[160,4,64]{0,2,1:T(8,128)}, f32[160,4,64]{0,2,1:T(8,128)S(1)}, u32[]{:S(2)}) copy-start(f32[160,4,64]{0,2,1:T(8,128)S(1)} %copy.162) | copy-start | bytes 491524
  64.2 185.1 %copy-start.42 = (f32[2048]{0:T(1024)}, f32[2048]{0:T(1024)S(1)}, u32[]{:S(2)}) copy-start(f32[2048]{0:T(1024)S(1)} %convert_element_type.125) | copy-start | bytes 24580
  64.4 184.8 %copy-start.46 = (f32[160]{0:T(256)}, f32[160]{0:T(256)S(1)}, u32[]{:S(2)}) copy-start(f32[160]{0:T(256)S(1)} %add_rsqrt_fusion.2) | copy-start | bytes 1924
  96.0 407.8 %copy-start.23 = (bf16[160,2048]{1,0:T(8,128)(2,1)}, bf16[160,2048]{1,0:T(8,128)(2,1)S(1)}, u32[]{:S(2)}) copy-start(bf16[160,2048]{1,0:T(8,128)(2,1)S(1)} %convolution_convert_fusion.2) | copy-start | bytes 1966084
  175.2 1.5 copy-start.31
  176.7 2.7 copy-start.41
  176.8 347.5 %all-gather.17.cloned.1.call-start = ((), (), s32[]{:S(2)}) async-start(), calls=%async_computation.4 | async-start | bytes 8650752 | tf_op jit(solution)/shard_map/all_gather | solution.py:173
  177.3 492.9 %all-gather.19.cloned.1.call-start = ((), (), s32[]{:S(2)}) async-start(), calls=%async_computation.5 | async-start | bytes 23789568 | tf_op jit(solution)/shard_map/all_gather | solution.py:181
  177.9 638.0 %all-gather.21.cloned.1.call-start = ((), (), s32[]{:S(2)}) async-start(), calls=%async_computation.6 | async-start | bytes 23789568 | tf_op jit(solution)/shard_map/all_gather | solution.py:182
  178.7 782.9 %all-gather.23.cloned.1.call-start = ((), (), s32[]{:S(2)}) async-start(), calls=%async_computation.7 | async-start | bytes 23789568 | tf_op jit(solution)/shard_map/all_gather | solution.py:192
  179.4 1052.7 %all-gather.25.cloned.1.call-start = ((), (), s32[]{:S(2)}) async-start(), calls=%async_computation.8 | async-start | bytes 17301504 | tf_op jit(solution)/shard_map/all_gather | solution.py:36
  179.7 837.1 %copy-start.14 = (f32[160,4,64]{0,2,1:T(8,128)}, f32[160,4,64]{0,2,1:T(8,128)S(1)}, u32[]{:S(2)}) copy-start(f32[160,4,64]{0,2,1:T(8,128)S(1)} %copy.160) | copy-start | bytes 491524
  219.4 795.3 %copy-start.34 = (f32[160,160]{1,0:T(8,128)}, f32[160,160]{1,0:T(8,128)S(1)}, u32[]{:S(2)}) copy-start(f32[160,160]{1,0:T(8,128)S(1)} %fusion.89) | copy-start | bytes 307204
  249.2 5.0 copy-start.32
  254.3 240.1 %copy-start.20 = (bf16[160,2048]{1,0:T(8,128)(2,1)}, bf16[160,2048]{1,0:T(8,128)(2,1)S(1)}, u32[]{:S(2)}) copy-start(bf16[160,2048]{1,0:T(8,128)(2,1)S(1)} %convolution_convert_fusion.1) | copy-start | bytes 1966084
  494.3 519.5 %copy-start = (f32[4,64,1024]{2,1,0:T(8,128)}, f32[4,64,1024]{2,1,0:T(8,128)S(1)}, u32[]{:S(2)}) copy-start(f32[4,64,1024]{2,1,0:T(8,128)S(1)} %get-tuple-element.238) | copy-start | bytes 3145732
  495.8 3.8 copy-start.27
  502.1 2.1 copy-start.36
  503.8 1.8 copy-start.29
  529.6 474.2 %copy-start.2 = (f32[160,2048]{1,0:T(8,128)}, f32[160,2048]{1,0:T(8,128)S(1)}, u32[]{:S(2)}) copy-start(f32[160,2048]{1,0:T(8,128)S(1)} %get-tuple-element.352) | copy-start | bytes 3932164
  975.7 13.7 copy-start.40
  1005.7 6.8 copy-start.6
  1005.7 6.8 copy-start.5
  1013.9 1.7 copy-start.10
  1017.8 10.3 copy-start.21
  1029.5 2078.4 %all-reduce.13.cloned.1.call-start = ((), (), s32[]{:S(2)}) async-start(), calls=%async_computation.11 | async-start | bytes 276824064
  1029.5 20.3 copy-start.12
  1174.4 40.4 %copy-start.15 = (f32[160,4,64]{0,2,1:T(8,128)S(1)}, f32[160,4,64]{0,2,1:T(8,128)}, u32[]{:S(2)}) copy-start(f32[160,4,64]{0,2,1:T(8,128)} %copy-done.14) | copy-start | bytes 491524
  1174.4 40.4 %copy-start.35 = (f32[160,160]{1,0:T(8,128)S(1)}, f32[160,160]{1,0:T(8,128)}, u32[]{:S(2)}) copy-start(f32[160,160]{1,0:T(8,128)} %copy-done.34) | copy-start | bytes 307204
  1174.4 40.4 %copy-start.44 = (f32[160,4,64]{2,1,0:T(4,128)S(1)}, f32[160,4,64]{2,1,0:T(4,128)}, u32[]{:S(2)}) copy-start(f32[160,4,64]{2,1,0:T(4,128)} %get-tuple-element.355) | copy-start | bytes 491524
  1174.4 41.0 %copy-start.33 = (bf16[160,2048]{1,0:T(8,128)(2,1)S(1)}, bf16[160,2048]{1,0:T(8,128)(2,1)}, u32[]{:S(2)}) copy-start(bf16[160,2048]{1,0:T(8,128)(2,1)} %copy-done.31) | copy-start | bytes 1966084
  1174.5 2639.4 %reduce-scatter.2.cloned.1.call-start = ((), (), s32[]{:S(2)}) async-start(), calls=%async_computation.9 | async-start | bytes 69206016 | tf_op jit(solution)/shard_map/reduce_scatter | solution.py:297
  1220.6 2.0 copy-start.13
  1232.1 44.0 %copy-start.17 = (f32[160,4,64]{0,2,1:T(8,128)S(1)}, f32[160,4,64]{0,2,1:T(8,128)}, u32[]{:S(2)}) copy-start(f32[160,4,64]{0,2,1:T(8,128)} %copy-done.16) | copy-start | bytes 491524
  1278.7 1.6 copy-start.25
  1351.8 7.6 copy-start.3
  1359.3 14.1 copy-start.19
  1373.5 7.0 copy-start.18
  1380.5 7.6 copy-start.48
  (17 other events, 20.4 us)
Sparse Core Ops, SparseCore 0:
  10.9 80.1 all-gather.10
  93.9 76.3 all-gather.14
  173.1 76.0 all-gather.12
  252.5 193.3 all-gather.26
  448.6 75.6 all-gather.16
  527.0 143.2 all-gather.18
  673.1 142.7 all-gather.20
  818.8 142.7 all-gather.22
  1029.6 113.0 all-gather.24
  1174.6 1933.2 all-reduce.12
  3110.3 703.5 reduce-scatter.1
where the time goes:
time: 3840 us; the launch traced here: 3820 us
  waiting for transfers between devices  3130 us (82%)
  other arithmetic  255 us (7%)
  matrix products  233 us (6%)
  blocking collectives  160 us (4%)
    unnamed x12, waiting for transfers between devices  1680 us
    reduce_scatter x1, waiting for transfers between devices, local(): lax.psum_scatter(jnp.concatenate([lax.dot_general(normed_b, projection_gr...  701 us
    all_gather x1, waiting for transfers between devices, entering(): everything = jax.tree.map(lambda part: lax.all_gather(part, axis), shard)  188 us
    all_gather x1, waiting for transfers between devices, local(): lax.all_gather(gate_weight, 'seq', axis=0, tiled=True)  140 us
    all_gather x1, waiting for transfers between devices, local(): lax.all_gather(up_weight, 'seq', axis=0, tiled=True)  134 us
    all_gather x1, waiting for transfers between devices, local(): lax.all_gather(down_weight, 'seq', axis=0, tiled=True)  134 us
    concatenate x1, other arithmetic, local(): jnp.concatenate([lax.dot_general(feed_input, feed_grads, contract_first,...  90.8 us
    unnamed x2, blocking collectives  81.1 us
  transfers between devices with their start and end apart: 11, of which 10 were waited for; matrix products, arithmetic and copies ran while one was open for 12% of the time, Pallas kernels for 0%

commit v1 on v0

v1 whole, which is shorter than its diff:
```python
import jax
import jax.numpy as jnp
from jax import lax
from jax.experimental import pallas as pl
from jax.experimental.pallas import tpu as pltpu
from jax.sharding import PartitionSpec as P

HEADS = 4
SLOTS = 64
PLANE = 8

epsilon = 1e-06
highest = lax.Precision.HIGHEST
bf16 = jnp.bfloat16
f32 = jnp.float32
MESH = pl.DeviceIdType.MESH
ANY = pl.BlockSpec(memory_space=pl.ANY)


def exchange(cid, arrays, outs, moves, plan):
    def kernel(*refs):
        ins = refs[: len(arrays)]
        dsts = refs[len(arrays) : len(arrays) + len(outs)]
        send, recv = refs[len(arrays) + len(outs) :]
        me = lax.axis_index("seq")
        peers, copies = plan(me, ins, dsts)
        barrier = pltpu.get_barrier_semaphore()
        for peer in peers:
            pl.semaphore_signal(barrier, inc=1, device_id=(peer,), device_id_type=MESH)
        pl.semaphore_wait(barrier, len(peers))
        started = []
        for k, (src, dst, device) in enumerate(copies):
            if device is None:
                copy = pltpu.make_async_copy(src, dst, send.at[k])
            else:
                copy = pltpu.make_async_remote_copy(
                    src_ref=src,
                    dst_ref=dst,
                    send_sem=send.at[k],
                    recv_sem=recv.at[k],
                    device_id=(device,),
                    device_id_type=MESH,
                )
            copy.start()
            started.append(copy)
        for copy in started:
            copy.wait()

    return pl.pallas_call(
        kernel,
        out_shape=[jax.ShapeDtypeStruct(s, d) for s, d in outs],
        in_specs=[ANY] * len(arrays),
        out_specs=[ANY] * len(outs),
        scratch_shapes=[
            pltpu.SemaphoreType.DMA((moves,)),
            pltpu.SemaphoreType.DMA((moves,)),
        ],
        compiler_params=pltpu.CompilerParams(collective_id=cid, has_side_effects=True),
    )(*arrays)


def chip_of(me):
    return lax.rem(lax.div(me, 2), HEADS)


def same_core(me, h, k):
    other = lax.rem(h + k, HEADS)
    return me + 2 * (other - h), other


def rows_at(ref, block, size):
    return ref.at[pl.ds(pl.multiple_of(block * size, size), size)]


def columns_at(ref, block, size):
    return ref.at[:, pl.ds(pl.multiple_of(block * size, 128), size)]


def gather_plane(cid, x):
    rows = x.shape[0]

    def plan(me, ins, outs):
        h = chip_of(me)
        peers = [same_core(me, h, k)[0] for k in (1, 2, 3)]
        dst = rows_at(outs[0], h, rows)
        return peers, [(ins[0], dst, p) for p in peers] + [(ins[0], dst, None)]

    return exchange(cid, [x], [((HEADS * rows, *x.shape[1:]), x.dtype)], 4, plan)[0]


def swap_plane(cid, x):
    rows = x.shape[0] // HEADS

    def plan(me, ins, outs):
        h = chip_of(me)
        dst = rows_at(outs[0], h, rows)
        pairs = [same_core(me, h, k) for k in (1, 2, 3)]
        moves = [(rows_at(ins[0], o, rows), dst, p) for p, o in pairs]
        return [p for p, _ in pairs], moves + [(rows_at(ins[0], h, rows), dst, None)]

    return exchange(cid, [x], [(x.shape, x.dtype)], 4, plan)[0]


def swap_core(cid, x):
    def plan(me, ins, outs):
        peer = me + 1 - 2 * lax.rem(me, 2)
        return [peer], [(ins[0], outs[0], peer)]

    return exchange(cid, [x], [(x.shape, x.dtype)], 1, plan)[0]


def gather_planes(cid, x, count):
    def plan(me, ins, outs):
        z = lax.div(me, PLANE)
        peers = [me + PLANE * (lax.rem(z + k, count) - z) for k in range(1, count)]
        dst = outs[0].at[z]
        return peers, [(ins[0], dst, p) for p in peers] + [(ins[0], dst, None)]

    return exchange(cid, [x], [((count, *x.shape), x.dtype)], count, plan)[0]


def swap_all(cid, x, count):
    def plan(me, ins, outs):
        peers = [lax.rem(me + k, count) for k in range(1, count)]
        moves = [(ins[0].at[p], outs[0].at[me], p) for p in peers]
        return peers, moves + [(ins[0].at[me], outs[0].at[me], None)]

    return exchange(cid, [x], [(x.shape, x.dtype)], count, plan)[0]


def first_exchange(cid, gains, weights, codes, count):
    rows, width = weights[0].shape
    part = width // HEADS

    def plan(me, ins, outs):
        g_in, q_in, k_in, v_in, c_in = ins
        g_out, w_out, c_out = outs
        h = chip_of(me)
        everyone = [lax.rem(me + k, count) for k in range(1, count)]
        moves = [(g_in, g_out.at[me], p) for p in everyone] + [(g_in, g_out.at[me], None)]
        targets = [same_core(me, h, k) for k in (1, 2, 3)] + [(None, h)]
        for device, other in targets:
            moves.append((c_in.at[other], c_out.at[h], device))
            for j, w in enumerate((q_in, k_in, v_in)):
                dst = w_out.at[
                    pl.ds(pl.multiple_of(h * rows, rows), rows), pl.ds(j * part, part)
                ]
                moves.append((columns_at(w, other, part), dst, device))
        return everyone, moves

    return exchange(
        cid,
        [gains, *weights, codes],
        [
            ((count, *gains.shape), gains.dtype),
            ((HEADS * rows, 3 * part), bf16),
            (codes.shape, codes.dtype),
        ],
        count + 16,
        plan,
    )


def second_exchange(cid, gate, up, down):
    rows, width = gate.shape
    part = width // HEADS

    def plan(me, ins, outs):
        h = chip_of(me)
        targets = [same_core(me, h, k) for k in (1, 2, 3)] + [(None, h)]
        at = pl.ds(pl.multiple_of(h * rows, rows), rows)
        moves = []
        for w, out, column in ((0, 0, 0), (1, 0, part), (2, 1, 0)):
            for device, other in targets:
                dst = outs[out].at[at, pl.ds(column, part)]
                moves.append((columns_at(ins[w], other, part), dst, device))
        return [p for p, _ in targets[:3]], moves

    return exchange(
        cid,
        [gate, up, down],
        [((HEADS * rows, 2 * part), bf16), ((HEADS * rows, part), bf16)],
        12,
        plan,
    )


def return_columns(cid, x, pieces):
    rows = x.shape[0] // HEADS
    part = x.shape[1] // pieces

    def plan(me, ins, outs):
        h = chip_of(me)
        targets = [same_core(me, h, k) for k in (1, 2, 3)] + [(None, h)]
        moves = []
        for device, other in targets:
            for j in range(pieces):
                src = ins[0].at[
                    pl.ds(pl.multiple_of(other * rows, rows), rows), pl.ds(j * part, part)
                ]
                moves.append((src, columns_at(outs[j], h, part), device))
        return [p for p, _ in targets[:3]], moves

    return exchange(
        cid, [x], [((rows, HEADS * part), x.dtype)] * pieces, 4 * pieces, plan
    )


def rms_factor(value_rows):
    return lax.rsqrt(jnp.mean(value_rows * value_rows, axis=-1, keepdims=True) + epsilon)


def precise(form, left, right):
    return jnp.einsum(form, left, right, precision=highest, preferred_element_type=f32)


def plain(form, left, right):
    return jnp.einsum(form, left, right, preferred_element_type=f32)


def local(
    tokens,
    cotangent,
    gate_codes,
    lengths,
    mixer_gain,
    query_weight,
    key_weight,
    value_weight,
    head_gain,
    output_weight,
    feed_gain,
    gate_weight,
    up_weight,
    down_weight,
):
    count = lax.axis_size("seq")
    planes = count // PLANE
    me = lax.axis_index("seq")
    z, h, core = me // PLANE, (me // 2) % HEADS, me % 2
    rows, width = tokens.shape
    strip = query_weight.shape[0]
    head_size = width // HEADS
    lines = [
        [p * PLANE + c * 2 + k for p in range(planes) for k in range(2)] for c in range(HEADS)
    ]

    def gather_line(x):
        return lax.all_gather(x, "seq", axis=0, tiled=True, axis_index_groups=lines)

    def scatter_line(x):
        return lax.psum_scatter(
            x, "seq", scatter_dimension=0, tiled=True, axis_index_groups=lines
        )

    def shuffled(x):
        y = x.reshape(*x.shape[:-1], planes, HEADS, 2, strip)
        return jnp.swapaxes(y, -3, -2).reshape(x.shape)

    def restored(x):
        y = x.reshape(*x.shape[:-1], planes, 2, HEADS, strip)
        return jnp.swapaxes(y, -3, -2).reshape(x.shape)

    gains = jnp.stack([mixer_gain, head_gain, feed_gain]).astype(f32)
    gains = jnp.pad(gains, ((0, 5), (0, 128 - strip)))
    codes = gate_codes.reshape(rows, HEADS, SLOTS).swapaxes(0, 1)
    gains_all, mixer_rows, codes_all = first_exchange(
        0, gains, (query_weight, key_weight, value_weight), codes, count
    )
    mixer_weight = gather_line(mixer_rows)
    feed_rows, down_rows = second_exchange(1, gate_weight, up_weight, down_weight)
    output_line = gather_line(shuffled(output_weight))
    feed_weight = gather_line(feed_rows)
    down_line = gather_line(down_rows)
    gain_of = gains_all[:, :3, :strip].swapaxes(0, 1).reshape(3, width)
    gain_one, gain_two = shuffled(gain_of[0]), shuffled(gain_of[2])
    head_gain_f = lax.dynamic_slice(gain_of[1], (h * head_size,), (head_size,))

    tokens_f = shuffled(tokens).astype(f32)
    factor_one = rms_factor(tokens_f)
    normed_one = tokens_f * factor_one
    h1 = gather_plane(2, (normed_one * gain_one).astype(bf16))
    cotangent_own = shuffled(cotangent)
    cotangent_all = gather_plane(3, cotangent_own)

    decay = jax.nn.log_sigmoid(codes_all.astype(f32) / 256.0)
    block = z * PLANE + 2 * jnp.arange(HEADS) + core
    first = (block * rows)[:, None]
    position = first + jnp.arange(rows)[None, :]
    order = jnp.arange(lengths.shape[0])
    first_token = jnp.sum(
        jnp.where(order[:, None] > order[None, :], lengths[None, :], 0), axis=1
    )
    seen = jnp.sum(
        jnp.where(
            (first_token[None, None, :] <= position[:, :, None])
            & (first_token[None, None, :] >= first[:, :, None]),
            1,
            0,
        ),
        axis=2,
    )
    places = jnp.arange(rows)
    before = places[:, None] >= places[None, :]
    same = jnp.where(before[None] & (seen[:, :, None] == seen[:, None, :]), 1.0, 0.0).astype(f32)
    fresh = jnp.where(seen == 0, 1.0, 0.0).astype(f32)[:, :, None]
    logsum = precise("ts,bsm->btm", before.astype(f32), decay)
    grow = jnp.exp(logsum)
    back = jnp.exp(-logsum) * -jnp.expm1(decay)
    tail = jnp.where(seen == seen[:, -1:], 1.0, 0.0).astype(f32)[:, :, None]
    weights = grow[:, -1:] * back * tail
    carried = fresh[:, -1] * grow[:, -1]

    blocked = (HEADS, rows, head_size)
    projected = jnp.dot(h1, mixer_weight, preferred_element_type=f32).astype(bf16)
    query = projected[:, :head_size].reshape(blocked)
    key = projected[:, head_size : 2 * head_size].reshape(blocked)
    value = projected[:, 2 * head_size :].reshape(blocked)
    query_f = query.astype(f32)

    def pack(state, gain):
        return jnp.concatenate(
            [state, jnp.broadcast_to(gain[..., None], (*gain.shape, 128))], axis=-1
        )

    def unpack(x):
        return x[..., :-128], x[..., -128]

    own = pack(
        jnp.concatenate(
            [
                precise("bsm,bsd->bmd", weights, key.astype(f32)),
                precise("bsm,bsd->bmd", weights, value.astype(f32)),
            ],
            axis=-1,
        ),
        carried,
    )
    other = swap_core(4, own)
    even, odd = jnp.where(core == 0, own, other), jnp.where(core == 0, other, own)
    run_state, run_gain = jnp.zeros_like(own[0, :, :-128]), jnp.ones_like(carried[0])
    entries = []
    for k in range(PLANE):
        state, gain = unpack((even, odd)[k % 2][k // 2])
        entries.append((run_state, run_gain))
        run_state, run_gain = gain[:, None] * run_state + state, gain * run_gain
    summaries = gather_planes(5, pack(run_state, run_gain), planes)
    plane_state = jnp.zeros_like(run_state)
    for k in range(planes):
        state, gain = unpack(summaries[k])
        plane_state = jnp.where(k < z, gain[:, None] * plane_state + state, plane_state)

    def pick(pairs, base):
        out = []
        for k in range(HEADS):
            (s0, g0), (s1, g1) = pairs[2 * k], pairs[2 * k + 1]
            s, g = jnp.where(core == 0, s0, s1), jnp.where(core == 0, g0, g1)
            out.append(g[:, None] * base + s)
        return jnp.stack(out)

    state_in = pick(entries, plane_state)
    key_state, value_state = state_in[..., :head_size], state_in[..., head_size:]

    affinity = plain("btd,bsd->bts", query, key) * same
    score = grow * precise("bts,bsm->btm", affinity, back) + grow * fresh * precise(
        "btd,bmd->btm", query_f, key_state
    )
    probs = jax.nn.softmax(score, axis=-1)
    lifted = probs * grow
    mixing = (precise("btm,bsm->bts", lifted, back) * same).astype(bf16)
    entry = lifted * fresh
    slot_out = plain("bts,bsd->btd", mixing, value) + precise("btm,bmd->btd", entry, value_state)
    head_factor = rms_factor(slot_out)
    unit_heads = slot_out * head_factor
    normed_heads = (unit_heads * head_gain_f).astype(bf16).reshape(HEADS * rows, head_size)

    quarter = planes // HEADS
    out_rows = swap_plane(6, output_line)
    out_weight = (
        out_rows.reshape(HEADS, quarter, 2 * strip, width)
        .swapaxes(0, 1)
        .reshape(head_size, width)
    )
    mixed = jnp.dot(normed_heads, out_weight, preferred_element_type=f32).astype(bf16)

    def summed(cid, partial):
        parts = swap_plane(cid, partial).reshape(HEADS, rows, width).astype(f32)
        return parts[0] + parts[1] + parts[2] + parts[3]

    residual = tokens_f + summed(7, mixed)
    factor_two = rms_factor(residual)
    normed_two = residual * factor_two
    h2 = gather_plane(8, (normed_two * gain_two).astype(bf16))

    part = down_line.shape[1]
    both = jnp.dot(h2, feed_weight, preferred_element_type=f32)
    gate, upward = both[:, :part], both[:, part:]
    sigma = jax.nn.sigmoid(gate)
    active = gate * sigma
    hidden = (active * upward).astype(bf16)
    hidden_grad = jnp.dot(cotangent_all, down_line, preferred_element_type=f32)
    gate_back = (hidden_grad * upward * sigma * (1.0 + gate * (1.0 - sigma))).astype(bf16)
    up_back = (hidden_grad * active).astype(bf16)
    both_back = jnp.concatenate([gate_back, up_back], axis=1)
    feed_in = plain("tf,df->td", both_back, feed_weight).astype(bf16)
    feed_in_grad = summed(9, feed_in)
    feed_sums = scatter_line(plain("td,tf->df", h2, both_back).astype(bf16))
    down_sums = scatter_line(plain("td,tf->df", cotangent_all, hidden).astype(bf16))
    feed_out = plain("tf,df->td", hidden, down_line).astype(bf16)
    block_out = restored((residual + summed(10, feed_out)).astype(bf16))

    feed_gain_part = jnp.sum(normed_two * feed_in_grad, axis=0)
    scaled_two = feed_in_grad * gain_two
    residual_grad = cotangent_own.astype(f32) + factor_two * (
        scaled_two - normed_two * jnp.mean(normed_two * scaled_two, axis=-1, keepdims=True)
    )
    mixed_grad = gather_plane(11, residual_grad.astype(bf16))

    heads_grad = plain("td,fd->tf", mixed_grad, out_weight).reshape(blocked)
    head_gain_part = jnp.sum(unit_heads * heads_grad, axis=(0, 1))
    scaled_heads = heads_grad * head_gain_f
    out_back = (
        head_factor
        * (scaled_heads - unit_heads * jnp.mean(unit_heads * scaled_heads, axis=-1, keepdims=True))
    ).astype(bf16)
    out_back_f = out_back.astype(f32)
    mixing_grad = plain("btd,bsd->bts", out_back, value) * same
    local_value = plain("bts,btd->bsd", mixing, out_back)
    lifted_grad = grow * precise("bts,bsm->btm", mixing_grad, back) + grow * fresh * precise(
        "btd,bmd->btm", out_back_f, value_state
    )
    score_grad = probs * (lifted_grad - jnp.sum(probs * lifted_grad, axis=-1, keepdims=True))
    inner_grad = grow * score_grad
    state_grad = inner_grad * fresh
    affinity_grad = (precise("btm,bsm->bts", inner_grad, back) * same).astype(bf16)
    own_back = pack(
        jnp.concatenate(
            [
                precise("btm,btd->bmd", state_grad, query_f),
                precise("btm,btd->bmd", entry, out_back_f),
            ],
            axis=-1,
        ),
        carried,
    )
    other_back = swap_core(12, own_back)
    even = jnp.where(core == 0, own_back, other_back)
    odd = jnp.where(core == 0, other_back, own_back)
    run_state, run_gain = jnp.zeros_like(run_state), jnp.ones_like(run_gain)
    leaving = [None] * PLANE
    for k in reversed(range(PLANE)):
        state, gain = unpack((even, odd)[k % 2][k // 2])
        leaving[k] = (run_state, run_gain)
        run_state, run_gain = gain[:, None] * run_state + state, gain * run_gain
    summaries = gather_planes(13, pack(run_state, run_gain), planes)
    plane_state = jnp.zeros_like(run_state)
    for k in reversed(range(planes)):
        state, gain = unpack(summaries[k])
        plane_state = jnp.where(k > z, gain[:, None] * plane_state + state, plane_state)
    later = pick(leaving, plane_state)
    later_key, later_value = later[..., :head_size], later[..., head_size:]

    query_back = plain("bts,bsd->btd", affinity_grad, key) + precise(
        "btm,bmd->btd", state_grad, key_state
    )
    key_back = plain("bts,btd->bsd", affinity_grad, query) + precise(
        "bsm,bmd->bsd", weights, later_key
    )
    value_back = local_value + precise("bsm,bmd->bsd", weights, later_value)
    backs = jnp.concatenate(
        [
            x.astype(bf16).reshape(HEADS * rows, head_size)
            for x in (query_back, key_back, value_back)
        ],
        axis=1,
    )
    mixer_in_grad = summed(14, plain("tf,df->td", backs, mixer_weight).astype(bf16))
    mixer_gain_part = jnp.sum(normed_one * mixer_in_grad, axis=0)
    scaled_one = mixer_in_grad * gain_one
    input_grad = residual_grad + factor_one * (
        scaled_one - normed_one * jnp.mean(normed_one * scaled_one, axis=-1, keepdims=True)
    )

    out_part = plain("tf,td->fd", normed_heads, mixed_grad).astype(bf16)
    out_part = (
        out_part.reshape(quarter, HEADS, 2 * strip, width)
        .swapaxes(0, 1)
        .reshape(head_size, width)
    )
    out_sums = scatter_line(swap_plane(15, out_part))
    mixer_sums = scatter_line(plain("td,tf->df", h1, backs).astype(bf16))
    gate_grad, up_grad = return_columns(16, feed_sums, 2)
    (down_grad,) = return_columns(17, down_sums, 1)
    query_grad, key_grad, value_grad = return_columns(18, mixer_sums, 3)

    head_whole = lax.dynamic_update_slice(
        jnp.zeros((width,), f32), head_gain_part, (h * head_size,)
    )
    gain_parts = jnp.stack([restored(mixer_gain_part), head_whole, restored(feed_gain_part)])
    gain_parts = gain_parts.reshape(3, count, strip).swapaxes(0, 1)
    gain_parts = jnp.pad(gain_parts, ((0, 0), (0, 5), (0, 128 - strip)))
    gain_sums = jnp.sum(swap_all(19, gain_parts, count), axis=0)[:3, :strip]
    return (
        block_out,
        restored(input_grad),
        gain_sums[0],
        query_grad.astype(f32),
        key_grad.astype(f32),
        value_grad.astype(f32),
        gain_sums[1],
        restored(out_sums).astype(f32),
        gain_sums[2],
        gate_grad.astype(f32),
        up_grad.astype(f32),
        down_grad.astype(f32),
    )


def solution(mesh):
    split, line = P("seq", None), P("seq")
    return jax.shard_map(
        local,
        mesh=mesh,
        in_specs=(split, split, split, P(), line, split, split, split, line, split, line, split, split, split),
        out_specs=(split, split, line, split, split, split, line, split, line, split, split, split),
        check_vma=False,
    )
```

time: 3840 us -> 817 us (0.21)
  waiting for transfers between devices: 3130 us -> 44.7 us
  Pallas kernels: 0 us -> 504 us
  other arithmetic: 255 us -> 66.4 us
  blocking collectives: 160 us -> 0 us
  matrix products: 233 us -> 119 us
    unnamed x12 -> x8, waiting for transfers between devices: 1680 us -> 0.64 us
    all_gather x9 -> x4, waiting for transfers between devices: 744 us -> 0.06 us  [gather_line(): return lax.all_gather(x, 'seq', axis=0, tiled=True, axis_index_groups=lines)]
    reduce_scatter x1 -> x4, waiting for transfers between devices: 701 us -> 44 us  [scatter_line(): lax.psum_scatter(x, 'seq', scatter_dimension=0, tiled=True, axis_index_gr...]
    pallas_call x0 -> x20, Pallas kernels: none -> 504 us  [exchange(): pl.pallas_call(kernel, out_shape=[jax.ShapeDtypeStruct(s, d) for s, d in...]
    concatenate x4, other arithmetic: 139 us -> 3.67 us  [pack(): jnp.concatenate([state, jnp.broadcast_to(gain[..., None], (*gain.shape, 1...]
    dot_general x38 -> x33, matrix products: 233 us -> 119 us  [the longest x14 68.3 us: plain(): return jnp.einsum(form, left, right, preferred_element_type=f32)]
    select_n x66 -> x7, other arithmetic: 89.9 us -> 6.27 us  [the longest x4 2.93 us: pick(): s, g = (jnp.where(core == 0, s0, s1), jnp.where(core == 0, g0, g1))]
    unnamed x2 -> x0, blocking collectives: 81.1 us -> none
  transfers between devices with their start and end apart: 11 -> 8, of which waited for: 10 -> 1; matrix products, arithmetic and copies ran while one was open for 12% -> 22% of each run, Pallas kernels for 0% -> 49%
where the time goes in v1:
time: 817 us; the launch traced here: 813 us
  Pallas kernels  504 us (62%)
  matrix products  119 us (15%)
  other arithmetic  66.4 us (8%)
  local copies, waits for them, and re-layouts  62.1 us (8%)
  waiting for transfers between devices  44.7 us (5%)
  between operations  16.3 us (2%)
    pallas_call x20, Pallas kernels, exchange(): pl.pallas_call(kernel, out_shape=[jax.ShapeDtypeStruct(s, d) for s, d in...  504 us
    dot_general x14, matrix products, plain(): return jnp.einsum(form, left, right, preferred_element_type=f32)  68.3 us
    reduce_scatter x4, waiting for transfers between devices, scatter_line(): lax.psum_scatter(x, 'seq', scatter_dimension=0, tiled=True, axis_index_gr...  44 us
    unnamed x227, local copies, waits for them, and re-layouts  27.3 us
  transfers between devices with their start and end apart: 8, of which 1 were waited for; matrix products, arithmetic and copies ran while one was open for 22% of the time, Pallas kernels for 49%

profile of v1, /device:TPU:0, one launch (start us, length us, event | category | flops | bytes accessed | tf_op | source)
XLA Modules:
  0.0 813.0 jit_solution(17697252758062498484)
XLA Ops:
  11.9 23.7 %shard_map.229 = (f32[32,8,128]{2,1,0:T(8,128)}, bf16[256,1536]{1,0:T(8,128)(2,1)}, s32[4,160,64]{2,1,0:T(8,128)}) custom-call(f32[8,128]{1,0:T(8,128)} %fusion.66.refs_0_, bf16[64,2048]{1,0:T(8,128)(2,1)} %refs_1_.2, bf16[64,2048]{1,0:T(8,128)(2,1)} %refs_2_.2, bf16[64,2048]{1,0:T(8,128)(2,1)} %refs_3_.1, s32[4,160,64]{2,1,0:T(8,128)} %bitcast.264), custom_call_target="tpu_custom_call" | custom-call | tf_op jit(solution)/shard_map/pallas_call | solution.py:49
  35.7 26.9 %shard_map.236 = (bf16[256,2816]{1,0:T(8,128)(2,1)}, bf16[256,1408]{1,0:T(8,128)(2,1)}) custom-call(bf16[64,5632]{1,0:T(8,128)(2,1)} %refs_0_.1, bf16[64,5632]{1,0:T(8,128)(2,1)} %refs_1_.3, bf16[64,5632]{1,0:T(8,128)(2,1)} %refs_2_.3), custom_call_target="tpu_custom_call" | custom-call | tf_op jit(solution)/shard_map/pallas_call | solution.py:49
  74.4 31.4 %shard_map.230 = bf16[640,2048]{1,0:T(8,128)(2,1)} custom-call(bf16[160,2048]{1,0:T(8,128)(2,1)} %multiply_convert_fusion.4.refs_0_), custom_call_target="tpu_custom_call" | custom-call | tf_op jit(solution)/shard_map/pallas_call | solution.py:49
  106.6 2.3 copy.202
  111.1 30.4 %shard_map.238 = bf16[640,2048]{1,0:T(8,128)(2,1)} custom-call(bf16[160,2048]{1,0:T(8,128)(2,1)} %copy.203.refs_0_), custom_call_target="tpu_custom_call" | custom-call | tf_op jit(solution)/shard_map/pallas_call | solution.py:49
  141.6 24.6 %shard_map.233 = bf16[512,2048]{1,0:T(8,128)(2,1)} custom-call(bf16[512,2048]{1,0:T(8,128)(2,1)} %all-gather.7.cloned.1.call-done.refs_0_), custom_call_target="tpu_custom_call" | custom-call | tf_op jit(solution)/shard_map/pallas_call | solution.py:49
  166.2 7.8 convolution_convert_fusion.7
  179.1 3.2 shard_map.231
  187.5 40.4 %shard_map.232 = f32[4,64,1152]{2,1,0:T(8,128)} custom-call(f32[64,1152]{1,0:T(8,128)} %pad_maximum_fusion.10.refs_0_), custom_call_target="tpu_custom_call" | custom-call | tf_op jit(solution)/shard_map/pallas_call | solution.py:49
  239.6 3.1 convolution_convert_fusion.6.refs_0_
  242.7 30.6 %shard_map.234 = bf16[640,2048]{1,0:T(8,128)(2,1)} custom-call(bf16[640,2048]{1,0:T(8,128)(2,1)} %convolution_convert_fusion.6.refs_0_), custom_call_target="tpu_custom_call" | custom-call | tf_op jit(solution)/shard_map/pallas_call | solution.py:49
  273.3 2.5 convert_element_type.173
  275.8 2.4 copy-done
  279.6 2.8 copy.195
  288.1 31.3 %shard_map.235 = bf16[640,2048]{1,0:T(8,128)(2,1)} custom-call(bf16[160,2048]{1,0:T(8,128)(2,1)} %multiply_convert_fusion.2.refs_0_), custom_call_target="tpu_custom_call" | custom-call | tf_op jit(solution)/shard_map/pallas_call | solution.py:49
  319.4 14.2 %fusion.83 = f32[640,2816]{1,0:T(8,128)} fusion(bf16[640,2048]{1,0:T(8,128)(2,1)} %shard_map.235, bf16[2048,2816]{1,0:T(8,128)(2,1)} %all-gather.9.cloned.1.call-done), kind=kOutput, calls=%fused_computation.291 | convolution fusion | flops 7381975040 | bytes 21364736 | tf_op jit(solution)/shard_map/dot_general | solution.py:396
  333.7 12.2 %fusion.4 = (bf16[640,1408]{1,0:T(8,128)(2,1)S(1)}, bf16[640,1408]{1,0:T(8,128)(2,1)S(1)}, bf16[640,1408]{1,0:T(8,128)(2,1)}) fusion(f32[640,2816]{1,0:T(8,128)} %fusion.83, bf16[640,2048]{1,0:T(8,128)(2,1)} %shard_map.238, bf16[2048,1408]{1,0:T(8,128)(2,1)} %all-gather.11.cloned.1.call-done), kind=kOutput, calls=%fused_computation.10 | convolution fusion | flops 3704504320 | bytes 21004288 | tf_op jit(solution)/shard_map/dot_general | solution.py:401
  347.7 8.9 %convolution_convert_fusion.4.refs_0_ = bf16[640,2048]{1,0:T(8,128)(2,1)} fusion(bf16[2048,2816]{1,0:T(8,128)(2,1)S(1)} %copy-done.107, bf16[640,1408]{1,0:T(8,128)(2,1)S(1)} %get-tuple-element.121, bf16[640,1408]{1,0:T(8,128)(2,1)S(1)} %get-tuple-element.120), kind=kOutput, calls=%fused_computation.16 | convolution fusion | flops 7390494720 | bytes 17760256 | tf_op jit(solution)/shard_map/tf,df->td/dot_general | solution.py:218
  356.7 30.2 %shard_map.239 = bf16[640,2048]{1,0:T(8,128)(2,1)} custom-call(bf16[640,2048]{1,0:T(8,128)(2,1)} %convolution_convert_fusion.4.refs_0_), custom_call_target="tpu_custom_call" | custom-call | tf_op jit(solution)/shard_map/pallas_call | solution.py:49
  386.8 2.4 convert_element_type.183
  393.0 2.8 copy.205
  395.8 3.6 multiply_reduce_fusion
  399.4 6.4 add_convert_fusion.refs_0_
  405.9 30.1 %shard_map.240 = bf16[640,2048]{1,0:T(8,128)(2,1)} custom-call(bf16[160,2048]{1,0:T(8,128)(2,1)} %add_convert_fusion.refs_0_), custom_call_target="tpu_custom_call" | custom-call | tf_op jit(solution)/shard_map/pallas_call | solution.py:49
  436.0 5.0 convolution_convert_fusion.8.refs_0_
  441.0 24.6 %shard_map.246 = bf16[512,2048]{1,0:T(8,128)(2,1)} custom-call(bf16[512,2048]{1,0:T(8,128)(2,1)} %convolution_convert_fusion.8.refs_0_), custom_call_target="tpu_custom_call" | custom-call | tf_op jit(solution)/shard_map/pallas_call | solution.py:49
  465.6 8.8 %fusion.1 = bf16[2048,1408]{1,0:T(8,128)(2,1)} fusion(bf16[640,1408]{1,0:T(8,128)(2,1)} %get-tuple-element.122, bf16[640,2048]{1,0:T(8,128)(2,1)} %shard_map.238), kind=kOutput, calls=%fused_computation.4 | convolution fusion | flops 3693871104 | bytes 10190848 | tf_op jit(solution)/shard_map/td,tf->df/dot_general | solution.py:218
  474.5 4.0 fusion.84
  486.4 3.2 shard_map.241
  494.7 44.5 %shard_map.242 = f32[4,64,1152]{2,1,0:T(8,128)} custom-call(f32[64,1152]{1,0:T(8,128)} %pad_maximum_fusion.11.refs_0_), custom_call_target="tpu_custom_call" | custom-call | tf_op jit(solution)/shard_map/pallas_call | solution.py:49
  549.5 7.7 convolution_convert_fusion.2
  557.2 14.4 %convolution_convert_fusion = bf16[2048,2816]{1,0:T(8,128)(2,1)} fusion(bf16[640,2048]{1,0:T(8,128)(2,1)} %shard_map.235, bf16[640,1408]{1,0:T(8,128)(2,1)} %copy-done.110, bf16[640,1408]{1,0:T(8,128)(2,1)} %copy-done.109), kind=kOutput, calls=%fused_computation.1 | convolution fusion | flops 7394951168 | bytes 17760256 | tf_op jit(solution)/shard_map/td,tf->df/dot_general | solution.py:218
  572.9 8.4 %convolution_convert_fusion.3.refs_0_ = bf16[640,2048]{1,0:T(8,128)(2,1)} fusion(bf16[2048,1536]{1,0:T(8,128)(2,1)} %all-gather.5.cloned.1.call-done, bf16[640,512]{1,0:T(8,128)(2,1)S(1)} %bitcast.269, bf16[640,512]{1,0:T(8,128)(2,1)S(1)} %bitcast.271, bf16[640,512]{1,0:T(8,128)(2,1)S(1)} %bitcast.267), kind=kOutput, calls=%fused_computation.15 | convolution fusion | flops 4033740800 | bytes 10878976 | tf_op jit(solution)/shard_map/tf,df->td/dot_general | solution.py:218
  581.3 29.3 %shard_map.243 = bf16[640,2048]{1,0:T(8,128)(2,1)} custom-call(bf16[640,2048]{1,0:T(8,128)(2,1)} %convolution_convert_fusion.3.refs_0_), custom_call_target="tpu_custom_call" | custom-call | tf_op jit(solution)/shard_map/pallas_call | solution.py:49
  610.5 2.4 convert_element_type.192
  616.2 9.0 %convolution_convert_fusion.5.refs_0_ = bf16[640,2048]{1,0:T(8,128)(2,1)} fusion(bf16[640,1408]{1,0:T(8,128)(2,1)} %get-tuple-element.122, bf16[2048,1408]{1,0:T(8,128)(2,1)} %all-gather.11.cloned.1.call-done), kind=kOutput, calls=%fused_computation.17 | convolution fusion | flops 3692298240 | bytes 10190848 | tf_op jit(solution)/shard_map/tf,df->td/dot_general | solution.py:218
  625.2 31.4 %shard_map.237 = bf16[640,2048]{1,0:T(8,128)(2,1)} custom-call(bf16[640,2048]{1,0:T(8,128)(2,1)} %convolution_convert_fusion.5.refs_0_), custom_call_target="tpu_custom_call" | custom-call | tf_op jit(solution)/shard_map/pallas_call | solution.py:49
  656.6 2.4 convert_element_type.177
  660.5 2.8 copy.199
  665.1 4.2 multiply_add_fusion
  669.4 2.4 copy.222
  671.7 2.7 copy.223
  676.5 26.1 %shard_map.244 = f32[32,8,128]{2,1,0:T(8,128)} custom-call(f32[32,8,128]{2,1,0:T(8,128)} %pad.12.refs_0_), custom_call_target="tpu_custom_call" | custom-call | tf_op jit(solution)/shard_map/pallas_call | solution.py:49
  708.1 12.7 %shard_map.248 = bf16[64,5632]{1,0:T(8,128)(2,1)} custom-call(bf16[256,1408]{1,0:T(8,128)(2,1)} %reduce-scatter.11.cloned.1.call-done.refs_0_), custom_call_target="tpu_custom_call" | custom-call | tf_op jit(solution)/shard_map/pallas_call | solution.py:49
  723.1 12.5 %shard_map.245 = (bf16[64,2048]{1,0:T(8,128)(2,1)}, bf16[64,2048]{1,0:T(8,128)(2,1)}, bf16[64,2048]{1,0:T(8,128)(2,1)}) custom-call(bf16[256,1536]{1,0:T(8,128)(2,1)} %reduce-scatter.5.cloned.1.call-done.refs_0_), custom_call_target="tpu_custom_call" | custom-call | tf_op jit(solution)/shard_map/pallas_call | solution.py:49
  740.9 44.0 %reduce-scatter.9.cloned.1.call-done.refs_0_ = bf16[256,2816]{1,0:T(8,128)(2,1)} async-done(((bf16[2048,2816]{1,0:T(8,128)(2,1)}), bf16[256,2816]{1,0:T(8,128)(2,1)}) %reduce-scatter.9.cloned.1.call-update) | async-done | bytes 1441808 | tf_op jit(solution)/shard_map/reduce_scatter | solution.py:252
  784.9 17.2 %shard_map.247 = (bf16[64,5632]{1,0:T(8,128)(2,1)}, bf16[64,5632]{1,0:T(8,128)(2,1)}) custom-call(bf16[256,2816]{1,0:T(8,128)(2,1)} %reduce-scatter.9.cloned.1.call-done.refs_0_), custom_call_target="tpu_custom_call" | custom-call | tf_op jit(solution)/shard_map/pallas_call | solution.py:49
  802.1 2.4 convert_element_type.203
  (375 shorter events, 100.5 us)
Async XLA Ops:
  7.2 3.0 copy-start.58
  7.2 4.1 copy-start.104
  7.2 4.1 copy-start.105
  7.2 4.1 copy-start.106
  7.2 134.4 %all-gather.7.cloned.1.call-start = ((), (), s32[]{:S(2)}) async-start(), calls=%async_computation.5 | async-start | bytes 2359296 | tf_op jit(solution)/shard_map/all_gather | solution.py:249
  10.2 156.1 %all-gather.5.cloned.1.call-start = ((), (), s32[]{:S(2)}) async-start(), calls=%async_computation.4 | async-start | bytes 7077888 | tf_op jit(solution)/shard_map/all_gather | solution.py:249
  35.6 28.5 %copy-start.67 = (f32[32,8,128]{2,1,0:T(8,128)S(1)}, f32[32,8,128]{2,1,0:T(8,128)}, u32[]{:S(2)}) copy-start(f32[32,8,128]{2,1,0:T(8,128)} %get-tuple-element.23) | copy-start | bytes 393220
  35.6 29.9 %copy-start.51 = (bf16[160,2048]{1,0:T(8,128)(2,1)S(1)}, bf16[160,2048]{1,0:T(8,128)(2,1)}, u32[]{:S(2)}) copy-start(bf16[160,2048]{1,0:T(8,128)(2,1)} %param.15) | copy-start | bytes 1966084
  35.6 283.8 %all-gather.9.cloned.1.call-start = ((), (), s32[]{:S(2)}) async-start(), calls=%async_computation.6 | async-start | bytes 12976128 | tf_op jit(solution)/shard_map/all_gather | solution.py:249
  62.6 4.2 copy-start.57
  62.6 271.1 %all-gather.11.cloned.1.call-start = ((), (), s32[]{:S(2)}) async-start(), calls=%async_computation.7 | async-start | bytes 6488064 | tf_op jit(solution)/shard_map/all_gather | solution.py:249
  63.2 640.9 %reduce-scatter.7.cloned.1.call-start = ((), (), s32[]{:S(2)}) async-start(), calls=%async_computation.9 | async-start | bytes 2359296 | tf_op jit(solution)/shard_map/reduce_scatter | solution.py:252
  72.4 33.4 %copy-start.61 = (f32[4,4,2,64]{3,1,2,0:T(4,128)}, f32[4,4,2,64]{3,1,2,0:T(4,128)S(1)}, u32[]{:S(2)}) copy-start(f32[4,4,2,64]{3,1,2,0:T(4,128)S(1)} %copy.260) | copy-start | bytes 24580
  106.1 35.4 %copy-start.68 = (s32[4,160]{1,0:T(4,128)}, s32[4,160]{1,0:T(4,128)S(1)}, u32[]{:S(2)}) copy-start(s32[4,160]{1,0:T(4,128)S(1)} %select_reduce_fusion.8) | copy-start | bytes 7684
  184.2 2.4 copy-start.36
  184.2 2.4 copy-start.38
  227.9 2.3 copy-start.35
  228.0 2.3 copy-start.37
  230.7 5.3 copy-start.10
  232.6 3.2 copy-start.18
  236.1 3.5 copy-start.44
  275.8 2.4 copy-start
  282.4 3.8 copy-start.1
  286.5 112.9 %copy-start.71 = (f32[160]{0:T(256)}, f32[160]{0:T(256)S(1)}, u32[]{:S(2)}) copy-start(f32[160]{0:T(256)S(1)} %add_rsqrt_fusion.1) | copy-start | bytes 1924
  333.7 14.1 %copy-start.107 = (bf16[2048,2816]{1,0:T(8,128)(2,1)S(1)}, bf16[2048,2816]{1,0:T(8,128)(2,1)}, u32[]{:S(2)}) copy-start(bf16[2048,2816]{1,0:T(8,128)(2,1)} %all-gather.9.cloned.1.call-done) | copy-start | bytes 34603012
  389.3 2.3 copy-start.2
  393.0 2.8 copy-start.59
  395.8 3.6 copy-start.13
  399.4 6.4 copy-start.75
  405.9 30.1 %copy-start.29 = (bf16[4,160,512]{2,1,0:T(8,128)(2,1)S(1)}, bf16[4,160,512]{2,1,0:T(8,128)(2,1)}, u32[]{:S(2)}) copy-start(bf16[4,160,512]{2,1,0:T(8,128)(2,1)} %copy-done.28) | copy-start | bytes 1966084
  465.6 242.5 %reduce-scatter.11.cloned.1.call-start = ((), (), s32[]{:S(2)}) async-start(), calls=%async_computation.11 | async-start | bytes 6488064 | tf_op jit(solution)/shard_map/reduce_scatter | solution.py:252
  474.5 248.6 %reduce-scatter.5.cloned.1.call-start = ((), (), s32[]{:S(2)}) async-start(), calls=%async_computation.8 | async-start | bytes 7077888 | tf_op jit(solution)/shard_map/reduce_scatter | solution.py:252
  474.5 4.1 copy-start.4
  482.9 2.4 copy-start.25
  485.3 4.3 copy-start.26
  486.4 3.2 copy-start.21
  491.4 2.4 copy-start.32
  491.5 2.4 copy-start.40
  539.2 2.3 copy-start.31
  539.2 2.3 copy-start.33
  539.2 2.3 copy-start.47
  546.4 2.5 copy-start.53
  548.9 8.3 %copy-start.55 = (bf16[4,160,512]{2,1,0:T(8,128)(2,1)}, bf16[4,160,512]{2,1,0:T(8,128)(2,1)S(1)}, u32[]{:S(2)}) copy-start(bf16[4,160,512]{2,1,0:T(8,128)(2,1)S(1)} %fusion.8) | copy-start | bytes 1966084
  557.2 227.7 %reduce-scatter.9.cloned.1.call-start = ((), (), s32[]{:S(2)}) async-start(), calls=%async_computation.10 | async-start | bytes 12976128 | tf_op jit(solution)/shard_map/reduce_scatter | solution.py:252
  660.5 2.8 copy-start.74
  671.7 2.7 copy-start.77
  671.7 4.0 copy-start.64
  802.1 2.4 copy-start.50
  (71 other events, 109.8 us)
Sparse Core Ops, SparseCore 0:
  10.3 31.7 all-gather.6
  43.8 64.2 all-gather.4
  109.7 130.9 all-gather.8
  242.1 59.3 all-gather.10
  465.7 47.4 reduce-scatter.6
  515.4 70.0 reduce-scatter.10
  587.8 74.9 reduce-scatter.4
  665.1 119.7 reduce-scatter.8

commit v2 on v1

v2 whole, which is shorter than its diff:
```python
import jax
import jax.numpy as jnp
from jax import lax
from jax.experimental import pallas as pl
from jax.experimental.pallas import tpu as pltpu
from jax.sharding import PartitionSpec as P

HEADS = 4
SLOTS = 64
PLANE = 8

epsilon = 1e-06
highest = lax.Precision.HIGHEST
bf16 = jnp.bfloat16
f32 = jnp.float32
MESH = pl.DeviceIdType.MESH
ANY = pl.BlockSpec(memory_space=pl.ANY)


def exchange(cid, arrays, outs, moves, plan):
    def kernel(*refs):
        ins = refs[: len(arrays)]
        dsts = refs[len(arrays) : len(arrays) + len(outs)]
        send, recv = refs[len(arrays) + len(outs) :]
        me = lax.axis_index("seq")
        peers, copies = plan(me, ins, dsts)
        barrier = pltpu.get_barrier_semaphore()
        for peer in peers:
            pl.semaphore_signal(barrier, inc=1, device_id=(peer,), device_id_type=MESH)
        pl.semaphore_wait(barrier, len(peers))
        started = []
        for k, (src, dst, device) in enumerate(copies):
            if device is None:
                copy = pltpu.make_async_copy(src, dst, send.at[k])
            else:
                copy = pltpu.make_async_remote_copy(
                    src_ref=src,
                    dst_ref=dst,
                    send_sem=send.at[k],
                    recv_sem=recv.at[k],
                    device_id=(device,),
                    device_id_type=MESH,
                )
            copy.start()
            started.append(copy)
        for copy in started:
            copy.wait()

    return pl.pallas_call(
        kernel,
        out_shape=[jax.ShapeDtypeStruct(s, d) for s, d in outs],
        in_specs=[ANY] * len(arrays),
        out_specs=[ANY] * len(outs),
        scratch_shapes=[
            pltpu.SemaphoreType.DMA((moves,)),
            pltpu.SemaphoreType.DMA((moves,)),
        ],
        compiler_params=pltpu.CompilerParams(collective_id=cid, has_side_effects=True),
    )(*arrays)


def chip_of(me):
    return lax.rem(lax.div(me, 2), HEADS)


def chip_on(me, h, k):
    turn = (k % 2) * (1 - 2 * lax.rem(h, 2)) + (k // 2) * (2 - 4 * lax.div(h, 2))
    return me + 2 * turn, h + turn


def rows_at(ref, block, size):
    return ref.at[pl.ds(pl.multiple_of(block * size, size), size)]


def columns_at(ref, block, size):
    return ref.at[:, pl.ds(pl.multiple_of(block * size, 128), size)]


def swap_all(cid, x, count):
    def plan(me, ins, outs):
        peers = [lax.rem(me + k, count) for k in range(1, count)]
        moves = [(ins[0].at[p], outs[0].at[me], p) for p in peers]
        return peers, moves + [(ins[0].at[me], outs[0].at[me], None)]

    return exchange(cid, [x], [(x.shape, x.dtype)], count, plan)[0]


def first_exchange(cid, weights, output_rows):
    rows, width = weights[0].shape
    part = width // HEADS

    def plan(me, ins, outs):
        h = chip_of(me)
        targets = [chip_on(me, h, k) for k in (2, 1, 3)] + [(None, h)]
        at = pl.ds(pl.multiple_of(h * rows, rows), rows)
        moves = []
        for device, other in targets:
            for j in range(3):
                dst = outs[0].at[at, pl.ds(j * part, part)]
                moves.append((columns_at(ins[j], other, part), dst, device))
        for k in range(HEADS):
            dst = outs[0].at[pl.ds(k * rows, rows), pl.ds(3 * part, part)]
            moves.append((ins[3].at[:, pl.ds(k * part, part)], dst, None))
        return [p for p, _ in targets[:3]], moves

    shape = (HEADS * rows, 4 * part)
    return exchange(cid, [*weights, output_rows], [(shape, bf16)], 16, plan)[0]


def second_exchange(cid, gains, codes, gate, up, down, count):
    rows, width = gate.shape
    part = width // HEADS

    def plan(me, ins, outs):
        h = chip_of(me)
        g_in, c_in = ins[:2]
        everyone = [lax.rem(me + k, count) for k in range(1, count)]
        targets = [chip_on(me, h, k) for k in (1, 2, 3)] + [(None, h)]
        at = pl.ds(pl.multiple_of(h * rows, rows), rows)
        moves = [(g_in, outs[0].at[me], p) for p in everyone] + [(g_in, outs[0].at[me], None)]
        for k, (device, other) in zip((1, 2, 3, 0), targets):
            moves.append((c_in.at[other], outs[1].at[k], device))
        for w, out, column in ((2, 2, 0), (3, 2, part), (4, 3, 0)):
            for device, other in targets:
                dst = outs[out].at[at, pl.ds(column, part)]
                moves.append((columns_at(ins[w], other, part), dst, device))
        return everyone, moves

    return exchange(
        cid,
        [gains, codes, gate, up, down],
        [
            ((count, *gains.shape), gains.dtype),
            (codes.shape, codes.dtype),
            ((HEADS * rows, 2 * part), bf16),
            ((HEADS * rows, part), bf16),
        ],
        count + 16,
        plan,
    )


def return_columns(cid, x, pieces):
    rows = x.shape[0] // HEADS
    part = x.shape[1] // pieces

    def plan(me, ins, outs):
        h = chip_of(me)
        targets = [chip_on(me, h, k) for k in (1, 2, 3)] + [(None, h)]
        moves = []
        for device, other in targets:
            for j in range(pieces):
                src = ins[0].at[
                    pl.ds(pl.multiple_of(other * rows, rows), rows), pl.ds(j * part, part)
                ]
                moves.append((src, columns_at(outs[j], h, part), device))
        return [p for p, _ in targets[:3]], moves

    return exchange(
        cid, [x], [((rows, HEADS * part), x.dtype)] * pieces, 4 * pieces, plan
    )


STEP = 16


def reorder(x, planes, back):
    strip = x.shape[1] // (planes * PLANE)
    pieces = []
    for p in range(planes):
        for i in range(PLANE):
            n = (i % 2) * HEADS + i // 2 if back else (i % HEADS) * 2 + i // HEADS
            at = (p * PLANE + n) * strip
            pieces.append(x[:, at : at + strip])
    return jnp.concatenate(pieces, axis=1)


def reordered(arrays, planes):
    def kernel(*refs):
        for src, dst in zip(refs[: len(arrays)], refs[len(arrays) :]):

            def step(i, carry, src=src, dst=dst):
                at = pl.ds(pl.multiple_of(i * STEP, STEP), STEP)
                dst[at, :] = reorder(src[at, :], planes, False)
                return carry

            lax.fori_loop(0, src.shape[0] // STEP, step, 0)

    vmem = pl.BlockSpec(memory_space=pltpu.VMEM)
    return pl.pallas_call(
        kernel,
        out_shape=[jax.ShapeDtypeStruct(x.shape, x.dtype) for x in arrays],
        in_specs=[vmem] * len(arrays),
        out_specs=[vmem] * len(arrays),
        compiler_params=pltpu.CompilerParams(vmem_limit_bytes=32 << 20),
    )(*arrays)


def plane_stage(cid, partial, blocks, body, own, gathered):
    rows, width = blocks[0].shape
    half = rows // 2
    has = int(partial is not None)
    low, high = pl.ds(0, half), pl.ds(half, half)

    def kernel(*refs):
        part = refs[0] if has else None
        block_refs = refs[has : has + len(blocks)]
        rest = refs[has + len(blocks) :]
        own_refs, rest = rest[: len(own)], rest[len(own) :]
        everything, rest = (rest[0], rest[1:]) if gathered else (None, rest)
        by_x, by_y, over_x, over_y, sum_x, sum_y, mine, send, recv, out_send, out_recv = rest
        me = lax.axis_index("seq")
        h = chip_of(me)
        x_side, y_side = chip_on(me, h, 1)[0], chip_on(me, h, 2)[0]
        barrier = pltpu.get_barrier_semaphore()
        for device in (x_side, y_side):
            pl.semaphore_signal(barrier, inc=1, device_id=(device,), device_id_type=MESH)
        pl.semaphore_wait(barrier, 2)

        def to(device, src, dst, sends, recvs, n):
            return pltpu.make_async_remote_copy(
                src_ref=src, dst_ref=dst, send_sem=sends.at[n], recv_sem=recvs.at[n],
                device_id=(device,), device_id_type=MESH,
            )

        def block(k, first):
            return pl.ds(k * rows + (0 if first else half), half)

        if has:
            copies = [
                to(x_side, part.at[block(3, True)], over_x, send, recv, 0),
                to(y_side, part.at[block(3, False)], over_y, send, recv, 1),
                to(x_side, part.at[block(1, True)], by_x.at[low], send, recv, 2),
                to(y_side, part.at[block(2, False)], by_y.at[high], send, recv, 3),
                to(y_side, sum_y, by_y.at[low], send, recv, 4),
                to(x_side, sum_x, by_x.at[high], send, recv, 5),
            ]
            for copy in copies[:4]:
                copy.start()
            copies[0].wait_recv()
            sum_y[...] = (part[block(2, True), :].astype(f32) + over_x[...].astype(f32)).astype(bf16)
            copies[4].start()
            copies[1].wait_recv()
            sum_x[...] = (part[block(1, False), :].astype(f32) + over_y[...].astype(f32)).astype(bf16)
            copies[5].start()
            for copy in copies[:2]:
                copy.wait_send()
            for copy in copies[2:]:
                copy.wait()

        def step(i, carry):
            at = pl.ds(pl.multiple_of(i * STEP, STEP), STEP)
            total = None
            if has:
                total = part[at, :].astype(f32) + by_x[at, :].astype(f32) + by_y[at, :].astype(f32)
            body(i, at, total, block_refs, own_refs, mine)
            return carry

        lax.fori_loop(0, rows // STEP, step, 0)
        if gathered:
            from_x, from_y = everything.at[block(1, True)], everything.at[block(2, False)]
            copies = [
                to(x_side, mine.at[low], from_x, out_send, out_recv, 0),
                to(y_side, mine.at[high], from_y, out_send, out_recv, 1),
                to(x_side, mine.at[high], everything.at[block(1, False)], out_send, out_recv, 2),
                to(y_side, mine.at[low], everything.at[block(2, True)], out_send, out_recv, 3),
                to(y_side, from_x, everything.at[block(3, True)], out_send, out_recv, 4),
                to(x_side, from_y, everything.at[block(3, False)], out_send, out_recv, 5),
            ]
            keep = pltpu.make_async_copy(mine, everything.at[pl.ds(0, rows)], out_send.at[6])
            for copy in copies[:4]:
                copy.start()
            keep.start()
            copies[0].wait_recv()
            copies[4].start()
            copies[1].wait_recv()
            copies[5].start()
            for copy in copies[:2]:
                copy.wait_send()
            for copy in copies[2:]:
                copy.wait()
            keep.wait()

    vmem = pl.BlockSpec(memory_space=pltpu.VMEM)
    shapes = [jax.ShapeDtypeStruct(s, d) for s, d in own]
    if gathered:
        shapes.append(jax.ShapeDtypeStruct((HEADS * rows, width), bf16))
    whole, part_of = ((rows, width), (half, width)) if has else ((STEP, 128), (STEP, 128))
    return pl.pallas_call(
        kernel,
        out_shape=shapes,
        in_specs=[vmem] * (has + len(blocks)),
        out_specs=[vmem] * len(own) + [ANY] * int(gathered),
        scratch_shapes=[pltpu.VMEM(s, bf16) for s in (whole, whole, part_of, part_of, part_of, part_of)]
        + [pltpu.VMEM((rows, width), bf16)]
        + [pltpu.SemaphoreType.DMA((n,)) for n in (6, 6, 7, 6)],
        compiler_params=pltpu.CompilerParams(
            collective_id=cid, has_side_effects=True, vmem_limit_bytes=40 << 20
        ),
    )(*([partial] if has else []), *blocks)


def factor_of(x):
    return lax.rsqrt(jnp.mean(x * x, axis=-1, keepdims=True) + epsilon)


def norm_body(i, at, total, blocks, own, mine):
    tokens, gain = blocks
    x = tokens[at, :].astype(f32)
    mine[at, :] = (x * factor_of(x) * gain[...]).astype(bf16)


def residual_body(i, at, total, blocks, own, mine):
    tokens, gain = blocks
    x = tokens[at, :].astype(f32) + total
    own[0][at, :] = x
    mine[at, :] = (x * factor_of(x) * gain[...]).astype(bf16)


def accumulate(i, ref, product):
    part = product[:8] + product[8:]

    @pl.when(i == 0)
    def _():
        ref[...] = part

    @pl.when(i > 0)
    def _():
        ref[...] += part


def residual_grad_body(i, at, total, blocks, own, mine):
    residual, cotangent, gain = blocks
    x = residual[at, :]
    factor = factor_of(x)
    normed = x * factor
    accumulate(i, own[1], normed * total)
    scaled = total * gain[...]
    grad = cotangent[at, :].astype(f32) + factor * (
        scaled - normed * jnp.mean(normed * scaled, axis=-1, keepdims=True)
    )
    own[0][at, :] = grad
    mine[at, :] = grad.astype(bf16)


def last_body(planes):
    def body(i, at, total, blocks, own, mine):
        tokens, later, gain, residual, *outs = blocks
        x = tokens[at, :].astype(f32)
        factor = factor_of(x)
        normed = x * factor
        accumulate(i, own[1], normed * total)
        scaled = total * gain[...]
        grad = later[at, :] + factor * (
            scaled - normed * jnp.mean(normed * scaled, axis=-1, keepdims=True)
        )
        own[0][at, :] = reorder(grad, planes, True)
        result = residual[at, :]
        for out in outs:
            result = result + out[at, :].astype(f32)
        own[2][at, :] = reorder(result.astype(bf16), planes, True)

    return body


def carry_states(cid, keys, values, gains, planes, reverse):
    sent = bf16 if reverse else f32
    _, slots, size = keys.shape
    half = slots // 2

    def kernel(k_in, v_in, g_in, k_out, v_out, k_all, v_all, g_all, k_pre, v_pre, g_pre, k_run, v_run, g_run,
               k_far, v_far, g_far, k_base, v_base, k_mine, v_mine, s_send, s_recv, z_send, z_recv, b_send, b_recv):
        me = lax.axis_index("seq")
        h = chip_of(me)
        core = lax.rem(me, 2)
        z = lax.div(me, PLANE)
        sibling = me + 1 - 2 * core
        barrier = pltpu.get_barrier_semaphore()
        others = [me + PLANE * (lax.rem(z + k, planes) - z) for k in range(1, planes)]
        for device in (sibling, *others):
            pl.semaphore_signal(barrier, inc=1, device_id=(device,), device_id_type=MESH)
        pl.semaphore_wait(barrier, planes)

        def remote(src, dst, s, r, device):
            return pltpu.make_async_remote_copy(
                src_ref=src, dst_ref=dst, send_sem=s, recv_sem=r, device_id=(device,), device_id_type=MESH
            )

        k_base[...] = jnp.zeros_like(k_base)
        v_base[...] = jnp.zeros_like(v_base)
        copies = []
        for k in range(HEADS):
            chip = chip_on(me, h, k)[1]
            for j, (src, dst) in enumerate(((g_in, g_all), (k_in, k_all), (v_in, v_all))):
                n = 3 * k + j
                copies.append(remote(src.at[k], dst.at[chip, core], s_send.at[n], s_recv.at[n], sibling))
        for copy in copies:
            copy.start()
        for k in range(HEADS):
            chip = chip_on(me, h, k)[1]
            for src, dst in ((g_in, g_all), (k_in, k_all), (v_in, v_all)):
                dst[chip, core] = src[k]
        for copy in copies:
            copy.wait()
        k_run[...] = jnp.zeros_like(k_run)
        v_run[...] = jnp.zeros_like(v_run)
        g_run[...] = jnp.ones_like(g_run)
        order = [(c, d) for c in range(HEADS) for d in range(2)]
        for c, d in reversed(order) if reverse else order:
            k_pre[c, d] = k_run[...]
            v_pre[c, d] = v_run[...]
            g_pre[c, d] = g_run[...]
            gain = g_all[c, d]
            k_run[...] = gain[:, :1] * k_run[...] + k_all[c, d]
            v_run[...] = gain[:, :1] * v_run[...] + v_all[c, d]
            g_run[...] = gain * g_run[...]
        mine = pl.ds(pl.multiple_of(core * half, half), half)
        k_mine[...] = k_run[mine, :].astype(sent)
        v_mine[...] = v_run[mine, :].astype(sent)

        def along(k, go):
            step = -PLANE * k if reverse else PLANE * k
            device = me + step if go else me - step
            return [
                remote(src, dst.at[k - 1], z_send.at[n], z_recv.at[n], device)
                for n, src, dst in (
                    (3 * k - 3, g_run.at[mine], g_far),
                    (3 * k - 2, k_mine, k_far),
                    (3 * k - 1, v_mine, v_far),
                )
            ]

        def ahead(k):
            return z - k >= 0 if reverse else z + k < planes

        def behind(k):
            return z + k < planes if reverse else z - k >= 0

        for k in range(1, planes):
            @pl.when(ahead(k))
            def _(k=k):
                for copy in along(k, True):
                    copy.start()

        for k in reversed(range(1, planes)):
            @pl.when(behind(k))
            def _(k=k):
                for copy in along(k, False):
                    copy.wait_recv()
                gain = g_far[k - 1][:, :1]
                k_base[mine, :] = gain * k_base[mine, :] + k_far[k - 1].astype(f32)
                v_base[mine, :] = gain * v_base[mine, :] + v_far[k - 1].astype(f32)

        copies = [
            remote(k_base.at[mine], k_base.at[mine], b_send.at[0], b_recv.at[0], sibling),
            remote(v_base.at[mine], v_base.at[mine], b_send.at[1], b_recv.at[1], sibling),
        ]
        for copy in copies:
            copy.start()
        for copy in copies:
            copy.wait()
        for k in range(HEADS):
            chip = chip_on(me, h, k)[1]
            gain = g_pre[chip, core][:, :1]
            k_out[k] = gain * k_base[...] + k_pre[chip, core]
            v_out[k] = gain * v_base[...] + v_pre[chip, core]
        for k in range(1, planes):
            @pl.when(ahead(k))
            def _(k=k):
                for copy in along(k, True):
                    copy.wait_send()

    vmem = pl.BlockSpec(memory_space=pltpu.VMEM)
    wide = [pltpu.VMEM((HEADS, 2, slots, n), f32) for n in (size, size, 128)]
    state = [pltpu.VMEM((slots, n), f32) for n in (size, size, 128)]
    far = [pltpu.VMEM((planes - 1, half, n), d) for n, d in ((size, sent), (size, sent), (128, f32))]
    sends = [pltpu.VMEM((half, size), sent)] * 2
    semaphores = [12, 12, 3 * planes - 3, 3 * planes - 3, 2, 2]
    return pl.pallas_call(
        kernel,
        out_shape=[jax.ShapeDtypeStruct(keys.shape, f32)] * 2,
        in_specs=[vmem] * 3,
        out_specs=[vmem] * 2,
        scratch_shapes=wide + wide + state + far + state[:2] + sends
        + [pltpu.SemaphoreType.DMA((n,)) for n in semaphores],
        compiler_params=pltpu.CompilerParams(
            collective_id=cid, has_side_effects=True, vmem_limit_bytes=32 << 20
        ),
    )(keys, values, gains)


def rms_factor(value_rows):
    return lax.rsqrt(jnp.mean(value_rows * value_rows, axis=-1, keepdims=True) + epsilon)


def precise(form, left, right):
    return jnp.einsum(form, left, right, precision=highest, preferred_element_type=f32)


def plain(form, left, right):
    return jnp.einsum(form, left, right, preferred_element_type=f32)


def local(
    tokens,
    cotangent,
    gate_codes,
    lengths,
    mixer_gain,
    query_weight,
    key_weight,
    value_weight,
    head_gain,
    output_weight,
    feed_gain,
    gate_weight,
    up_weight,
    down_weight,
):
    count = lax.axis_size("seq")
    planes = count // PLANE
    me = lax.axis_index("seq")
    z, h, core = me // PLANE, (me // 2) % HEADS, me % 2
    rows, width = tokens.shape
    strip = query_weight.shape[0]
    head_size = width // HEADS
    lines = [
        [p * PLANE + c * 2 + k for p in range(planes) for k in range(2)] for c in range(HEADS)
    ]

    def gather_line(x):
        return lax.all_gather(x, "seq", axis=0, tiled=True, axis_index_groups=lines)

    def scatter_line(x):
        return lax.psum_scatter(
            x, "seq", scatter_dimension=0, tiled=True, axis_index_groups=lines
        )

    def shuffled(x):
        y = x.reshape(*x.shape[:-1], planes, HEADS, 2, strip)
        return jnp.swapaxes(y, -3, -2).reshape(x.shape)

    def restored(x):
        y = x.reshape(*x.shape[:-1], planes, 2, HEADS, strip)
        return jnp.swapaxes(y, -3, -2).reshape(x.shape)

    turns = [
        [(d, d - 2 * (d // 2 % HEADS) + 2 * (d // 2 % HEADS ^ k)) for d in range(count)]
        for k in range(HEADS)
    ]

    def send_on(x, k):
        return lax.ppermute(x, "seq", turns[k])

    def in_chip_order(parts):
        whole = jnp.stack(parts)
        return jnp.stack(
            [lax.dynamic_index_in_dim(whole, j ^ h, keepdims=False) for j in range(HEADS)]
        )

    gains = jnp.stack([mixer_gain, head_gain, feed_gain]).astype(f32)
    gains = jnp.pad(gains, ((0, 5), (0, 128 - strip)))
    codes = gate_codes.reshape(rows, HEADS, SLOTS).swapaxes(0, 1)
    (output_own,) = reordered([output_weight], planes)
    mixer_rows = first_exchange(0, (query_weight, key_weight, value_weight), output_own)
    mixer_line = gather_line(mixer_rows)
    gains_all, codes_all, feed_rows, down_rows = second_exchange(
        1, gains, codes, gate_weight, up_weight, down_weight, count
    )
    feed_weight = gather_line(feed_rows)
    down_line = gather_line(down_rows)
    gain_of = gains_all[:, :3, :strip].swapaxes(0, 1).reshape(3, width)
    gain_one, gain_two = shuffled(gain_of[0])[None], shuffled(gain_of[2])[None]
    head_gain_f = lax.dynamic_slice(gain_of[1], (h * head_size,), (head_size,))

    tokens_own, cotangent_own = reordered([tokens, cotangent], planes)
    (h1,) = plane_stage(2, None, [tokens_own, gain_one], norm_body, [], True)
    h1, cotangent_sent = lax.optimization_barrier((h1, cotangent_own))
    cotangent_parts = [cotangent_own] + [send_on(cotangent_sent, k) for k in (1, 2, 3)]

    decay = jax.nn.log_sigmoid(codes_all.astype(f32) / 256.0)
    block = z * PLANE + 2 * ((h ^ jnp.arange(HEADS))) + core
    first = (block * rows)[:, None]
    position = first + jnp.arange(rows)[None, :]
    order = jnp.arange(lengths.shape[0])
    first_token = jnp.sum(
        jnp.where(order[:, None] > order[None, :], lengths[None, :], 0), axis=1
    )
    seen = jnp.sum(
        jnp.where(
            (first_token[None, None, :] <= position[:, :, None])
            & (first_token[None, None, :] >= first[:, :, None]),
            1,
            0,
        ),
        axis=2,
    )
    places = jnp.arange(rows)
    before = places[:, None] >= places[None, :]
    same = jnp.where(before[None] & (seen[:, :, None] == seen[:, None, :]), 1.0, 0.0).astype(f32)
    fresh = jnp.where(seen == 0, 1.0, 0.0).astype(f32)[:, :, None]
    logsum = precise("ts,bsm->btm", before.astype(f32), decay)
    grow = jnp.exp(logsum)
    back = jnp.exp(-logsum) * -jnp.expm1(decay)
    tail = jnp.where(seen == seen[:, -1:], 1.0, 0.0).astype(f32)[:, :, None]
    weights = grow[:, -1:] * back * tail
    carried = fresh[:, -1] * grow[:, -1]
    carried = jnp.broadcast_to(carried[:, :, None], (HEADS, SLOTS, 128))

    blocked = (HEADS, rows, head_size)
    mixer_weight = mixer_line[:, : 3 * head_size]
    projected = jnp.dot(h1, mixer_weight, preferred_element_type=f32).astype(bf16)
    query = projected[:, :head_size].reshape(blocked)
    key = projected[:, head_size : 2 * head_size].reshape(blocked)
    value = projected[:, 2 * head_size :].reshape(blocked)
    query_f = query.astype(f32)

    key_state, value_state = carry_states(
        3,
        precise("bsm,bsd->bmd", weights, key.astype(f32)),
        precise("bsm,bsd->bmd", weights, value.astype(f32)),
        carried,
        planes,
        False,
    )

    affinity = plain("btd,bsd->bts", query, key) * same
    score = grow * precise("bts,bsm->btm", affinity, back) + grow * fresh * precise(
        "btd,bmd->btm", query_f, key_state
    )
    probs = jax.nn.softmax(score, axis=-1)
    lifted = probs * grow
    mixing = (precise("btm,bsm->bts", lifted, back) * same).astype(bf16)
    entry = lifted * fresh
    slot_out = plain("bts,bsd->btd", mixing, value) + precise("btm,bmd->btd", entry, value_state)
    head_factor = rms_factor(slot_out)
    unit_heads = slot_out * head_factor
    normed_heads = (unit_heads * head_gain_f).astype(bf16).reshape(HEADS * rows, head_size)

    quarter = planes // HEADS
    output_line = mixer_line[:, 3 * head_size :].reshape(planes, 2, HEADS, strip, head_size)
    pieces = [
        lax.dynamic_slice_in_dim(output_line, (h ^ k) * quarter, quarter)
        for k in range(HEADS)
    ]
    pieces = in_chip_order([pieces[0]] + [send_on(pieces[k], k) for k in (1, 2, 3)])
    out_weight = pieces.transpose(1, 0, 2, 4, 3, 5).reshape(head_size, width)
    mixed = jnp.dot(normed_heads, out_weight, preferred_element_type=f32).astype(bf16)
    residual, h2 = plane_stage(
        4, mixed, [tokens_own, gain_two], residual_body, [((rows, width), f32)], True
    )

    h2, *cotangent_parts = lax.optimization_barrier((h2, *cotangent_parts))
    cotangent_all = jnp.concatenate(cotangent_parts)
    part = down_line.shape[1]
    both = jnp.dot(h2, feed_weight, preferred_element_type=f32)
    sigma = jax.nn.sigmoid(both[:, :part])
    hidden = (both[:, :part] * sigma * both[:, part:]).astype(bf16)
    hidden, both = lax.optimization_barrier((hidden, both))
    down_part = plain("td,tf->df", cotangent_all, hidden).astype(bf16)
    down_part, down_line = lax.optimization_barrier((down_part, down_line))
    down_sums = scatter_line(down_part)
    gate, upward = both[:, :part], both[:, part:]
    sigma = jax.nn.sigmoid(gate)
    hidden_grad = jnp.dot(cotangent_all, down_line, preferred_element_type=f32)
    gate_back = (hidden_grad * upward * sigma * (1.0 + gate * (1.0 - sigma))).astype(bf16)
    up_back = (hidden_grad * (gate * sigma)).astype(bf16)
    both_back = jnp.concatenate([gate_back, up_back], axis=1)
    feed_part = plain("td,tf->df", h2, both_back).astype(bf16)
    feed_part, both_back = lax.optimization_barrier((feed_part, both_back))
    feed_sums = scatter_line(feed_part)
    feed_in = plain("tf,df->td", both_back, feed_weight).astype(bf16)
    residual_grad, feed_gain_part, mixed_grad = plane_stage(
        5,
        feed_in,
        [residual, cotangent_own, gain_two],
        residual_grad_body,
        [((rows, width), f32), ((8, width), f32)],
        True,
    )
    mixed_grad, hidden = lax.optimization_barrier((mixed_grad, hidden))
    feed_out = plain("tf,df->td", hidden, down_line).astype(bf16)
    feed_outs = [feed_out[:rows]]
    feed_outs += [send_on(feed_out[k * rows : (k + 1) * rows], k) for k in (1, 2, 3)]

    mixed_grad, down_sums = lax.optimization_barrier((mixed_grad, down_sums))
    heads_grad = plain("td,fd->tf", mixed_grad, out_weight).reshape(blocked)
    head_gain_part = jnp.sum(unit_heads * heads_grad, axis=(0, 1))
    scaled_heads = heads_grad * head_gain_f
    out_back = (
        head_factor
        * (scaled_heads - unit_heads * jnp.mean(unit_heads * scaled_heads, axis=-1, keepdims=True))
    ).astype(bf16)
    out_back_f = out_back.astype(f32)
    mixing_grad = plain("btd,bsd->bts", out_back, value) * same
    local_value = plain("bts,btd->bsd", mixing, out_back)
    lifted_grad = grow * precise("bts,bsm->btm", mixing_grad, back) + grow * fresh * precise(
        "btd,bmd->btm", out_back_f, value_state
    )
    score_grad = probs * (lifted_grad - jnp.sum(probs * lifted_grad, axis=-1, keepdims=True))
    inner_grad = grow * score_grad
    state_grad = inner_grad * fresh
    affinity_grad = (precise("btm,bsm->bts", inner_grad, back) * same).astype(bf16)
    first_key = precise("btm,btd->bmd", state_grad, query_f)
    first_value = precise("btm,btd->bmd", entry, out_back_f)
    first_key, feed_outs = lax.optimization_barrier((first_key, feed_outs))
    later_key, later_value = carry_states(6, first_key, first_value, carried, planes, True)

    query_back = plain("bts,bsd->btd", affinity_grad, key) + precise(
        "btm,bmd->btd", state_grad, key_state
    )
    key_back = plain("bts,btd->bsd", affinity_grad, query) + precise(
        "bsm,bmd->bsd", weights, later_key
    )
    value_back = local_value + precise("bsm,bmd->bsd", weights, later_value)
    backs = jnp.concatenate(
        [
            x.astype(bf16).reshape(HEADS * rows, head_size)
            for x in (query_back, key_back, value_back)
        ],
        axis=1,
    )
    out_part = plain("tf,td->fd", normed_heads, mixed_grad).astype(bf16)
    out_part = out_part.reshape(quarter, HEADS, 2, strip, HEADS, head_size)
    pieces = [
        lax.dynamic_index_in_dim(out_part, h ^ k, 1, keepdims=False) for k in range(HEADS)
    ]
    pieces = in_chip_order([pieces[0]] + [send_on(pieces[k], k) for k in (1, 2, 3)])
    out_part = pieces.transpose(0, 1, 2, 4, 3, 5).reshape(width, head_size)
    mixer_part = plain("td,tf->df", h1, backs).astype(bf16)
    mixer_part = jnp.concatenate([mixer_part, out_part], axis=1)
    mixer_part, feed_sums = lax.optimization_barrier((mixer_part, feed_sums))
    mixer_sums = scatter_line(mixer_part)
    mixer_in = plain("tf,df->td", backs, mixer_weight).astype(bf16)
    input_grad, mixer_gain_part, block_out = plane_stage(
        7,
        mixer_in,
        [tokens_own, residual_grad, gain_one, residual, *feed_outs],
        last_body(planes),
        [((rows, width), f32), ((8, width), f32), ((rows, width), bf16)],
        False,
    )

    (down_grad,) = return_columns(8, down_sums, 1)
    gate_grad, up_grad = return_columns(9, feed_sums, 2)
    query_grad, key_grad, value_grad = return_columns(10, mixer_sums[:, : 3 * head_size], 3)
    out_sums = mixer_sums[:, 3 * head_size :].reshape(HEADS, strip, head_size)
    out_sums = out_sums.swapaxes(0, 1).reshape(strip, width)

    head_whole = lax.dynamic_update_slice(
        jnp.zeros((width,), f32), head_gain_part, (h * head_size,)
    )
    gain_parts = jnp.stack(
        [
            restored(jnp.sum(mixer_gain_part, axis=0)),
            head_whole,
            restored(jnp.sum(feed_gain_part, axis=0)),
        ]
    )
    gain_parts = gain_parts.reshape(3, count, strip).swapaxes(0, 1)
    gain_parts = jnp.pad(gain_parts, ((0, 0), (0, 5), (0, 128 - strip)))
    gain_sums = jnp.sum(swap_all(11, gain_parts, count), axis=0)[:3, :strip]
    return (
        block_out,
        input_grad,
        gain_sums[0],
        query_grad.astype(f32),
        key_grad.astype(f32),
        value_grad.astype(f32),
        gain_sums[1],
        restored(out_sums).astype(f32),
        gain_sums[2],
        gate_grad.astype(f32),
        up_grad.astype(f32),
        down_grad.astype(f32),
    )


def solution(mesh):
    split, line = P("seq", None), P("seq")
    return jax.shard_map(
        local,
        mesh=mesh,
        in_specs=(split, split, split, P(), line, split, split, split, line, split, line, split, split, split),
        out_specs=(split, split, line, split, split, split, line, split, line, split, split, split),
        check_vma=False,
    )
```

time: 817 us -> 611 us (0.75)
  Pallas kernels: 504 us -> 312 us
  other arithmetic: 66.4 us -> 27.6 us
  waiting for transfers between devices: 44.7 us -> 72.4 us
  starting transfers between devices: 0.54 us -> 14.3 us
  local copies, waits for them, and re-layouts: 62.1 us -> 48.4 us
    pallas_call x20 -> x6, Pallas kernels: 504 us -> 107 us  [exchange(): pl.pallas_call(kernel, out_shape=[jax.ShapeDtypeStruct(s, d) for s, d in...]
    pallas_call x0 -> x8, Pallas kernels: none -> 205 us  [the longest x4 158 us: plane_stage(): pl.pallas_call(kernel, out_shape=shapes, in_specs=[vmem] * (has + len(blo...]
    all_gather x4 -> x3, waiting for transfers between devices: 0.06 us -> 50.9 us  [gather_line(): return lax.all_gather(x, 'seq', axis=0, tiled=True, axis_index_groups=lines)]
    reduce_scatter x4 -> x3, waiting for transfers between devices: 44 us -> 3.27 us  [scatter_line(): lax.psum_scatter(x, 'seq', scatter_dimension=0, tiled=True, axis_index_gr...]
    ppermute x0 -> x12, waiting for transfers between devices: none -> 18.1 us  [send_on(): return lax.ppermute(x, 'seq', turns[k])]
    convert_element_type x8 -> x2, other arithmetic: 19 us -> 1.11 us  [the longest x1 1.06 us: local(): hidden = (both[:, :part] * sigma * both[:, part:]).astype(bf16)]
    ppermute x0 -> x12, starting transfers between devices: none -> 14.1 us  [send_on(): return lax.ppermute(x, 'seq', turns[k])]
    add x8 -> x0, other arithmetic: 14 us -> none  [the longest x4 5.79 us: summed(): return parts[0] + parts[1] + parts[2] + parts[3]]
  transfers between devices with their start and end apart: 8 -> 18, of which waited for: 1 -> 6; matrix products, arithmetic and copies ran while one was open for 22% -> 27% of each run, Pallas kernels for 49% -> 47%
where the time goes in v2:
time: 611 us; the launch traced here: 603 us
  Pallas kernels  312 us (51%)
  matrix products  112 us (18%)
  waiting for transfers between devices  72.4 us (12%)
  local copies, waits for them, and re-layouts  48.4 us (8%)
  other arithmetic  27.6 us (5%)
  between operations  15.9 us (3%)
  starting transfers between devices  14.3 us (2%)
    pallas_call x4, Pallas kernels, plane_stage(): pl.pallas_call(kernel, out_shape=shapes, in_specs=[vmem] * (has + len(blo...  158 us
    pallas_call x6, Pallas kernels, exchange(): pl.pallas_call(kernel, out_shape=[jax.ShapeDtypeStruct(s, d) for s, d in...  107 us
    dot_general x14, matrix products, plain(): return jnp.einsum(form, left, right, preferred_element_type=f32)  66.4 us
    all_gather x3, waiting for transfers between devices, gather_line(): return lax.all_gather(x, 'seq', axis=0, tiled=True, axis_index_groups=lines)  50.9 us
    pallas_call x2, Pallas kernels, carry_states(): pl.pallas_call(kernel, out_shape=[jax.ShapeDtypeStruct(keys.shape, f32)]...  45.1 us
    unnamed x136, local copies, waits for them, and re-layouts  19.2 us
    ppermute x12, waiting for transfers between devices, send_on(): return lax.ppermute(x, 'seq', turns[k])  18.1 us
    ppermute x12, starting transfers between devices, send_on(): return lax.ppermute(x, 'seq', turns[k])  14.1 us
  transfers between devices with their start and end apart: 18, of which 6 were waited for; matrix products, arithmetic and copies ran while one was open for 27% of the time, Pallas kernels for 47%

profile of v2, /device:TPU:0, one launch (start us, length us, event | category | flops | bytes accessed | tf_op | source)
XLA Modules:
  0.0 603.0 jit_solution(9501360006196122112)
XLA Ops:
  9.2 19.2 %shard_map.233 = bf16[256,2048]{1,0:T(8,128)(2,1)} custom-call(bf16[64,2048]{1,0:T(8,128)(2,1)} %refs_0_.5, bf16[64,2048]{1,0:T(8,128)(2,1)} %refs_1_.3, bf16[64,2048]{1,0:T(8,128)(2,1)} %refs_2_.3, bf16[64,2048]{1,0:T(8,128)(2,1)} %copy-done.12), custom_call_target="tpu_custom_call" | custom-call | tf_op jit(solution)/shard_map/pallas_call | solution.py:49
  30.2 36.8 %shard_map.229 = (f32[32,8,128]{2,1,0:T(8,128)}, s32[4,160,64]{2,1,0:T(8,128)}, bf16[256,2816]{1,0:T(8,128)(2,1)}, bf16[256,1408]{1,0:T(8,128)(2,1)}) custom-call(f32[8,128]{1,0:T(8,128)} %fusion.54.refs_0_, s32[4,160,64]{2,1,0:T(8,128)} %bitcast.170, bf16[64,5632]{1,0:T(8,128)(2,1)} %refs_2_.2, bf16[64,5632]{1,0:T(8,128)(2,1)} %refs_3_.1, ...), custom_call_target="tpu_custom_call" | custom-call | tf_op jit(solution)/shard_map/pallas_call | solution.py:49
  68.2 1.7 shard_map.230
  70.0 24.9 %shard_map.231 = bf16[640,2048]{1,0:T(8,128)(2,1)S(1)} custom-call(bf16[160,2048]{1,0:T(8,128)(2,1)S(1)} %get-tuple-element.60.refs_0_.refs_1_, f32[1,2048]{1,0:T(1,128)S(1)} %broadcast_in_dim_reshape.6.refs_1_.refs_3_), custom_call_target="tpu_custom_call" | custom-call | tf_op jit(solution)/shard_map/pallas_call | solution.py:289
  101.2 8.8 %all-gather.4.cloned.1.call-done = bf16[2048,2048]{1,0:T(8,128)(2,1)} async-done(((bf16[256,2048]{1,0:T(8,128)(2,1)}), bf16[2048,2048]{1,0:T(8,128)(2,1)}) %all-gather.4.cloned.1.call-update) | async-done | bytes 8388624 | tf_op jit(solution)/shard_map/all_gather | solution.py:532
  110.0 1.6 slice-done
  111.8 2.5 collective-permute-start.2
  115.3 7.6 %fusion.6 = bf16[640,1536]{1,0:T(8,128)(2,1)S(1)} fusion(bf16[640,2048]{1,0:T(8,128)(2,1)S(1)} %copy-done.1, bf16[2048,2048]{1,0:T(8,128)(2,1)} %all-gather.4.cloned.1.call-done), kind=kOutput, calls=%fused_computation.15 | convolution fusion | flops 4027514880 | bytes 10878976 | tf_op jit(solution)/shard_map/dot_general | solution.py:612
  124.5 23.7 %shard_map.234 = (f32[4,64,512]{2,1,0:T(8,128)S(1)}, f32[4,64,512]{2,1,0:T(8,128)S(1)}) custom-call(f32[4,64,512]{2,1,0:T(8,128)S(1)} %fusion.29.k_in, f32[4,64,512]{2,1,0:T(8,128)S(1)} %fusion.28.v_in, f32[4,64,128]{2,1,0:T(8,128)S(1)} %broadcast_in_dim.77.g_in), custom_call_target="tpu_custom_call" | custom-call | tf_op jit(solution)/shard_map/pallas_call | solution.py:479
  157.3 1.6 copy.139
  160.2 1.5 convolution_convert_fusion.5.refs_0_
  161.8 54.8 %shard_map.235 = (f32[160,2048]{1,0:T(8,128)S(1)}, bf16[640,2048]{1,0:T(8,128)(2,1)S(1)}) custom-call(bf16[640,2048]{1,0:T(8,128)(2,1)S(1)} %convolution_convert_fusion.5.refs_0_, bf16[160,2048]{1,0:T(8,128)(2,1)S(1)} %get-tuple-element.60.refs_0_.refs_1_, f32[1,2048]{1,0:T(1,128)S(1)} %broadcast_in_dim_reshape.7.refs_2_.refs_3_), custom_call_target="tpu_custom_call" | custom-call | tf_op jit(solution)/shard_map/pallas_call | solution.py:289
  216.6 1.6 copy-done.18
  219.9 2.0 constant_dynamic-update-slice_fusion.1
  221.9 2.0 constant_dynamic-update-slice_fusion
  223.9 11.9 %fusion.68 = f32[640,2816]{1,0:T(8,128)S(1)} fusion(bf16[640,2048]{1,0:T(8,128)(2,1)} %copy-done.18, bf16[2048,2816]{1,0:T(8,128)(2,1)} %all-gather.6.cloned.1.call-done), kind=kOutput, calls=%fused_computation.157 | convolution fusion | flops 7381975040 | bytes 21364736 | tf_op jit(solution)/shard_map/dot_general | solution.py:656
  236.9 1.8 copy-done.35
  240.0 9.1 %convolution_convert_fusion.2 = bf16[2048,1408]{1,0:T(8,128)(2,1)} fusion(bf16[640,2048]{1,0:T(8,128)(2,1)} %constant_dynamic-update-slice_fusion, bf16[640,1408]{1,0:T(8,128)(2,1)S(1)} %fusion.5), kind=kOutput, calls=%fused_computation.4 | convolution fusion | flops 3693871104 | bytes 10190848 | tf_op jit(solution)/shard_map/td,tf->df/dot_general | solution.py:501
  249.1 42.1 %all-gather.8.cloned.1.call-done = bf16[2048,1408]{1,0:T(8,128)(2,1)} async-done(((bf16[256,1408]{1,0:T(8,128)(2,1)}), bf16[2048,1408]{1,0:T(8,128)(2,1)}) %all-gather.8.cloned.1.call-update) | async-done | bytes 5767184 | tf_op jit(solution)/shard_map/all_gather | solution.py:532
  291.2 10.6 %multiply_convert_fusion.1 = (bf16[640,1408]{1,0:T(8,128)(2,1)S(1)}, bf16[640,1408]{1,0:T(8,128)(2,1)S(1)}) fusion(f32[640,2816]{1,0:T(8,128)} %copy-done.35, bf16[640,2048]{1,0:T(8,128)(2,1)} %constant_dynamic-update-slice_fusion, bf16[2048,1408]{1,0:T(8,128)(2,1)} %all-gather.8.cloned.1.call-done), kind=kOutput, calls=%fused_computation.13 | convolution fusion | flops 3702702080 | bytes 19202048 | tf_op jit(solution)/shard_map/dot_general | solution.py:665
  301.8 2.1 pad_maximum_fusion.1
  304.8 12.0 %convolution_convert_fusion = bf16[2048,2816]{1,0:T(8,128)(2,1)} fusion(bf16[640,2048]{1,0:T(8,128)(2,1)S(1)} %copy-done.19, bf16[640,1408]{1,0:T(8,128)(2,1)S(1)} %get-tuple-element.109, bf16[640,1408]{1,0:T(8,128)(2,1)S(1)} %get-tuple-element.108), kind=kOutput, calls=%fused_computation.1 | convolution fusion | flops 7394951168 | bytes 17760256 | tf_op jit(solution)/shard_map/td,tf->df/dot_general | solution.py:501
  316.9 4.7 reshape.262
  321.6 11.7 %convolution_convert_fusion.4.refs_0_ = bf16[640,2048]{1,0:T(8,128)(2,1)S(1)} fusion(bf16[640,2816]{1,0:T(8,128)(2,1)} %pad_maximum_fusion.1, bf16[2048,2816]{1,0:T(8,128)(2,1)} %all-gather.6.cloned.1.call-done), kind=kOutput, calls=%fused_computation.18 | convolution fusion | flops 7383285760 | bytes 17760256 | tf_op jit(solution)/shard_map/tf,df->td/dot_general | solution.py:501
  333.3 49.5 %shard_map.236 = (f32[160,2048]{1,0:T(8,128)S(1)}, f32[8,2048]{1,0:T(8,128)S(1)}, bf16[640,2048]{1,0:T(8,128)(2,1)S(1)}) custom-call(bf16[640,2048]{1,0:T(8,128)(2,1)S(1)} %convolution_convert_fusion.4.refs_0_, f32[160,2048]{1,0:T(8,128)S(1)} %get-tuple-element.79.refs_1_.refs_4_, bf16[160,2048]{1,0:T(8,128)(2,1)S(1)} %get-tuple-element.69.refs_2_, ...), custom_call_target="tpu_custom_call" | custom-call | tf_op jit(solution)/shard_map/pallas_call | solution.py:289
  382.8 8.5 %convolution_convert_fusion.3 = bf16[640,2048]{1,0:T(8,128)(2,1)S(1)} fusion(bf16[640,1408]{1,0:T(8,128)(2,1)S(1)} %copy-done.48, bf16[2048,1408]{1,0:T(8,128)(2,1)} %all-gather.8.cloned.1.call-done), kind=kOutput, calls=%fused_computation.17 | convolution fusion | flops 3692298240 | bytes 10190848 | tf_op jit(solution)/shard_map/tf,df->td/dot_general | solution.py:501
  396.2 4.6 multiply_reduce_fusion
  405.6 6.1 %collective-permute-done.8.refs_8_ = bf16[160,2048]{1,0:T(8,128)(2,1)} collective-permute-done((bf16[160,2048]{1,0:T(8,128)(2,1)}, bf16[160,2048]{1,0:T(8,128)(2,1)}, u32[]{:S(2)}, u32[]{:S(2)}) %collective-permute-start.8) | collective-permute-done | bytes 655392 | tf_op jit(solution)/shard_map/ppermute | solution.py:553
  411.6 12.0 %collective-permute-done.7.refs_7_ = bf16[160,2048]{1,0:T(8,128)(2,1)} collective-permute-done((bf16[160,2048]{1,0:T(8,128)(2,1)}, bf16[160,2048]{1,0:T(8,128)(2,1)}, u32[]{:S(2)}, u32[]{:S(2)}) %collective-permute-start.7) | collective-permute-done | bytes 655392 | tf_op jit(solution)/shard_map/ppermute | solution.py:553
  423.7 3.2 convolution_convert_fusion.6
  426.9 4.7 reshape.255
  431.6 2.2 constant_dynamic-slice_fusion.7
  438.2 21.4 %shard_map.237 = (f32[4,64,512]{2,1,0:T(8,128)S(1)}, f32[4,64,512]{2,1,0:T(8,128)S(1)}) custom-call(f32[4,64,512]{2,1,0:T(8,128)S(1)} %copy-done.7, f32[4,64,512]{2,1,0:T(8,128)S(1)} %fusion.25.v_in, f32[4,64,128]{2,1,0:T(8,128)S(1)} %broadcast_in_dim.77.g_in), custom_call_target="tpu_custom_call" | custom-call | tf_op jit(solution)/shard_map/pallas_call | solution.py:479
  465.6 7.6 %convolution_convert_fusion.1 = bf16[2048,1536]{1,0:T(8,128)(2,1)} fusion(bf16[640,2048]{1,0:T(8,128)(2,1)S(1)} %copy-done.2, bf16[640,512]{1,0:T(8,128)(2,1)S(1)} %bitcast.175, bf16[640,512]{1,0:T(8,128)(2,1)S(1)} %bitcast.177, bf16[640,512]{1,0:T(8,128)(2,1)S(1)} %bitcast.173), kind=kOutput, calls=%fused_computation.3 | convolution fusion | flops 4035575808 | bytes 10878976 | tf_op jit(solution)/shard_map/td,tf->df/dot_general | solution.py:501
  473.8 1.6 pad_maximum_fusion.4
  475.4 8.3 %pad_maximum_fusion = bf16[2048,2048]{1,0:T(8,128)(2,1)} fusion(bf16[2048,512]{1,0:T(8,128)(2,1)} %bitcast.159, bf16[2048,1536]{1,0:T(8,128)(2,1)} %convolution_convert_fusion.1), kind=kLoop, calls=%fused_computation.2 | loop fusion | flops 16777216 | bytes 16777216 | tf_op jit(solution)/shard_map/concatenate | solution.py:731
  483.8 11.9 %shard_map.242 = bf16[64,5632]{1,0:T(8,128)(2,1)} custom-call(bf16[256,1408]{1,0:T(8,128)(2,1)} %reduce-scatter.4.cloned.1.call-done.refs_0_), custom_call_target="tpu_custom_call" | custom-call | tf_op jit(solution)/shard_map/pallas_call | solution.py:49
  497.0 7.6 %fusion.9.refs_0_ = bf16[640,2048]{1,0:T(8,128)(2,1)S(1)} fusion(bf16[2048,2048]{1,0:T(8,128)(2,1)} %all-gather.4.cloned.1.call-done, bf16[640,512]{1,0:T(8,128)(2,1)} %bitcast.176, bf16[640,512]{1,0:T(8,128)(2,1)} %bitcast.178, bf16[640,512]{1,0:T(8,128)(2,1)S(1)} %bitcast.174), kind=kOutput, calls=%fused_computation.16 | convolution fusion | flops 4033740800 | bytes 10878976 | tf_op jit(solution)/shard_map/tf,df->td/dot_general | solution.py:501
  504.6 29.0 %shard_map.238 = (f32[160,2048]{1,0:T(8,128)S(1)}, f32[8,2048]{1,0:T(8,128)S(1)}, bf16[160,2048]{1,0:T(8,128)(2,1)S(1)}) custom-call(bf16[640,2048]{1,0:T(8,128)(2,1)S(1)} %fusion.9.refs_0_, bf16[160,2048]{1,0:T(8,128)(2,1)S(1)} %get-tuple-element.60.refs_0_.refs_1_, f32[160,2048]{1,0:T(8,128)S(1)} %copy-done.9, f32[1,2048]{1,0:T(1,128)S(1)} %copy-done.17, ...), custom_call_target="tpu_custom_call" | custom-call | tf_op jit(solution)/shard_map/pallas_call | solution.py:289
  535.5 8.4 %shard_map.239 = f32[32,8,128]{2,1,0:T(8,128)} custom-call(f32[32,8,128]{2,1,0:T(8,128)} %pad.12.refs_0_), custom_call_target="tpu_custom_call" | custom-call | tf_op jit(solution)/shard_map/pallas_call | solution.py:49
  544.9 2.3 convert_element_type.133
  547.7 20.5 %shard_map.241 = (bf16[64,5632]{1,0:T(8,128)(2,1)}, bf16[64,5632]{1,0:T(8,128)(2,1)}) custom-call(bf16[256,2816]{1,0:T(8,128)(2,1)} %reduce-scatter.6.cloned.1.call-done.refs_0_), custom_call_target="tpu_custom_call" | custom-call | tf_op jit(solution)/shard_map/pallas_call | solution.py:49
  568.2 2.4 convert_element_type.131
  571.8 3.3 reduce-scatter.8.cloned.1.call-done
  575.1 2.1 slice.129.refs_0_
  577.2 10.2 %shard_map.240 = (bf16[64,2048]{1,0:T(8,128)(2,1)}, bf16[64,2048]{1,0:T(8,128)(2,1)}, bf16[64,2048]{1,0:T(8,128)(2,1)}) custom-call(bf16[256,1536]{1,0:T(8,128)(2,1)} %slice.129.refs_0_), custom_call_target="tpu_custom_call" | custom-call | tf_op jit(solution)/shard_map/pallas_call | solution.py:49
  587.4 1.8 convert_element_type.123
  590.4 1.8 reshape.258
  (258 shorter events, 59.9 us)
Async XLA Ops:
  7.2 102.9 %all-gather.4.cloned.1.call-start = ((), (), s32[]{:S(2)}) async-start(), calls=%async_computation.3 | async-start | bytes 9437184 | tf_op jit(solution)/shard_map/all_gather | solution.py:532
  8.2 20.4 %copy-start.59 = (s32[160,256]{1,0:T(8,128)S(1)}, s32[160,256]{1,0:T(8,128)}, u32[]{:S(2)}) copy-start(s32[160,256]{1,0:T(8,128)} %param.16) | copy-start | bytes 491524
  8.2 21.4 %copy-start.60 = (bf16[64]{0:T(256)(128)(2,1)S(1)}, bf16[64]{0:T(256)(128)(2,1)}, u32[]{:S(2)}) copy-start(bf16[64]{0:T(256)(128)(2,1)} %param.24) | copy-start | bytes 388
  8.2 21.4 %copy-start.61 = (bf16[64]{0:T(256)(128)(2,1)S(1)}, bf16[64]{0:T(256)(128)(2,1)}, u32[]{:S(2)}) copy-start(bf16[64]{0:T(256)(128)(2,1)} %param.22) | copy-start | bytes 388
  8.2 21.4 %copy-start.62 = (bf16[64]{0:T(256)(128)(2,1)S(1)}, bf16[64]{0:T(256)(128)(2,1)}, u32[]{:S(2)}) copy-start(bf16[64]{0:T(256)(128)(2,1)} %param.18) | copy-start | bytes 388
  28.5 39.7 %copy-start.13 = (bf16[160,2048]{1,0:T(8,128)(2,1)S(1)}, bf16[160,2048]{1,0:T(8,128)(2,1)}, u32[]{:S(2)}) copy-start(bf16[160,2048]{1,0:T(8,128)(2,1)} %refs_0_.3) | copy-start | bytes 1966084
  28.5 39.7 %copy-start.14 = (bf16[160,2048]{1,0:T(8,128)(2,1)S(1)}, bf16[160,2048]{1,0:T(8,128)(2,1)}, u32[]{:S(2)}) copy-start(bf16[160,2048]{1,0:T(8,128)(2,1)} %refs_1_.2) | copy-start | bytes 1966084
  28.5 195.4 %all-gather.6.cloned.1.call-start = ((), (), s32[]{:S(2)}) async-start(), calls=%async_computation.4 | async-start | bytes 12976128 | tf_op jit(solution)/shard_map/all_gather | solution.py:532
  67.1 224.1 %all-gather.8.cloned.1.call-start = ((), (), s32[]{:S(2)}) async-start(), calls=%async_computation.5 | async-start | bytes 6488064 | tf_op jit(solution)/shard_map/all_gather | solution.py:532
  68.2 30.2 %copy-start.16 = (f32[1,2048]{1,0:T(1,128)}, f32[1,2048]{1,0:T(1,128)S(1)}, u32[]{:S(2)}) copy-start(f32[1,2048]{1,0:T(1,128)S(1)} %broadcast_in_dim_reshape.6.refs_1_.refs_3_) | copy-start | bytes 24580
  68.2 30.4 %copy-start.63 = (s32[4]{0:T(128)S(1)}, s32[4]{0:T(128)}, u32[]{:S(2)}) copy-start(s32[4]{0:T(128)} %param.17) | copy-start | bytes 52
  68.2 31.4 %copy-start.56 = (s32[4,160,64]{2,1,0:T(8,128)S(1)}, s32[4,160,64]{2,1,0:T(8,128)}, u32[]{:S(2)}) copy-start(s32[4,160,64]{2,1,0:T(8,128)} %get-tuple-element.59) | copy-start | bytes 491524
  96.4 121.8 %collective-permute-start.5 = (bf16[160,2048]{1,0:T(8,128)(2,1)S(1)}, bf16[160,2048]{1,0:T(8,128)(2,1)}, u32[]{:S(2)}, u32[]{:S(2)}) collective-permute-start(bf16[160,2048]{1,0:T(8,128)(2,1)S(1)} %get-tuple-element.69.refs_2_), channel_id=1, source_target_pairs={{0,6},{1,7},{2,4},{3,5},{4,2},{5,3},{6,0},{7,1},{8,14},{9,15},{10,... | collective-permute-start | bytes 1966088 | tf_op jit(solution)/shard_map/ppermute | solution.py:553
  97.8 120.3 %collective-permute-start.4 = (bf16[160,2048]{1,0:T(8,128)(2,1)S(1)}, bf16[160,2048]{1,0:T(8,128)(2,1)}, u32[]{:S(2)}, u32[]{:S(2)}) collective-permute-start(bf16[160,2048]{1,0:T(8,128)(2,1)S(1)} %get-tuple-element.69.refs_2_), channel_id=1, source_target_pairs={{0,4},{1,5},{2,6},{3,7},{4,0},{5,1},{6,2},{7,3},{8,12},{9,13},{10,... | collective-permute-start | bytes 1966088 | tf_op jit(solution)/shard_map/ppermute | solution.py:553
  98.4 297.8 %reduce-scatter.4.cloned.1.call-start = ((), (), s32[]{:S(2)}) async-start(), calls=%async_computation.6 | async-start | bytes 6488064 | tf_op jit(solution)/shard_map/reduce_scatter | solution.py:535
  100.2 52.3 %copy-start.21 = (f32[4,64,160]{2,1,0:T(8,128)}, f32[4,64,160]{2,1,0:T(8,128)S(1)}, u32[]{:S(2)}) copy-start(f32[4,64,160]{2,1,0:T(8,128)S(1)} %fusion.38) | copy-start | bytes 491524
  101.2 22.6 %copy-start.24 = (f32[4,160,64]{2,1,0:T(8,128)}, f32[4,160,64]{2,1,0:T(8,128)S(1)}, u32[]{:S(2)}) copy-start(f32[4,160,64]{2,1,0:T(8,128)S(1)} %bitcast_multiply_fusion) | copy-start | bytes 491524
  111.8 43.3 %collective-permute-start.2 = (bf16[1,2,4,64,512]{4,3,2,1,0:T(8,128)(2,1)S(1)}, bf16[1,2,4,64,512]{4,3,2,1,0:T(8,128)(2,1)S(1)}, u32[]{:S(2)}, u32[]{:S(2)}) collective-permute-start(bf16[1,2,4,64,512]{4,3,2,1,0:T(8,128)(2,1)S(1)} %get-tuple-element.127), channel_id=1, source_target_pairs={{0,6},{1,7},{2,4},{3,5},{4,2},{5,3},{6,0},{7,1},{8,14},{9,15},{10,... | collective-permute-start | bytes 1572872 | tf_op jit(solution)/shard_map/ppermute | solution.py:553
  114.3 42.2 %collective-permute-start.1 = (bf16[1,2,4,64,512]{4,3,2,1,0:T(8,128)(2,1)S(1)}, bf16[1,2,4,64,512]{4,3,2,1,0:T(8,128)(2,1)S(1)}, u32[]{:S(2)}, u32[]{:S(2)}) collective-permute-start(bf16[1,2,4,64,512]{4,3,2,1,0:T(8,128)(2,1)S(1)} %get-tuple-element.128), channel_id=1, source_target_pairs={{0,4},{1,5},{2,6},{3,7},{4,0},{5,1},{6,2},{7,3},{8,12},{9,13},{10,... | collective-permute-start | bytes 1572872 | tf_op jit(solution)/shard_map/ppermute | solution.py:553
  114.8 41.7 %collective-permute-start = (bf16[1,2,4,64,512]{4,3,2,1,0:T(8,128)(2,1)S(1)}, bf16[1,2,4,64,512]{4,3,2,1,0:T(8,128)(2,1)S(1)}, u32[]{:S(2)}, u32[]{:S(2)}) collective-permute-start(bf16[1,2,4,64,512]{4,3,2,1,0:T(8,128)(2,1)S(1)} %get-tuple-element.129), channel_id=1, source_target_pairs={{0,2},{1,3},{2,0},{3,1},{4,6},{5,7},{6,4},{7,5},{8,10},{9,11},{10,... | collective-permute-start | bytes 1572872 | tf_op jit(solution)/shard_map/ppermute | solution.py:553
  123.1 25.9 %copy-start.32 = (bf16[640,512]{1,0:T(8,128)(2,1)}, bf16[640,512]{1,0:T(8,128)(2,1)S(1)}, u32[]{:S(2)}) copy-start(bf16[640,512]{1,0:T(8,128)(2,1)S(1)} %get-tuple-element.132) | copy-start | bytes 1966084
  123.1 25.9 %copy-start.39 = (bf16[640,512]{1,0:T(8,128)(2,1)}, bf16[640,512]{1,0:T(8,128)(2,1)S(1)}, u32[]{:S(2)}) copy-start(bf16[640,512]{1,0:T(8,128)(2,1)S(1)} %get-tuple-element.131) | copy-start | bytes 1966084
  123.1 28.7 %copy-start.41 = (bf16[640,512]{1,0:T(8,128)(2,1)}, bf16[640,512]{1,0:T(8,128)(2,1)S(1)}, u32[]{:S(2)}) copy-start(bf16[640,512]{1,0:T(8,128)(2,1)S(1)} %get-tuple-element.130) | copy-start | bytes 1966084
  124.5 24.9 %copy-start.25 = (f32[4,160,64]{2,1,0:T(8,128)S(1)}, f32[4,160,64]{2,1,0:T(8,128)}, u32[]{:S(2)}) copy-start(f32[4,160,64]{2,1,0:T(8,128)} %copy-done.24) | copy-start | bytes 491524
  155.1 63.1 %collective-permute-start.3 = (bf16[160,2048]{1,0:T(8,128)(2,1)S(1)}, bf16[160,2048]{1,0:T(8,128)(2,1)S(1)}, u32[]{:S(2)}, u32[]{:S(2)}) collective-permute-start(bf16[160,2048]{1,0:T(8,128)(2,1)S(1)} %get-tuple-element.69.refs_2_), channel_id=1, source_target_pairs={{0,2},{1,3},{2,0},{3,1},{4,6},{5,7},{6,4},{7,5},{8,10},{9,11},{10,... | collective-permute-start | bytes 1966088 | tf_op jit(solution)/shard_map/ppermute | solution.py:553
  291.2 192.5 %reduce-scatter.6.cloned.1.call-start = ((), (), s32[]{:S(2)}) async-start(), calls=%async_computation.7 | async-start | bytes 12976128 | tf_op jit(solution)/shard_map/reduce_scatter | solution.py:535
  316.9 258.2 %reduce-scatter.8.cloned.1.call-start = ((), (), s32[]{:S(2)}) async-start(), calls=%async_computation.8 | async-start | bytes 9437184 | tf_op jit(solution)/shard_map/reduce_scatter | solution.py:535
  333.3 49.5 %copy-start.48 = (bf16[640,1408]{1,0:T(8,128)(2,1)S(1)}, bf16[640,1408]{1,0:T(8,128)(2,1)}, u32[]{:S(2)}) copy-start(bf16[640,1408]{1,0:T(8,128)(2,1)} %copy-done.47) | copy-start | bytes 5406724
  382.8 8.6 %copy-start.3 = (bf16[640,2048]{1,0:T(8,128)(2,1)}, bf16[640,2048]{1,0:T(8,128)(2,1)S(1)}, u32[]{:S(2)}) copy-start(bf16[640,2048]{1,0:T(8,128)(2,1)S(1)} %get-tuple-element.83) | copy-start | bytes 7864324
  382.8 8.6 %copy-start.8 = (f32[160,2048]{1,0:T(8,128)}, f32[160,2048]{1,0:T(8,128)S(1)}, u32[]{:S(2)}) copy-start(f32[160,2048]{1,0:T(8,128)S(1)} %get-tuple-element.88.refs_2_) | copy-start | bytes 3932164
  392.7 18.9 %collective-permute-start.8 = (bf16[160,2048]{1,0:T(8,128)(2,1)}, bf16[160,2048]{1,0:T(8,128)(2,1)}, u32[]{:S(2)}, u32[]{:S(2)}) collective-permute-start(bf16[160,2048]{1,0:T(8,128)(2,1)} %get-tuple-element.110), channel_id=1, source_target_pairs={{0,6},{1,7},{2,4},{3,5},{4,2},{5,3},{6,0},{7,1},{8,14},{9,15},{10,... | collective-permute-start | bytes 1966088 | tf_op jit(solution)/shard_map/ppermute | solution.py:553
  394.2 29.4 %collective-permute-start.7 = (bf16[160,2048]{1,0:T(8,128)(2,1)}, bf16[160,2048]{1,0:T(8,128)(2,1)}, u32[]{:S(2)}, u32[]{:S(2)}) collective-permute-start(bf16[160,2048]{1,0:T(8,128)(2,1)} %get-tuple-element.111), channel_id=1, source_target_pairs={{0,4},{1,5},{2,6},{3,7},{4,0},{5,1},{6,2},{7,3},{8,12},{9,13},{10,... | collective-permute-start | bytes 1966088 | tf_op jit(solution)/shard_map/ppermute | solution.py:553
  395.7 28.0 %collective-permute-start.6 = (bf16[160,2048]{1,0:T(8,128)(2,1)}, bf16[160,2048]{1,0:T(8,128)(2,1)}, u32[]{:S(2)}, u32[]{:S(2)}) collective-permute-start(bf16[160,2048]{1,0:T(8,128)(2,1)} %get-tuple-element.112), channel_id=1, source_target_pairs={{0,2},{1,3},{2,0},{3,1},{4,6},{5,7},{6,4},{7,5},{8,10},{9,11},{10,... | collective-permute-start | bytes 1966088 | tf_op jit(solution)/shard_map/ppermute | solution.py:553
  403.3 20.4 %copy-start.4 = (bf16[640,2048]{1,0:T(8,128)(2,1)S(1)}, bf16[640,2048]{1,0:T(8,128)(2,1)}, u32[]{:S(2)}) copy-start(bf16[640,2048]{1,0:T(8,128)(2,1)} %copy-done.3) | copy-start | bytes 7864324
  403.3 20.4 %copy-start.44 = (bf16[4,160,512]{2,1,0:T(8,128)(2,1)S(1)}, bf16[4,160,512]{2,1,0:T(8,128)(2,1)}, u32[]{:S(2)}) copy-start(bf16[4,160,512]{2,1,0:T(8,128)(2,1)} %copy-done.43) | copy-start | bytes 1966084
  434.0 25.7 %copy-start.27 = (f32[4,160,64]{2,1,0:T(8,128)S(1)}, f32[4,160,64]{2,1,0:T(8,128)}, u32[]{:S(2)}) copy-start(f32[4,160,64]{2,1,0:T(8,128)} %copy-done.24) | copy-start | bytes 491524
  434.0 25.7 %copy-start.46 = (f32[4,160,64]{1,2,0:T(8,128)S(1)}, f32[4,160,64]{1,2,0:T(8,128)}, u32[]{:S(2)}) copy-start(f32[4,160,64]{1,2,0:T(8,128)} %copy-done.45) | copy-start | bytes 491524
  434.1 26.5 %copy-start.50 = (bf16[4,160,160]{2,1,0:T(8,128)(2,1)S(1)}, bf16[4,160,160]{2,1,0:T(8,128)(2,1)}, u32[]{:S(2)}) copy-start(bf16[4,160,160]{2,1,0:T(8,128)(2,1)} %copy-done.49) | copy-start | bytes 614404
  434.2 39.0 %collective-permute-start.9 = (bf16[1,2,64,4,512]{4,2,3,1,0:T(8,128)(2,1)S(1)}, bf16[1,2,64,4,512]{4,2,3,1,0:T(8,128)(2,1)S(1)}, u32[]{:S(2)}, u32[]{:S(2)}) collective-permute-start(bf16[1,2,64,4,512]{4,2,3,1,0:T(8,128)(2,1)S(1)} %bitcast.181), channel_id=1, source_target_pairs={{0,2},{1,3},{2,0},{3,1},{4,6},{5,7},{6,4},{7,5},{8,10},{9,11},{10,... | collective-permute-start | bytes 1572872 | tf_op jit(solution)/shard_map/ppermute | solution.py:553
  435.7 37.5 %collective-permute-start.10 = (bf16[1,2,64,4,512]{4,2,3,1,0:T(8,128)(2,1)S(1)}, bf16[1,2,64,4,512]{4,2,3,1,0:T(8,128)(2,1)S(1)}, u32[]{:S(2)}, u32[]{:S(2)}) collective-permute-start(bf16[1,2,64,4,512]{4,2,3,1,0:T(8,128)(2,1)S(1)} %bitcast.180), channel_id=1, source_target_pairs={{0,4},{1,5},{2,6},{3,7},{4,0},{5,1},{6,2},{7,3},{8,12},{9,13},{10,... | collective-permute-start | bytes 1572872 | tf_op jit(solution)/shard_map/ppermute | solution.py:553
  436.3 36.9 %collective-permute-start.11 = (bf16[1,2,64,4,512]{4,2,3,1,0:T(8,128)(2,1)S(1)}, bf16[1,2,64,4,512]{4,2,3,1,0:T(8,128)(2,1)S(1)}, u32[]{:S(2)}, u32[]{:S(2)}) collective-permute-start(bf16[1,2,64,4,512]{4,2,3,1,0:T(8,128)(2,1)S(1)} %bitcast.179), channel_id=1, source_target_pairs={{0,6},{1,7},{2,4},{3,5},{4,2},{5,3},{6,0},{7,1},{8,14},{9,15},{10,... | collective-permute-start | bytes 1572872 | tf_op jit(solution)/shard_map/ppermute | solution.py:553
  438.2 22.8 %copy-start.34 = (bf16[640,512]{1,0:T(8,128)(2,1)S(1)}, bf16[640,512]{1,0:T(8,128)(2,1)}, u32[]{:S(2)}) copy-start(bf16[640,512]{1,0:T(8,128)(2,1)} %copy-done.32) | copy-start | bytes 1966084
  464.3 8.9 %copy-start.54 = (bf16[4,160,512]{2,1,0:T(8,128)(2,1)}, bf16[4,160,512]{2,1,0:T(8,128)(2,1)S(1)}, u32[]{:S(2)}) copy-start(bf16[4,160,512]{2,1,0:T(8,128)(2,1)S(1)} %fusion.13) | copy-start | bytes 1966084
  465.5 7.6 %copy-start.55 = (bf16[4,160,512]{2,1,0:T(8,128)(2,1)}, bf16[4,160,512]{2,1,0:T(8,128)(2,1)S(1)}, u32[]{:S(2)}) copy-start(bf16[4,160,512]{2,1,0:T(8,128)(2,1)S(1)} %fusion.12) | copy-start | bytes 1966084
  483.6 13.4 %copy-start.53 = (bf16[4,160,512]{2,1,0:T(8,128)(2,1)S(1)}, bf16[4,160,512]{2,1,0:T(8,128)(2,1)}, u32[]{:S(2)}) copy-start(bf16[4,160,512]{2,1,0:T(8,128)(2,1)} %copy-done.52) | copy-start | bytes 1966084
  497.0 7.6 %copy-start.9 = (f32[160,2048]{1,0:T(8,128)S(1)}, f32[160,2048]{1,0:T(8,128)}, u32[]{:S(2)}) copy-start(f32[160,2048]{1,0:T(8,128)} %copy-done.8) | copy-start | bytes 3932164
  497.0 7.6 %copy-start.17 = (f32[1,2048]{1,0:T(1,128)S(1)}, f32[1,2048]{1,0:T(1,128)}, u32[]{:S(2)}) copy-start(f32[1,2048]{1,0:T(1,128)} %copy-done.16) | copy-start | bytes 24580
  575.1 14.1 %slice-start.1 = ((bf16[256,2048]{1,0:T(8,128)(2,1)}), bf16[256,512]{1,0:T(8,128)(2,1)S(1)}, s32[]{:S(2)}) async-start(bf16[256,2048]{1,0:T(8,128)(2,1)} %reduce-scatter.8.cloned.1.call-done), calls=%async_computation.10 | async-start | bytes 524288 | tf_op jit(solution)/shard_map/slice | solution.py:747
  (36 other events, 85.4 us)
Sparse Core Ops, SparseCore 0:
  28.6 81.4 all-gather.3
  111.7 110.5 all-gather.5
  223.9 67.1 all-gather.7
  293.3 63.5 reduce-scatter.3
  359.0 123.0 reduce-scatter.5
  484.2 90.7 reduce-scatter.7

commit v3 on v2

--- a/solution.py
+++ b/solution.py
@@ -17,7 +17,11 @@
 ANY = pl.BlockSpec(memory_space=pl.ANY)
 
 
-def exchange(cid, arrays, outs, moves, plan):
+def lasting(us):
+    return pl.CostEstimate(flops=0, bytes_accessed=us * 3_400_000, transcendentals=0)
+
+
+def exchange(cid, us, arrays, outs, moves, plan):
     def kernel(*refs):
         ins = refs[: len(arrays)]
         dsts = refs[len(arrays) : len(arrays) + len(outs)]
@@ -56,6 +60,7 @@
             pltpu.SemaphoreType.DMA((moves,)),
         ],
         compiler_params=pltpu.CompilerParams(collective_id=cid, has_side_effects=True),
+        cost_estimate=lasting(us),
     )(*arrays)
 
 
@@ -74,15 +79,6 @@
 
 def columns_at(ref, block, size):
     return ref.at[:, pl.ds(pl.multiple_of(block * size, 128), size)]
-
-
-def swap_all(cid, x, count):
-    def plan(me, ins, outs):
-        peers = [lax.rem(me + k, count) for k in range(1, count)]
-        moves = [(ins[0].at[p], outs[0].at[me], p) for p in peers]
-        return peers, moves + [(ins[0].at[me], outs[0].at[me], None)]
-
-    return exchange(cid, [x], [(x.shape, x.dtype)], count, plan)[0]
 
 
 def first_exchange(cid, weights, output_rows):
@@ -104,7 +100,7 @@
         return [p for p, _ in targets[:3]], moves
 
     shape = (HEADS * rows, 4 * part)
-    return exchange(cid, [*weights, output_rows], [(shape, bf16)], 16, plan)[0]
+    return exchange(cid, 18, [*weights, output_rows], [(shape, bf16)], 16, plan)[0]
 
 
 def second_exchange(cid, gains, codes, gate, up, down, count):
@@ -128,6 +124,7 @@
 
     return exchange(
         cid,
+        36,
         [gains, codes, gate, up, down],
         [
             ((count, *gains.shape), gains.dtype),
@@ -140,38 +137,95 @@
     )
 
 
-def return_columns(cid, x, pieces):
+def return_columns(cid, x, pieces, part, planes, gains):
     rows = x.shape[0] // HEADS
-    part = x.shape[1] // pieces
-
-    def plan(me, ins, outs):
+    last = planes > 0
+    count = planes * PLANE
+
+    def kernel(*refs):
+        src, refs = refs[0], refs[1:]
+        shares, refs = (refs[0], refs[1:]) if last else (None, refs)
+        outs, rest = refs[:pieces], refs[pieces:]
+        extra, gain_out, rest = (rest[0], rest[1], rest[2:]) if last else (None, None, rest)
+        landed, send, recv, gain_in, gain_send, gain_recv = rest
+        me = lax.axis_index("seq")
         h = chip_of(me)
-        targets = [chip_on(me, h, k) for k in (1, 2, 3)] + [(None, h)]
-        moves = []
-        for device, other in targets:
+        targets = [chip_on(me, h, k) for k in (3, 1, 2)]
+        everyone = [lax.rem(me + k, count) for k in range(1, count)]
+        peers = everyone if last else [device for device, _ in targets]
+        barrier = pltpu.get_barrier_semaphore()
+        for device in peers:
+            pl.semaphore_signal(barrier, inc=1, device_id=(device,), device_id_type=MESH)
+        pl.semaphore_wait(barrier, len(peers))
+
+        def to(device, source, dst, sends, recvs, n):
+            return pltpu.make_async_remote_copy(
+                src_ref=source, dst_ref=dst, send_sem=sends.at[n], recv_sem=recvs.at[n],
+                device_id=(device,), device_id_type=MESH,
+            )
+
+        copies = []
+        for k, (device, other) in enumerate(targets):
             for j in range(pieces):
-                src = ins[0].at[
+                source = src.at[
                     pl.ds(pl.multiple_of(other * rows, rows), rows), pl.ds(j * part, part)
                 ]
-                moves.append((src, columns_at(outs[j], h, part), device))
-        return [p for p, _ in targets[:3]], moves
-
-    return exchange(
-        cid, [x], [((rows, HEADS * part), x.dtype)] * pieces, 4 * pieces, plan
-    )
+                copies.append(to(device, source, landed.at[j, h], send, recv, k * pieces + j))
+        if last:
+            for n, device in enumerate(everyone):
+                copies.append(to(device, shares.at[device], gain_in.at[me], gain_send, gain_recv, n))
+        for copy in copies:
+            copy.start()
+        own = pl.ds(pl.multiple_of(h * rows, rows), rows)
+        for j in range(pieces):
+            landed[j, h] = src[own, pl.ds(j * part, part)]
+        if last:
+            gain_in[me] = shares[me]
+            blocks = [src[pl.ds(k * rows, rows), pl.ds(pieces * part, part)] for k in range(HEADS)]
+            extra[...] = reorder(jnp.concatenate(blocks, axis=1).astype(f32), planes, True)
+        for copy in copies:
+            copy.wait()
+        for j in range(pieces):
+            for k in range(HEADS):
+                outs[j][:, pl.ds(k * part, part)] = landed[j, k].astype(f32)
+        if last:
+            total = gain_in[0]
+            for k in range(1, count):
+                total = total + gain_in[k]
+            gain_out[...] = total
+
+    vmem = pl.BlockSpec(memory_space=pltpu.VMEM)
+    shapes = [(rows, HEADS * part)] * (pieces + int(last)) + [(8, 128)] * int(last)
+    return pl.pallas_call(
+        kernel,
+        out_shape=[jax.ShapeDtypeStruct(shape, f32) for shape in shapes],
+        in_specs=[vmem] * (1 + int(last)),
+        out_specs=[vmem] * len(shapes),
+        scratch_shapes=[
+            pltpu.VMEM((pieces, HEADS, rows, part), x.dtype),
+            pltpu.SemaphoreType.DMA((3 * pieces,)),
+            pltpu.SemaphoreType.DMA((3 * pieces,)),
+            pltpu.VMEM((max(count, 1), 8, 128), f32),
+            pltpu.SemaphoreType.DMA((max(count, 2),)),
+            pltpu.SemaphoreType.DMA((max(count, 2),)),
+        ],
+        compiler_params=pltpu.CompilerParams(
+            collective_id=cid, has_side_effects=True, vmem_limit_bytes=40 << 20
+        ),
+        cost_estimate=lasting(14),
+    )(*([x, gains] if last else [x]))
 
 
 STEP = 16
 
 
 def reorder(x, planes, back):
-    strip = x.shape[1] // (planes * PLANE)
+    chips = planes * HEADS
+    strip = x.shape[1] // (2 * chips)
     pieces = []
-    for p in range(planes):
-        for i in range(PLANE):
-            n = (i % 2) * HEADS + i // 2 if back else (i % HEADS) * 2 + i // HEADS
-            at = (p * PLANE + n) * strip
-            pieces.append(x[:, at : at + strip])
+    for i in range(2 * chips):
+        n = (i % 2) * chips + i // 2 if back else (i % chips) * 2 + i // chips
+        pieces.append(x[:, n * strip : (n + 1) * strip])
     return jnp.concatenate(pieces, axis=1)
 
 
@@ -196,7 +250,7 @@
     )(*arrays)
 
 
-def plane_stage(cid, partial, blocks, body, own, gathered):
+def plane_stage(cid, partial, blocks, body, own, gathered, product=None):
     rows, width = blocks[0].shape
     half = rows // 2
     has = int(partial is not None)
@@ -206,8 +260,11 @@
         part = refs[0] if has else None
         block_refs = refs[has : has + len(blocks)]
         rest = refs[has + len(blocks) :]
+        factors, rest = (rest[:2], rest[2:]) if product else (None, rest)
         own_refs, rest = rest[: len(own)], rest[len(own) :]
         everything, rest = (rest[0], rest[1:]) if gathered else (None, rest)
+        results, rest = (rest[:HEADS], rest[HEADS:]) if product else (None, rest)
+        (left, right, load), rest = (rest[:3], rest[3:]) if product else ((None,) * 3, rest)
         by_x, by_y, over_x, over_y, sum_x, sum_y, mine, send, recv, out_send, out_recv = rest
         me = lax.axis_index("seq")
         h = chip_of(me)
@@ -225,6 +282,20 @@
 
         def block(k, first):
             return pl.ds(k * rows + (0 if first else half), half)
+
+        loads = []
+        if product:
+            loads = [
+                pltpu.make_async_copy(src, dst, load.at[n])
+                for n, (src, dst) in enumerate(zip(factors, (left, right)))
+            ]
+
+        def multiply(k):
+            if product:
+                results[k][...] = lax.dot_general(
+                    left[pl.ds(k * rows, rows), :], right[...], (((1,), (1,)), ((), ())),
+                    preferred_element_type=f32,
+                ).astype(bf16)
 
         if has:
             copies = [
@@ -237,12 +308,18 @@
             ]
             for copy in copies[:4]:
                 copy.start()
+            for copy in loads:
+                copy.start()
+            for copy in loads:
+                copy.wait()
+            multiply(0)
             copies[0].wait_recv()
             sum_y[...] = (part[block(2, True), :].astype(f32) + over_x[...].astype(f32)).astype(bf16)
             copies[4].start()
             copies[1].wait_recv()
             sum_x[...] = (part[block(1, False), :].astype(f32) + over_y[...].astype(f32)).astype(bf16)
             copies[5].start()
+            multiply(1)
             for copy in copies[:2]:
                 copy.wait_send()
             for copy in copies[2:]:
@@ -271,10 +348,12 @@
             for copy in copies[:4]:
                 copy.start()
             keep.start()
+            multiply(2)
             copies[0].wait_recv()
             copies[4].start()
             copies[1].wait_recv()
             copies[5].start()
+            multiply(3)
             for copy in copies[:2]:
                 copy.wait_send()
             for copy in copies[2:]:
@@ -285,19 +364,72 @@
     shapes = [jax.ShapeDtypeStruct(s, d) for s, d in own]
     if gathered:
         shapes.append(jax.ShapeDtypeStruct((HEADS * rows, width), bf16))
+    factors_in, loaded = [], []
+    if product:
+        shapes += [jax.ShapeDtypeStruct((rows, width), bf16)] * HEADS
+        factors_in = list(product)
+        loaded = [pltpu.VMEM(x.shape, x.dtype) for x in product] + [pltpu.SemaphoreType.DMA((2,))]
     whole, part_of = ((rows, width), (half, width)) if has else ((STEP, 128), (STEP, 128))
     return pl.pallas_call(
         kernel,
         out_shape=shapes,
-        in_specs=[vmem] * (has + len(blocks)),
-        out_specs=[vmem] * len(own) + [ANY] * int(gathered),
-        scratch_shapes=[pltpu.VMEM(s, bf16) for s in (whole, whole, part_of, part_of, part_of, part_of)]
+        in_specs=[vmem] * (has + len(blocks)) + [ANY] * len(factors_in),
+        out_specs=[vmem] * len(own) + [ANY] * int(gathered) + [vmem] * (HEADS if product else 0),
+        scratch_shapes=loaded + [pltpu.VMEM(s, bf16) for s in (whole, whole, part_of, part_of, part_of, part_of)]
         + [pltpu.VMEM((rows, width), bf16)]
         + [pltpu.SemaphoreType.DMA((n,)) for n in (6, 6, 7, 6)],
         compiler_params=pltpu.CompilerParams(
             collective_id=cid, has_side_effects=True, vmem_limit_bytes=40 << 20
         ),
-    )(*([partial] if has else []), *blocks)
+        cost_estimate=lasting(25 * has + 25 * int(gathered)),
+    )(*([partial] if has else []), *blocks, *factors_in)
+
+
+def chip_sum(core, left, right, other_left, other_right, extra=None):
+    tokens, columns = right.shape
+    half = left.shape[1] // 2
+    block = min(half, 256)
+    steps = half // block
+    more = 0 if extra is None else extra.shape[1]
+    contract = (((0,), (0,)), ((), ()))
+    pieces = 2 if columns % 256 == 0 and columns > 2048 else 1
+    size = columns // pieces
+
+    def kernel(which, a, b, c, d, *rest):
+        out = rest[-1]
+        for n in range(pieces):
+            at = pl.ds(n * size, size)
+            total = lax.dot_general(a[...], b[:, at], contract, preferred_element_type=f32)
+            total += lax.dot_general(c[...], d[:, at], contract, preferred_element_type=f32)
+            out[:, at] = total.astype(bf16)
+        if more:
+            out[:, pl.ds(columns, more)] = rest[0][...]
+
+    whole = pl.BlockSpec((tokens, columns), lambda i, w: (0, 0), pipeline_mode=pl.Buffered(1))
+    specs = [
+        pl.BlockSpec((tokens, block), lambda i, w: (0, w[0] * steps + i)),
+        whole,
+        pl.BlockSpec((tokens, block), lambda i, w: (0, i)),
+        whole,
+    ]
+    if more:
+        specs.append(pl.BlockSpec((block, more), lambda i, w: (i, 0)))
+    return pl.pallas_call(
+        kernel,
+        out_shape=jax.ShapeDtypeStruct((half, columns + more), bf16),
+        grid_spec=pltpu.PrefetchScalarGridSpec(
+            num_scalar_prefetch=1,
+            grid=(steps,),
+            in_specs=specs,
+            out_specs=pl.BlockSpec((block, columns + more), lambda i, w: (i, 0)),
+        ),
+        compiler_params=pltpu.CompilerParams(vmem_limit_bytes=40 << 20),
+        cost_estimate=pl.CostEstimate(
+            flops=4 * tokens * half * columns,
+            bytes_accessed=4 * tokens * (half + columns) + 2 * half * columns,
+            transcendentals=0,
+        ),
+    )(core.reshape(1), left, right, other_left, other_right, *(() if extra is None else (extra,)))
 
 
 def factor_of(x):
@@ -363,13 +495,23 @@
     return body
 
 
-def carry_states(cid, keys, values, gains, planes, reverse):
+def carry_states(cid, keys, values, gains, planes, reverse, rows_out=None):
+    more = int(rows_out is not None)
     sent = bf16 if reverse else f32
     _, slots, size = keys.shape
     half = slots // 2
-
-    def kernel(k_in, v_in, g_in, k_out, v_out, k_all, v_all, g_all, k_pre, v_pre, g_pre, k_run, v_run, g_run,
-               k_far, v_far, g_far, k_base, v_base, k_mine, v_mine, s_send, s_recv, z_send, z_recv, b_send, b_recv):
+    quarter, _, strip, _ = rows_out.shape if more else (1, 0, 0, 0)
+
+    def kernel(k_in, v_in, g_in, *refs):
+        r_in, refs = (refs[0], refs[1:]) if more else (None, refs)
+        k_out, v_out, refs = refs[0], refs[1], refs[2:]
+        r_out, refs = (refs[0], refs[1:]) if more else (None, refs)
+        r_all, r_send, r_recv, refs = (*refs[:3], refs[3:]) if more else (None, None, None, refs)
+        main(k_in, v_in, g_in, k_out, v_out, *refs, r_in=r_in, r_out=r_out, r_all=r_all, r_send=r_send, r_recv=r_recv)
+
+    def main(k_in, v_in, g_in, k_out, v_out, k_all, v_all, g_all, k_pre, v_pre, g_pre, k_run, v_run, g_run,
+               k_far, v_far, g_far, k_base, v_base, k_mine, v_mine, s_send, s_recv, z_send, z_recv, b_send, b_recv,
+             *, r_in, r_out, r_all, r_send, r_recv):
         me = lax.axis_index("seq")
         h = chip_of(me)
         core = lax.rem(me, 2)
@@ -377,9 +519,11 @@
         sibling = me + 1 - 2 * core
         barrier = pltpu.get_barrier_semaphore()
         others = [me + PLANE * (lax.rem(z + k, planes) - z) for k in range(1, planes)]
-        for device in (sibling, *others):
+        chips = [chip_on(me, h, k) for k in (1, 2, 3)]
+        greeted = [sibling, *others] + ([device for device, _ in chips] if more else [])
+        for device in greeted:
             pl.semaphore_signal(barrier, inc=1, device_id=(device,), device_id_type=MESH)
-        pl.semaphore_wait(barrier, planes)
+        pl.semaphore_wait(barrier, len(greeted))
 
         def remote(src, dst, s, r, device):
             return pltpu.make_async_remote_copy(
@@ -396,6 +540,18 @@
                 copies.append(remote(src.at[k], dst.at[chip, core], s_send.at[n], s_recv.at[n], sibling))
         for copy in copies:
             copy.start()
+        swaps = []
+        if more:
+            for n, (device, chip) in enumerate(chips):
+                for q in range(quarter):
+                    at = quarter * n + q
+                    swaps.append(
+                        remote(r_in.at[q, chip], r_all.at[h, q], r_send.at[at], r_recv.at[at], device)
+                    )
+            for swap in swaps:
+                swap.start()
+            for q in range(quarter):
+                r_all[h, q] = r_in[q, h]
         for k in range(HEADS):
             chip = chip_on(me, h, k)[1]
             for src, dst in ((g_in, g_all), (k_in, k_all), (v_in, v_all)):
@@ -464,6 +620,14 @@
             gain = g_pre[chip, core][:, :1]
             k_out[k] = gain * k_base[...] + k_pre[chip, core]
             v_out[k] = gain * v_base[...] + v_pre[chip, core]
+        for swap in swaps:
+            swap.wait()
+        if more:
+            for c in range(HEADS):
+                for q in range(quarter):
+                    for b in range(HEADS):
+                        at = ((c * quarter + q) * HEADS + b) * strip
+                        r_out[pl.ds(at, strip), :] = r_all[c, q, :, pl.ds(b * size, size)]
         for k in range(1, planes):
             @pl.when(ahead(k))
             def _(k=k):
@@ -475,18 +639,24 @@
     state = [pltpu.VMEM((slots, n), f32) for n in (size, size, 128)]
     far = [pltpu.VMEM((planes - 1, half, n), d) for n, d in ((size, sent), (size, sent), (128, f32))]
     sends = [pltpu.VMEM((half, size), sent)] * 2
+    side = []
+    if more:
+        side = [pltpu.VMEM((HEADS, quarter, strip, HEADS * size), bf16)]
+        side += [pltpu.SemaphoreType.DMA((3 * quarter,))] * 2
     semaphores = [12, 12, 3 * planes - 3, 3 * planes - 3, 2, 2]
     return pl.pallas_call(
         kernel,
-        out_shape=[jax.ShapeDtypeStruct(keys.shape, f32)] * 2,
-        in_specs=[vmem] * 3,
-        out_specs=[vmem] * 2,
-        scratch_shapes=wide + wide + state + far + state[:2] + sends
+        out_shape=[jax.ShapeDtypeStruct(keys.shape, f32)] * 2
+        + [jax.ShapeDtypeStruct((HEADS * quarter * HEADS * strip, size), bf16)] * more,
+        in_specs=[vmem] * (3 + more),
+        out_specs=[vmem] * (2 + more),
+        scratch_shapes=side + wide + wide + state + far + state[:2] + sends
         + [pltpu.SemaphoreType.DMA((n,)) for n in semaphores],
         compiler_params=pltpu.CompilerParams(
             collective_id=cid, has_side_effects=True, vmem_limit_bytes=32 << 20
         ),
-    )(keys, values, gains)
+        cost_estimate=lasting(22),
+    )(keys, values, gains, *([rows_out] if more else []))
 
 
 def rms_factor(value_rows):
@@ -525,23 +695,33 @@
     strip = query_weight.shape[0]
     head_size = width // HEADS
     lines = [
-        [p * PLANE + c * 2 + k for p in range(planes) for k in range(2)] for c in range(HEADS)
+        [p * PLANE + c * 2 + k for k in range(2) for p in range(planes)] for c in range(HEADS)
     ]
 
     def gather_line(x):
         return lax.all_gather(x, "seq", axis=0, tiled=True, axis_index_groups=lines)
 
-    def scatter_line(x):
+    columns = [[p * PLANE + k for p in range(planes)] for k in range(PLANE)]
+
+    def scatter_column(x):
         return lax.psum_scatter(
-            x, "seq", scatter_dimension=0, tiled=True, axis_index_groups=lines
+            x, "seq", scatter_dimension=0, tiled=True, axis_index_groups=columns
         )
 
+    def to_sibling(x):
+        return lax.ppermute(x, "seq", [(d, d ^ 1) for d in range(count)])
+
+    def cut(x, side):
+        part_width = x.shape[1] // 2
+        return lax.dynamic_slice_in_dim(x, (core ^ side) * part_width, part_width, axis=1)
+
+
     def shuffled(x):
-        y = x.reshape(*x.shape[:-1], planes, HEADS, 2, strip)
+        y = x.reshape(*x.shape[:-1], planes * HEADS, 2, strip)
         return jnp.swapaxes(y, -3, -2).reshape(x.shape)
 
     def restored(x):
-        y = x.reshape(*x.shape[:-1], planes, 2, HEADS, strip)
+        y = x.reshape(*x.shape[:-1], 2, planes * HEADS, strip)
         return jnp.swapaxes(y, -3, -2).reshape(x.shape)
 
     turns = [
@@ -576,6 +756,7 @@
     tokens_own, cotangent_own = reordered([tokens, cotangent], planes)
     (h1,) = plane_stage(2, None, [tokens_own, gain_one], norm_body, [], True)
     h1, cotangent_sent = lax.optimization_barrier((h1, cotangent_own))
+    h1_other = to_sibling(cut(h1, 1))
     cotangent_parts = [cotangent_own] + [send_on(cotangent_sent, k) for k in (1, 2, 3)]
 
     decay = jax.nn.log_sigmoid(codes_all.astype(f32) / 256.0)
@@ -638,13 +819,13 @@
     normed_heads = (unit_heads * head_gain_f).astype(bf16).reshape(HEADS * rows, head_size)
 
     quarter = planes // HEADS
-    output_line = mixer_line[:, 3 * head_size :].reshape(planes, 2, HEADS, strip, head_size)
+    output_line = mixer_line[:, 3 * head_size :].reshape(2, planes, HEADS, strip, head_size)
     pieces = [
-        lax.dynamic_slice_in_dim(output_line, (h ^ k) * quarter, quarter)
+        lax.dynamic_slice_in_dim(output_line, (h ^ k) * quarter, quarter, axis=1)
         for k in range(HEADS)
     ]
     pieces = in_chip_order([pieces[0]] + [send_on(pieces[k], k) for k in (1, 2, 3)])
-    out_weight = pieces.transpose(1, 0, 2, 4, 3, 5).reshape(head_size, width)
+    out_weight = pieces.transpose(2, 0, 1, 4, 3, 5).reshape(head_size, width)
     mixed = jnp.dot(normed_heads, out_weight, preferred_element_type=f32).astype(bf16)
     residual, h2 = plane_stage(
         4, mixed, [tokens_own, gain_two], residual_body, [((rows, width), f32)], True
@@ -657,31 +838,39 @@
     sigma = jax.nn.sigmoid(both[:, :part])
     hidden = (both[:, :part] * sigma * both[:, part:]).astype(bf16)
     hidden, both = lax.optimization_barrier((hidden, both))
-    down_part = plain("td,tf->df", cotangent_all, hidden).astype(bf16)
-    down_part, down_line = lax.optimization_barrier((down_part, down_line))
-    down_sums = scatter_line(down_part)
+    down_part = chip_sum(
+        core, cotangent_all, hidden, to_sibling(cut(cotangent_all, 1)), to_sibling(hidden)
+    )
+    down_sums = scatter_column(down_part)
+    h2_other = to_sibling(cut(h2, 1))
+    (heads_cut,) = reordered([normed_heads], quarter)
+    heads_other = to_sibling(cut(heads_cut, 1))
+    _, down_line, out_weight, h2_other, heads_other = lax.optimization_barrier(
+        (down_part, down_line, out_weight, h2_other, heads_other)
+    )
     gate, upward = both[:, :part], both[:, part:]
     sigma = jax.nn.sigmoid(gate)
     hidden_grad = jnp.dot(cotangent_all, down_line, preferred_element_type=f32)
     gate_back = (hidden_grad * upward * sigma * (1.0 + gate * (1.0 - sigma))).astype(bf16)
     up_back = (hidden_grad * (gate * sigma)).astype(bf16)
     both_back = jnp.concatenate([gate_back, up_back], axis=1)
-    feed_part = plain("td,tf->df", h2, both_back).astype(bf16)
-    feed_part, both_back = lax.optimization_barrier((feed_part, both_back))
-    feed_sums = scatter_line(feed_part)
+    both_other = to_sibling(both_back)
     feed_in = plain("tf,df->td", both_back, feed_weight).astype(bf16)
-    residual_grad, feed_gain_part, mixed_grad = plane_stage(
+    both_other, feed_in = lax.optimization_barrier((both_other, feed_in))
+    feed_part = chip_sum(core, h2, both_back, h2_other, both_other)
+    feed_part, feed_in = lax.optimization_barrier((feed_part, feed_in))
+    feed_sums = scatter_column(feed_part)
+    residual_grad, feed_gain_part, mixed_grad, *feed_out = plane_stage(
         5,
         feed_in,
         [residual, cotangent_own, gain_two],
         residual_grad_body,
         [((rows, width), f32), ((8, width), f32)],
         True,
-    )
-    mixed_grad, hidden = lax.optimization_barrier((mixed_grad, hidden))
-    feed_out = plain("tf,df->td", hidden, down_line).astype(bf16)
-    feed_outs = [feed_out[:rows]]
-    feed_outs += [send_on(feed_out[k * rows : (k + 1) * rows], k) for k in (1, 2, 3)]
+        (hidden, down_line),
+    )
+    mixed_other = to_sibling(mixed_grad)
+    feed_outs = [feed_out[0]] + [send_on(feed_out[k], k) for k in (1, 2, 3)]
 
     mixed_grad, down_sums = lax.optimization_barrier((mixed_grad, down_sums))
     heads_grad = plain("td,fd->tf", mixed_grad, out_weight).reshape(blocked)
@@ -703,8 +892,12 @@
     affinity_grad = (precise("btm,bsm->bts", inner_grad, back) * same).astype(bf16)
     first_key = precise("btm,btd->bmd", state_grad, query_f)
     first_value = precise("btm,btd->bmd", entry, out_back_f)
-    first_key, feed_outs = lax.optimization_barrier((first_key, feed_outs))
-    later_key, later_value = carry_states(6, first_key, first_value, carried, planes, True)
+    out_part = chip_sum(core, heads_cut, mixed_grad, heads_other, mixed_other)
+    out_part = out_part.reshape(quarter, HEADS, strip, width)
+    later_key, later_value, out_part = carry_states(
+        6, first_key, first_value, carried, planes, True, out_part
+    )
+    later_key, feed_outs = lax.optimization_barrier((later_key, feed_outs))
 
     query_back = plain("bts,bsd->btd", affinity_grad, key) + precise(
         "btm,bmd->btd", state_grad, key_state
@@ -720,17 +913,10 @@
         ],
         axis=1,
     )
-    out_part = plain("tf,td->fd", normed_heads, mixed_grad).astype(bf16)
-    out_part = out_part.reshape(quarter, HEADS, 2, strip, HEADS, head_size)
-    pieces = [
-        lax.dynamic_index_in_dim(out_part, h ^ k, 1, keepdims=False) for k in range(HEADS)
-    ]
-    pieces = in_chip_order([pieces[0]] + [send_on(pieces[k], k) for k in (1, 2, 3)])
-    out_part = pieces.transpose(0, 1, 2, 4, 3, 5).reshape(width, head_size)
-    mixer_part = plain("td,tf->df", h1, backs).astype(bf16)
-    mixer_part = jnp.concatenate([mixer_part, out_part], axis=1)
-    mixer_part, feed_sums = lax.optimization_barrier((mixer_part, feed_sums))
-    mixer_sums = scatter_line(mixer_part)
+    backs_other = to_sibling(backs)
+    mixer_part = chip_sum(core, h1, backs, h1_other, backs_other, out_part)
+    mixer_part, feed_sums, backs = lax.optimization_barrier((mixer_part, feed_sums, backs))
+    mixer_sums = scatter_column(mixer_part)
     mixer_in = plain("tf,df->td", backs, mixer_weight).astype(bf16)
     input_grad, mixer_gain_part, block_out = plane_stage(
         7,
@@ -741,12 +927,6 @@
         False,
     )
 
-    (down_grad,) = return_columns(8, down_sums, 1)
-    gate_grad, up_grad = return_columns(9, feed_sums, 2)
-    query_grad, key_grad, value_grad = return_columns(10, mixer_sums[:, : 3 * head_size], 3)
-    out_sums = mixer_sums[:, 3 * head_size :].reshape(HEADS, strip, head_size)
-    out_sums = out_sums.swapaxes(0, 1).reshape(strip, width)
-
     head_whole = lax.dynamic_update_slice(
         jnp.zeros((width,), f32), head_gain_part, (h * head_size,)
     )
@@ -759,20 +939,25 @@
     )
     gain_parts = gain_parts.reshape(3, count, strip).swapaxes(0, 1)
     gain_parts = jnp.pad(gain_parts, ((0, 0), (0, 5), (0, 128 - strip)))
-    gain_sums = jnp.sum(swap_all(11, gain_parts, count), axis=0)[:3, :strip]
+    (down_grad,) = return_columns(8, down_sums, 1, part, 0, None)
+    gate_grad, up_grad = return_columns(9, feed_sums, 2, part, 0, None)
+    query_grad, key_grad, value_grad, output_grad, gain_sums = return_columns(
+        10, mixer_sums, 3, head_size, planes, gain_parts
+    )
+    gain_sums = gain_sums[:3, :strip]
     return (
         block_out,
         input_grad,
         gain_sums[0],
-        query_grad.astype(f32),
-        key_grad.astype(f32),
-        value_grad.astype(f32),
+        query_grad,
+        key_grad,
+        value_grad,
         gain_sums[1],
-        restored(out_sums).astype(f32),
+        output_grad,
         gain_sums[2],
-        gate_grad.astype(f32),
-        up_grad.astype(f32),
-        down_grad.astype(f32),
+        gate_grad,
+        up_grad,
+        down_grad,
     )
 
 

time: 611 us -> 583 us (0.954)
  matrix products: 112 us -> 71.1 us
  Pallas kernels: 312 us -> 344 us
  waiting for transfers between devices: 72.4 us -> 54.9 us
  other arithmetic: 27.6 us -> 12.2 us
  local copies, waits for them, and re-layouts: 48.4 us -> 62.7 us
    pallas_call x0 -> x7, Pallas kernels: none -> 77.7 us  [the longest x3 47.1 us: return_columns(): pl.pallas_call(kernel, out_shape=[jax.ShapeDtypeStruct(shape, f32) for sh...]
    pallas_call x6 -> x2, Pallas kernels: 107 us -> 56 us  [exchange(): pl.pallas_call(kernel, out_shape=[jax.ShapeDtypeStruct(s, d) for s, d in...]
    dot_general x14 -> x9, matrix products: 66.4 us -> 25.7 us  [plain(): return jnp.einsum(form, left, right, preferred_element_type=f32)]
    unnamed x136 -> x163, local copies, waits for them, and re-layouts: 19.2 us -> 47.1 us
    ppermute x12 -> x9, waiting for transfers between devices: 18.1 us -> 0.02 us  [send_on(): return lax.ppermute(x, 'seq', turns[k])]
    all_gather x3, waiting for transfers between devices: 50.9 us -> 36.9 us  [gather_line(): return lax.all_gather(x, 'seq', axis=0, tiled=True, axis_index_groups=lines)]
    reduce_scatter x3, waiting for transfers between devices: 3.27 us -> 14.8 us  [scatter_column(): lax.psum_scatter(x, 'seq', scatter_dimension=0, tiled=True, axis_index_gr...]
    convert_element_type x7 -> x0, other arithmetic: 9.36 us -> none  [the longest x1 2.38 us: local(): gate_grad.astype(f32)]
  transfers between devices with their start and end apart: 18 -> 23, of which waited for: 6 -> 5; matrix products, arithmetic and copies ran while one was open for 27% -> 18% of each run, Pallas kernels for 47% -> 53%
where the time goes in v3:
time: 583 us; the launch traced here: 574 us
  Pallas kernels  344 us (59%)
  matrix products  71.1 us (12%)
  local copies, waits for them, and re-layouts  62.7 us (11%)
  waiting for transfers between devices  54.9 us (9%)
  between operations  15.6 us (3%)
  starting transfers between devices  14.1 us (2%)
  other arithmetic  12.2 us (2%)
    pallas_call x4, Pallas kernels, plane_stage(): pl.pallas_call(kernel, out_shape=shapes, in_specs=[vmem] * (has + len(blo...  158 us
    pallas_call x2, Pallas kernels, exchange(): pl.pallas_call(kernel, out_shape=[jax.ShapeDtypeStruct(s, d) for s, d in...  56 us
    pallas_call x2, Pallas kernels, carry_states(): pl.pallas_call(kernel, out_shape=[jax.ShapeDtypeStruct(keys.shape, f32)]...  47.4 us
    unnamed x163, local copies, waits for them, and re-layouts  47.1 us
    pallas_call x3, Pallas kernels, return_columns(): pl.pallas_call(kernel, out_shape=[jax.ShapeDtypeStruct(shape, f32) for sh...  47.1 us
    all_gather x3, waiting for transfers between devices, gather_line(): return lax.all_gather(x, 'seq', axis=0, tiled=True, axis_index_groups=lines)  36.9 us
    pallas_call x4, Pallas kernels, chip_sum(): pl.pallas_call(kernel, out_shape=jax.ShapeDtypeStruct((half, columns + mo...  30.6 us
    dot_general x9, matrix products, plain(): return jnp.einsum(form, left, right, preferred_element_type=f32)  25.7 us
  transfers between devices with their start and end apart: 23, of which 5 were waited for; matrix products, arithmetic and copies ran while one was open for 18% of the time, Pallas kernels for 53%

profile of v3, /device:TPU:0, one launch (start us, length us, event | category | flops | bytes accessed | tf_op | source)
XLA Modules:
  0.0 574.1 jit_solution(14624819975035267246)
XLA Ops:
  9.2 19.2 %shard_map.233 = bf16[256,2048]{1,0:T(8,128)(2,1)} custom-call(bf16[64,2048]{1,0:T(8,128)(2,1)} %refs_0_.5, bf16[64,2048]{1,0:T(8,128)(2,1)} %refs_1_.3, bf16[64,2048]{1,0:T(8,128)(2,1)} %refs_2_.3, bf16[64,2048]{1,0:T(8,128)(2,1)} %copy-done.27), custom_call_target="tpu_custom_call" | custom-call | bytes 61200000 | tf_op jit(solution)/shard_map/pallas_call | solution.py:53
  30.2 36.9 %shard_map.230 = (f32[32,8,128]{2,1,0:T(8,128)}, s32[4,160,64]{2,1,0:T(8,128)}, bf16[256,2816]{1,0:T(8,128)(2,1)}, bf16[256,1408]{1,0:T(8,128)(2,1)}) custom-call(f32[8,128]{1,0:T(8,128)} %fusion.54.refs_0_, s32[4,160,64]{2,1,0:T(8,128)} %bitcast.145, bf16[64,5632]{1,0:T(8,128)(2,1)} %refs_2_.2, bf16[64,5632]{1,0:T(8,128)(2,1)} %refs_3_.1, ...), custom_call_target="tpu_custom_call" | custom-call | bytes 122400000 | tf_op jit(solution)/shard_map/pallas_call | solution.py:53
  68.2 1.7 shard_map.229
  70.0 24.9 %shard_map.231.a = bf16[640,2048]{1,0:T(8,128)(2,1)S(1)} custom-call(bf16[160,2048]{1,0:T(8,128)(2,1)S(1)} %get-tuple-element.69.refs_0_.refs_1_, f32[1,2048]{1,0:T(1,128)S(1)} %broadcast_in_dim_reshape.6.refs_1_.refs_3_), custom_call_target="tpu_custom_call" | custom-call | bytes 85000000 | tf_op jit(solution)/shard_map/pallas_call | solution.py:373
  101.7 8.3 %all-gather.4.cloned.1.call-done = bf16[2048,2048]{1,0:T(8,128)(2,1)} async-done(((bf16[256,2048]{1,0:T(8,128)(2,1)}), bf16[2048,2048]{1,0:T(8,128)(2,1)}) %all-gather.4.cloned.1.call-update) | async-done | bytes 8388624 | tf_op jit(solution)/shard_map/all_gather | solution.py:702
  110.0 1.6 slice-done
  112.2 1.6 collective-permute-start
  114.2 1.5 collective-permute-start.1
  116.7 7.8 %fusion.6 = bf16[640,1536]{1,0:T(8,128)(2,1)S(1)} fusion(bf16[640,2048]{1,0:T(8,128)(2,1)S(1)} %copy-done.1, bf16[2048,2048]{1,0:T(8,128)(2,1)} %all-gather.4.cloned.1.call-done), kind=kOutput, calls=%fused_computation.11 | convolution fusion | flops 4027514880 | bytes 10878976 | tf_op jit(solution)/shard_map/dot_general | solution.py:793
  126.1 23.7 %shard_map.234 = (f32[4,64,512]{2,1,0:T(8,128)S(1)}, f32[4,64,512]{2,1,0:T(8,128)S(1)}) custom-call(f32[4,64,512]{2,1,0:T(8,128)S(1)} %fusion.29.k_in, f32[4,64,512]{2,1,0:T(8,128)S(1)} %fusion.28.v_in, f32[4,64,128]{2,1,0:T(8,128)S(1)} %broadcast_in_dim.77.g_in), custom_call_target="tpu_custom_call" | custom-call | bytes 74800000 | tf_op jit(solution)/shard_map/pallas_call | solution.py:647
  156.2 2.4 collective-permute-start.5
  158.6 1.9 pad_maximum_fusion.1
  161.3 2.0 pad_maximum_fusion.2
  165.3 1.5 convolution_convert_fusion.1.refs_0_
  166.8 52.9 %shard_map.235 = (f32[160,2048]{1,0:T(8,128)S(1)}, bf16[640,2048]{1,0:T(8,128)(2,1)S(1)}) custom-call(bf16[640,2048]{1,0:T(8,128)(2,1)S(1)} %convolution_convert_fusion.1.refs_0_, bf16[160,2048]{1,0:T(8,128)(2,1)S(1)} %get-tuple-element.69.refs_0_.refs_1_, f32[1,2048]{1,0:T(1,128)S(1)} %broadcast_in_dim_reshape.7.refs_2_.refs_3_), custom_call_target="tpu_custom_call" | custom-call | bytes 170000000 | tf_op jit(solution)/shard_map/pallas_call | solution.py:373
  220.8 1.5 copy-done.39
  223.4 2.0 constant_dynamic-update-slice_fusion.2
  225.4 12.3 %fusion.65 = f32[640,2816]{1,0:T(8,128)S(1)} fusion(bf16[640,2048]{1,0:T(8,128)(2,1)} %copy-done.39, bf16[2048,2816]{1,0:T(8,128)(2,1)} %all-gather.6.cloned.1.call-done), kind=kOutput, calls=%fused_computation.138 | convolution fusion | flops 7381975040 | bytes 21364736 | tf_op jit(solution)/shard_map/dot_general | solution.py:837
  238.8 2.0 copy-done.53
  240.8 2.0 constant_dynamic-update-slice_fusion.1
  243.7 2.6 constant_dynamic-slice_fusion.3
  249.2 2.9 shard_map.237.a
  253.4 7.4 %shard_map.236 = bf16[1024,1408]{1,0:T(8,128)(2,1)S(1)} custom-call(s32[1]{0:T(128)} %bitcast.which, bf16[640,2048]{1,0:T(8,128)(2,1)} %constant_dynamic-update-slice_fusion.a, bf16[640,1408]{1,0:T(8,128)(2,1)S(1)} %fusion.5.b.refs_4_, bf16[640,1024]{1,0:T(8,128)(2,1)} %collective-permute-done.6.c, bf16[640,1408]{1,0:T(8,128)(2,1)} %collective-permute-done.7.d), custom_call_target="tpu_custom_call" | custom-call | flops 3690987520 | bytes 9109504 | tf_op jit(solution)/shard_map/pallas_call | solution.py:417
  260.8 1.5 copy-done.7
  262.4 28.6 %all-gather.8.cloned.1.call-done.refs_5_ = bf16[2048,1408]{1,0:T(8,128)(2,1)} async-done(((bf16[256,1408]{1,0:T(8,128)(2,1)}), bf16[2048,1408]{1,0:T(8,128)(2,1)}) %all-gather.8.cloned.1.call-update) | async-done | bytes 5767184 | tf_op jit(solution)/shard_map/all_gather | solution.py:702
  291.0 10.6 %multiply_convert_fusion.1 = (bf16[640,1408]{1,0:T(8,128)(2,1)S(1)}, bf16[640,1408]{1,0:T(8,128)(2,1)S(1)}) fusion(f32[640,2816]{1,0:T(8,128)} %copy-done.53, bf16[640,2048]{1,0:T(8,128)(2,1)} %constant_dynamic-update-slice_fusion.a, bf16[2048,1408]{1,0:T(8,128)(2,1)} %all-gather.8.cloned.1.call-done.refs_5_), kind=kOutput, calls=%fused_computation.9 | convolution fusion | flops 3702702080 | bytes 19202048 | tf_op jit(solution)/shard_map/dot_general | solution.py:853
  302.2 11.8 %convolution_convert_fusion.refs_0_ = bf16[640,2048]{1,0:T(8,128)(2,1)} fusion(bf16[2048,2816]{1,0:T(8,128)(2,1)} %all-gather.6.cloned.1.call-done, bf16[640,1408]{1,0:T(8,128)(2,1)S(1)} %get-tuple-element.129, bf16[640,1408]{1,0:T(8,128)(2,1)S(1)} %get-tuple-element.128), kind=kOutput, calls=%fused_computation.13 | convolution fusion | flops 7390494720 | bytes 17760256 | tf_op jit(solution)/shard_map/tf,df->td/dot_general | solution.py:671
  313.9 12.7 %shard_map.238 = bf16[1024,2816]{1,0:T(8,128)(2,1)} custom-call(s32[1]{0:T(128)} %bitcast.which, bf16[640,2048]{1,0:T(8,128)(2,1)S(1)} %copy-done.41, bf16[640,2816]{1,0:T(8,128)(2,1)S(1)} %pad_maximum_fusion.b, bf16[640,1024]{1,0:T(8,128)(2,1)} %collective-permute-done.8.c, bf16[640,2816]{1,0:T(8,128)(2,1)S(1)} %collective-permute-done.10.d), custom_call_target="tpu_custom_call" | custom-call | flops 7381975040 | bytes 15597568 | tf_op jit(solution)/shard_map/pallas_call | solution.py:417
  328.0 1.7 copy-done.10
  330.9 50.9 %shard_map.239 = (f32[160,2048]{1,0:T(8,128)S(1)}, f32[8,2048]{1,0:T(8,128)S(1)}, bf16[640,2048]{1,0:T(8,128)(2,1)}, bf16[160,2048]{1,0:T(8,128)(2,1)S(1)}, bf16...) custom-call(bf16[640,2048]{1,0:T(8,128)(2,1)S(1)} %copy-done.10, ...), custom_call_target="tpu_custom_call" | custom-call | bytes 170000000 | tf_op jit(solution)/shard_map/pallas_call | solution.py:373
  383.7 1.5 collective-permute-start.12
  385.7 1.5 collective-permute-start.14
  387.2 4.0 fusion.66
  399.9 4.5 shard_map.240
  404.3 23.7 %shard_map.241 = (f32[4,64,512]{2,1,0:T(8,128)S(1)}, f32[4,64,512]{2,1,0:T(8,128)S(1)}, bf16[1024,512]{1,0:T(8,128)(2,1)S(1)}) custom-call(f32[4,64,512]{2,1,0:T(8,128)S(1)} %fusion.22.k_in, f32[4,64,512]{2,1,0:T(8,128)S(1)} %fusion.25.v_in, f32[4,64,128]{2,1,0:T(8,128)S(1)} %broadcast_in_dim.77.g_in, bf16[1,4,64,2048]{3,2,1,0:T(8,128)(2,1)S(1)} %bitcast.122), custom_call_target="tpu_custom_call" | custom-call | bytes 74800000 | tf_op jit(solution)/shard_map/pallas_call | solution.py:647
  431.2 1.9 copy-done.2
  433.6 3.1 collective-permute-done.15.c
  436.7 6.1 %shard_map.242 = bf16[1024,2048]{1,0:T(8,128)(2,1)S(1)} custom-call(s32[1]{0:T(128)} %bitcast.which, bf16[640,2048]{1,0:T(8,128)(2,1)S(1)} %copy-done.2, bf16[640,1536]{1,0:T(8,128)(2,1)S(1)} %pad_maximum_fusion.3.b, bf16[640,1024]{1,0:T(8,128)(2,1)S(1)} %collective-permute-done.15.c, bf16[640,1536]{1,0:T(8,128)(2,1)S(1)} %collective-permute-done.16.d, ...), custom_call_target="tpu_custom_call" | custom-call | flops 4026531840 | bytes 9699328 | tf_op jit(solution)/shard_map/pallas_call | solution.py:417
  442.8 2.0 copy-done.6
  444.8 12.9 %reduce-scatter.6.cloned.1.call-done.refs_0_ = bf16[256,2816]{1,0:T(8,128)(2,1)} async-done(((bf16[1024,2816]{1,0:T(8,128)(2,1)}), bf16[256,2816]{1,0:T(8,128)(2,1)}) %reduce-scatter.6.cloned.1.call-update) | async-done | bytes 1441808 | tf_op jit(solution)/shard_map/reduce_scatter | solution.py:707
  460.3 11.3 %shard_map.246 = f32[64,5632]{1,0:T(8,128)S(1)} custom-call(bf16[256,1408]{1,0:T(8,128)(2,1)S(1)} %copy-done.28), custom_call_target="tpu_custom_call" | custom-call | bytes 47600000 | tf_op jit(solution)/shard_map/pallas_call | solution.py:199
  471.7 7.8 %fusion.9.refs_0_ = bf16[640,2048]{1,0:T(8,128)(2,1)S(1)} fusion(bf16[640,1536]{1,0:T(8,128)(2,1)} %copy-done.17, bf16[2048,2048]{1,0:T(8,128)(2,1)} %all-gather.4.cloned.1.call-done), kind=kOutput, calls=%fused_computation.12 | convolution fusion | flops 4027842560 | bytes 10878976 | tf_op jit(solution)/shard_map/tf,df->td/dot_general | solution.py:671
  479.5 28.8 %shard_map.243 = (f32[160,2048]{1,0:T(8,128)S(1)}, f32[8,2048]{1,0:T(8,128)S(1)}, bf16[160,2048]{1,0:T(8,128)(2,1)S(1)}) custom-call(bf16[640,2048]{1,0:T(8,128)(2,1)S(1)} %fusion.9.refs_0_, bf16[160,2048]{1,0:T(8,128)(2,1)S(1)} %get-tuple-element.69.refs_0_.refs_1_, f32[160,2048]{1,0:T(8,128)S(1)} %copy-done.24, ...), custom_call_target="tpu_custom_call" | custom-call | bytes 85000000 | tf_op jit(solution)/shard_map/pallas_call | solution.py:373
  510.8 1.5 reduce_sum.87
  514.6 18.7 %shard_map.245 = (f32[64,5632]{1,0:T(8,128)S(1)}, f32[64,5632]{1,0:T(8,128)S(1)}) custom-call(bf16[256,2816]{1,0:T(8,128)(2,1)S(1)} %copy-done.18), custom_call_target="tpu_custom_call" | custom-call | bytes 47600000 | tf_op jit(solution)/shard_map/pallas_call | solution.py:199
  535.5 1.9 reduce-scatter.8.cloned.1.call-done.refs_0_
  539.5 17.1 %shard_map.244 = (f32[64,2048]{1,0:T(8,128)S(1)}, f32[64,2048]{1,0:T(8,128)S(1)}, f32[64,2048]{1,0:T(8,128)S(1)}, f32[64,2048]{1,0:T(8,128)S(1)}, f32[8,128]{1,0:T(8,128)S(1)}) custom-call(bf16[256,2048]{1,0:T(8,128)(2,1)S(1)} %copy-done.26, f32[32,8,128]{2,1,0:T(8,128)S(1)} %copy-done.42), custom_call_target="tpu_custom_call" | custom-call | bytes 47600000 | tf_op jit(solution)/shard_map/pallas_call | solution.py:199
  558.0 2.5 copy.173
  (275 shorter events, 69.4 us)
Async XLA Ops:
  7.2 102.9 %all-gather.4.cloned.1.call-start = ((), (), s32[]{:S(2)}) async-start(), calls=%async_computation.3 | async-start | bytes 9437184 | tf_op jit(solution)/shard_map/all_gather | solution.py:702
  8.2 20.3 %copy-start.66 = (s32[160,256]{1,0:T(8,128)S(1)}, s32[160,256]{1,0:T(8,128)}, u32[]{:S(2)}) copy-start(s32[160,256]{1,0:T(8,128)} %param.16) | copy-start | bytes 491524
  9.2 20.3 %copy-start.69 = (bf16[64]{0:T(256)(128)(2,1)S(1)}, bf16[64]{0:T(256)(128)(2,1)}, u32[]{:S(2)}) copy-start(bf16[64]{0:T(256)(128)(2,1)} %param.24) | copy-start | bytes 388
  9.2 20.3 %copy-start.70 = (bf16[64]{0:T(256)(128)(2,1)S(1)}, bf16[64]{0:T(256)(128)(2,1)}, u32[]{:S(2)}) copy-start(bf16[64]{0:T(256)(128)(2,1)} %param.22) | copy-start | bytes 388
  9.2 20.3 %copy-start.71 = (bf16[64]{0:T(256)(128)(2,1)S(1)}, bf16[64]{0:T(256)(128)(2,1)}, u32[]{:S(2)}) copy-start(bf16[64]{0:T(256)(128)(2,1)} %param.18) | copy-start | bytes 388
  28.5 196.9 %all-gather.6.cloned.1.call-start = ((), (), s32[]{:S(2)}) async-start(), calls=%async_computation.4 | async-start | bytes 12976128 | tf_op jit(solution)/shard_map/all_gather | solution.py:702
  30.2 38.0 %copy-start.35 = (bf16[160,2048]{1,0:T(8,128)(2,1)S(1)}, bf16[160,2048]{1,0:T(8,128)(2,1)}, u32[]{:S(2)}) copy-start(bf16[160,2048]{1,0:T(8,128)(2,1)} %refs_0_.3) | copy-start | bytes 1966084
  30.2 38.0 %copy-start.36 = (bf16[160,2048]{1,0:T(8,128)(2,1)S(1)}, bf16[160,2048]{1,0:T(8,128)(2,1)}, u32[]{:S(2)}) copy-start(bf16[160,2048]{1,0:T(8,128)(2,1)} %refs_1_.2) | copy-start | bytes 1966084
  67.1 224.0 %all-gather.8.cloned.1.call-start = ((), (), s32[]{:S(2)}) async-start(), calls=%async_computation.5 | async-start | bytes 6488064 | tf_op jit(solution)/shard_map/all_gather | solution.py:702
  70.0 152.4 %copy-start.11 = (bf16[160,2048]{1,0:T(8,128)(2,1)}, bf16[160,2048]{1,0:T(8,128)(2,1)S(1)}, u32[]{:S(2)}) copy-start(bf16[160,2048]{1,0:T(8,128)(2,1)S(1)} %get-tuple-element.79.refs_2_) | copy-start | bytes 1966084
  70.0 29.3 %copy-start.72 = (s32[4]{0:T(128)S(1)}, s32[4]{0:T(128)}, u32[]{:S(2)}) copy-start(s32[4]{0:T(128)} %param.17) | copy-start | bytes 52
  70.0 29.8 %copy-start.65 = (s32[4,160,64]{2,1,0:T(8,128)S(1)}, s32[4,160,64]{2,1,0:T(8,128)}, u32[]{:S(2)}) copy-start(s32[4,160,64]{2,1,0:T(8,128)} %get-tuple-element.73) | copy-start | bytes 491524
  96.4 125.9 %collective-permute-start.3 = (bf16[160,2048]{1,0:T(8,128)(2,1)S(1)}, bf16[160,2048]{1,0:T(8,128)(2,1)}, u32[]{:S(2)}, u32[]{:S(2)}) collective-permute-start(bf16[160,2048]{1,0:T(8,128)(2,1)S(1)} %get-tuple-element.79.refs_2_), channel_id=1, source_target_pairs={{0,2},{1,3},{2,0},{3,1},{4,6},{5,7},{6,4},{7,5},{8,10},{9,11},{10,... | collective-permute-start | bytes 1966088 | tf_op jit(solution)/shard_map/ppermute | solution.py:733
  97.0 125.3 %collective-permute-start.4 = (bf16[160,2048]{1,0:T(8,128)(2,1)S(1)}, bf16[160,2048]{1,0:T(8,128)(2,1)}, u32[]{:S(2)}, u32[]{:S(2)}) collective-permute-start(bf16[160,2048]{1,0:T(8,128)(2,1)S(1)} %get-tuple-element.79.refs_2_), channel_id=1, source_target_pairs={{0,4},{1,5},{2,6},{3,7},{4,0},{5,1},{6,2},{7,3},{8,12},{9,13},{10,... | collective-permute-start | bytes 1966088 | tf_op jit(solution)/shard_map/ppermute | solution.py:733
  98.4 288.7 %reduce-scatter.4.cloned.1.call-start = ((), (), s32[]{:S(2)}) async-start(), calls=%async_computation.6 | async-start | bytes 3604480 | tf_op jit(solution)/shard_map/reduce_scatter | solution.py:707
  100.5 53.6 %copy-start.47 = (f32[4,64,160]{2,1,0:T(8,128)}, f32[4,64,160]{2,1,0:T(8,128)S(1)}, u32[]{:S(2)}) copy-start(f32[4,64,160]{2,1,0:T(8,128)S(1)} %fusion.38) | copy-start | bytes 491524
  101.1 51.4 %copy-start.49 = (f32[4,160,64]{2,1,0:T(8,128)}, f32[4,160,64]{2,1,0:T(8,128)S(1)}, u32[]{:S(2)}) copy-start(f32[4,160,64]{2,1,0:T(8,128)S(1)} %bitcast_multiply_fusion) | copy-start | bytes 491524
  112.2 44.0 %collective-permute-start = (bf16[2,1,4,64,512]{4,2,3,0,1:T(4,128)(2,1)S(1)}, bf16[2,1,4,64,512]{4,2,3,0,1:T(4,128)(2,1)S(1)}, u32[]{:S(2)}, u32[]{:S(2)}) collective-permute-start(bf16[2,1,4,64,512]{4,2,3,0,1:T(4,128)(2,1)S(1)} %copy.149), channel_id=1, source_target_pairs={{0,2},{1,3},{2,0},{3,1},{4,6},{5,7},{6,4},{7,5},{8,10},{9,11},{10,... | collective-permute-start | bytes 1572872 | tf_op jit(solution)/shard_map/ppermute | solution.py:733
  114.2 44.4 %collective-permute-start.1 = (bf16[2,1,4,64,512]{4,2,3,0,1:T(4,128)(2,1)S(1)}, bf16[2,1,4,64,512]{4,2,3,0,1:T(4,128)(2,1)S(1)}, u32[]{:S(2)}, u32[]{:S(2)}) collective-permute-start(bf16[2,1,4,64,512]{4,2,3,0,1:T(4,128)(2,1)S(1)} %copy.150), channel_id=1, source_target_pairs={{0,4},{1,5},{2,6},{3,7},{4,0},{5,1},{6,2},{7,3},{8,12},{9,13},{10,... | collective-permute-start | bytes 1572872 | tf_op jit(solution)/shard_map/ppermute | solution.py:733
  116.1 42.5 %collective-permute-start.2 = (bf16[2,1,4,64,512]{4,2,3,0,1:T(4,128)(2,1)S(1)}, bf16[2,1,4,64,512]{4,2,3,0,1:T(4,128)(2,1)S(1)}, u32[]{:S(2)}, u32[]{:S(2)}) collective-permute-start(bf16[2,1,4,64,512]{4,2,3,0,1:T(4,128)(2,1)S(1)} %copy.151), channel_id=1, source_target_pairs={{0,6},{1,7},{2,4},{3,5},{4,2},{5,3},{6,0},{7,1},{8,14},{9,15},{10,... | collective-permute-start | bytes 1572872 | tf_op jit(solution)/shard_map/ppermute | solution.py:733
  124.6 25.9 %copy-start.51 = (bf16[640,512]{1,0:T(8,128)(2,1)}, bf16[640,512]{1,0:T(8,128)(2,1)S(1)}, u32[]{:S(2)}) copy-start(bf16[640,512]{1,0:T(8,128)(2,1)S(1)} %get-tuple-element.140) | copy-start | bytes 1966084
  124.6 25.9 %copy-start.56 = (bf16[640,512]{1,0:T(8,128)(2,1)}, bf16[640,512]{1,0:T(8,128)(2,1)S(1)}, u32[]{:S(2)}) copy-start(bf16[640,512]{1,0:T(8,128)(2,1)S(1)} %get-tuple-element.139) | copy-start | bytes 1966084
  124.7 28.7 %copy-start.58 = (bf16[640,512]{1,0:T(8,128)(2,1)}, bf16[640,512]{1,0:T(8,128)(2,1)S(1)}, u32[]{:S(2)}) copy-start(bf16[640,512]{1,0:T(8,128)(2,1)S(1)} %get-tuple-element.138) | copy-start | bytes 1966084
  125.3 25.3 %copy-start.67 = (pred[160,160]{1,0:T(8,128)(4,1)S(1)}, pred[160,160]{1,0:T(8,128)(4,1)}, u32[]{:S(2)}) copy-start(pred[160,160]{1,0:T(8,128)(4,1)} %iota_compare_fusion) | copy-start | bytes 76804
  156.1 7.8 %copy-start.8 = (bf16[4,160,512]{2,1,0:T(8,128)(2,1)}, bf16[4,160,512]{2,1,0:T(8,128)(2,1)S(1)}, u32[]{:S(2)}) copy-start(bf16[4,160,512]{2,1,0:T(8,128)(2,1)S(1)} %multiply_convert_fusion.3) | copy-start | bytes 1966084
  156.2 66.1 %collective-permute-start.5 = (bf16[160,2048]{1,0:T(8,128)(2,1)S(1)}, bf16[160,2048]{1,0:T(8,128)(2,1)S(1)}, u32[]{:S(2)}, u32[]{:S(2)}) collective-permute-start(bf16[160,2048]{1,0:T(8,128)(2,1)S(1)} %get-tuple-element.79.refs_2_), channel_id=1, source_target_pairs={{0,6},{1,7},{2,4},{3,5},{4,2},{5,3},{6,0},{7,1},{8,14},{9,15},{10,... | collective-permute-start | bytes 1966088 | tf_op jit(solution)/shard_map/ppermute | solution.py:733
  240.8 12.6 %collective-permute-start.7 = (bf16[640,1408]{1,0:T(8,128)(2,1)S(1)}, bf16[640,1408]{1,0:T(8,128)(2,1)}, u32[]{:S(2)}, u32[]{:S(2)}) collective-permute-start(bf16[640,1408]{1,0:T(8,128)(2,1)S(1)} %fusion.5.b.refs_4_), channel_id=1, source_target_pairs={{0,1},{1,0},{2,3},{3,2},{4,5},{5,4},{6,7},{7,6},{8,9},{9,8},{10,11... | collective-permute-start | bytes 5406728 | tf_op jit(solution)/shard_map/ppermute | solution.py:712
  246.3 7.0 %collective-permute-start.6 = (bf16[640,1024]{1,0:T(8,128)(2,1)}, bf16[640,1024]{1,0:T(8,128)(2,1)}, u32[]{:S(2)}, u32[]{:S(2)}) collective-permute-start(bf16[640,1024]{1,0:T(8,128)(2,1)} %constant_dynamic-slice_fusion.3), channel_id=1, source_target_pairs={{0,1},{1,0},{2,3},{3,2},{4,5},{5,4},{6,7},{7,6},{8,9},{9,8},{10,11... | collective-permute-start | bytes 3932168 | tf_op jit(solution)/shard_map/ppermute | solution.py:712
  248.1 42.9 %collective-permute-start.8 = (bf16[640,1024]{1,0:T(8,128)(2,1)}, bf16[640,1024]{1,0:T(8,128)(2,1)}, u32[]{:S(2)}, u32[]{:S(2)}) collective-permute-start(bf16[640,1024]{1,0:T(8,128)(2,1)} %constant_dynamic-slice_fusion.2), channel_id=1, source_target_pairs={{0,1},{1,0},{2,3},{3,2},{4,5},{5,4},{6,7},{7,6},{8,9},{9,8},{10,11... | collective-permute-start | bytes 3932168 | tf_op jit(solution)/shard_map/ppermute | solution.py:712
  252.9 38.2 %collective-permute-start.9 = (bf16[640,256]{1,0:T(8,128)(2,1)}, bf16[640,256]{1,0:T(8,128)(2,1)}, u32[]{:S(2)}, u32[]{:S(2)}) collective-permute-start(bf16[640,256]{1,0:T(8,128)(2,1)} %constant_dynamic-slice_fusion.1), channel_id=1, source_target_pairs={{0,1},{1,0},{2,3},{3,2},{4,5},{5,4},{6,7},{7,6},{8,9},{9,8},{10,11... | collective-permute-start | bytes 983048 | tf_op jit(solution)/shard_map/ppermute | solution.py:712
  262.4 195.3 %reduce-scatter.6.cloned.1.call-start = ((), (), s32[]{:S(2)}) async-start(), calls=%async_computation.7 | async-start | bytes 7208960 | tf_op jit(solution)/shard_map/reduce_scatter | solution.py:707
  301.9 12.1 %copy-start.41 = (bf16[640,2048]{1,0:T(8,128)(2,1)S(1)}, bf16[640,2048]{1,0:T(8,128)(2,1)}, u32[]{:S(2)}) copy-start(bf16[640,2048]{1,0:T(8,128)(2,1)} %copy-done.39) | copy-start | bytes 7864324
  301.9 12.1 %collective-permute-start.10 = (bf16[640,2816]{1,0:T(8,128)(2,1)S(1)}, bf16[640,2816]{1,0:T(8,128)(2,1)S(1)}, u32[]{:S(2)}, u32[]{:S(2)}) collective-permute-start(bf16[640,2816]{1,0:T(8,128)(2,1)S(1)} %pad_maximum_fusion.b), channel_id=1, source_target_pairs={{0,1},{1,0},{2,3},{3,2},{4,5},{5,4},{6,7},{7,6},{8,9},{9,8},{10,11... | collective-permute-start | bytes 10813448 | tf_op jit(solution)/shard_map/ppermute | solution.py:712
  326.7 210.8 %reduce-scatter.8.cloned.1.call-start = ((), (), s32[]{:S(2)}) async-start(), calls=%async_computation.8 | async-start | bytes 5242880 | tf_op jit(solution)/shard_map/reduce_scatter | solution.py:707
  383.7 16.2 %collective-permute-start.11 = (bf16[640,2048]{1,0:T(8,128)(2,1)}, bf16[640,2048]{1,0:T(8,128)(2,1)}, u32[]{:S(2)}, u32[]{:S(2)}) collective-permute-start(bf16[640,2048]{1,0:T(8,128)(2,1)} %get-tuple-element.94.b), channel_id=1, source_target_pairs={{0,1},{1,0},{2,3},{3,2},{4,5},{5,4},{6,7},{7,6},{8,9},{9,8},{10,11... | collective-permute-start | bytes 7864328 | tf_op jit(solution)/shard_map/ppermute | solution.py:712
  383.7 44.4 %collective-permute-start.12 = (bf16[160,2048]{1,0:T(8,128)(2,1)}, bf16[160,2048]{1,0:T(8,128)(2,1)S(1)}, u32[]{:S(2)}, u32[]{:S(2)}) collective-permute-start(bf16[160,2048]{1,0:T(8,128)(2,1)} %get-tuple-element.99), channel_id=1, source_target_pairs={{0,2},{1,3},{2,0},{3,1},{4,6},{5,7},{6,4},{7,5},{8,10},{9,11},{10,... | collective-permute-start | bytes 1966088 | tf_op jit(solution)/shard_map/ppermute | solution.py:733
  385.2 42.9 %collective-permute-start.13 = (bf16[160,2048]{1,0:T(8,128)(2,1)}, bf16[160,2048]{1,0:T(8,128)(2,1)S(1)}, u32[]{:S(2)}, u32[]{:S(2)}) collective-permute-start(bf16[160,2048]{1,0:T(8,128)(2,1)} %get-tuple-element.100), channel_id=1, source_target_pairs={{0,4},{1,5},{2,6},{3,7},{4,0},{5,1},{6,2},{7,3},{8,12},{9,13},{10,... | collective-permute-start | bytes 1966088 | tf_op jit(solution)/shard_map/ppermute | solution.py:733
  385.7 42.4 %collective-permute-start.14 = (bf16[160,2048]{1,0:T(8,128)(2,1)}, bf16[160,2048]{1,0:T(8,128)(2,1)}, u32[]{:S(2)}, u32[]{:S(2)}) collective-permute-start(bf16[160,2048]{1,0:T(8,128)(2,1)} %get-tuple-element.101), channel_id=1, source_target_pairs={{0,6},{1,7},{2,4},{3,5},{4,2},{5,3},{6,0},{7,1},{8,14},{9,15},{10,... | collective-permute-start | bytes 1966088 | tf_op jit(solution)/shard_map/ppermute | solution.py:733
  430.8 5.9 %collective-permute-start.16 = (bf16[640,1536]{1,0:T(8,128)(2,1)S(1)}, bf16[640,1536]{1,0:T(8,128)(2,1)S(1)}, u32[]{:S(2)}, u32[]{:S(2)}) collective-permute-start(bf16[640,1536]{1,0:T(8,128)(2,1)S(1)} %pad_maximum_fusion.3.b), channel_id=1, source_target_pairs={{0,1},{1,0},{2,3},{3,2},{4,5},{5,4},{6,7},{7,6},{8,9},{9,8},{10,11... | collective-permute-start | bytes 5898248 | tf_op jit(solution)/shard_map/ppermute | solution.py:712
  433.2 3.5 collective-permute-start.15
  444.8 15.5 %copy-start.28 = (bf16[256,1408]{1,0:T(8,128)(2,1)S(1)}, bf16[256,1408]{1,0:T(8,128)(2,1)}, u32[]{:S(2)}) copy-start(bf16[256,1408]{1,0:T(8,128)(2,1)} %reduce-scatter.4.cloned.1.call-done.refs_0_) | copy-start | bytes 2162692
  471.6 7.8 %copy-start.5 = (f32[160,2048]{1,0:T(8,128)S(1)}, f32[160,2048]{1,0:T(8,128)}, u32[]{:S(2)}) copy-start(f32[160,2048]{1,0:T(8,128)} %copy-done.3) | copy-start | bytes 3932164
  471.6 7.8 %copy-start.24 = (f32[160,2048]{1,0:T(8,128)S(1)}, f32[160,2048]{1,0:T(8,128)}, u32[]{:S(2)}) copy-start(f32[160,2048]{1,0:T(8,128)} %copy-done.23) | copy-start | bytes 3932164
  471.7 7.8 %copy-start.30 = (bf16[160,2048]{1,0:T(8,128)(2,1)S(1)}, bf16[160,2048]{1,0:T(8,128)(2,1)}, u32[]{:S(2)}) copy-start(bf16[160,2048]{1,0:T(8,128)(2,1)} %copy-done.29) | copy-start | bytes 1966084
  471.7 7.8 %copy-start.32 = (bf16[160,2048]{1,0:T(8,128)(2,1)S(1)}, bf16[160,2048]{1,0:T(8,128)(2,1)}, u32[]{:S(2)}) copy-start(bf16[160,2048]{1,0:T(8,128)(2,1)} %copy-done.31) | copy-start | bytes 1966084
  471.7 7.8 %copy-start.34 = (bf16[160,2048]{1,0:T(8,128)(2,1)S(1)}, bf16[160,2048]{1,0:T(8,128)(2,1)}, u32[]{:S(2)}) copy-start(bf16[160,2048]{1,0:T(8,128)(2,1)} %copy-done.33) | copy-start | bytes 1966084
  479.5 35.1 %copy-start.18 = (bf16[256,2816]{1,0:T(8,128)(2,1)S(1)}, bf16[256,2816]{1,0:T(8,128)(2,1)}, u32[]{:S(2)}) copy-start(bf16[256,2816]{1,0:T(8,128)(2,1)} %reduce-scatter.6.cloned.1.call-done.refs_0_) | copy-start | bytes 4325380
  510.8 46.4 %copy-start.38 = (bf16[160,2048]{1,0:T(8,128)(2,1)S(1)}, bf16[160,2048]{1,0:T(8,128)(2,1)}, u32[]{:S(2)}) copy-start(bf16[160,2048]{1,0:T(8,128)(2,1)} %copy-done.37) | copy-start | bytes 1966084
  (49 other events, 93.0 us)
Sparse Core Ops, SparseCore 0:
  28.6 81.4 all-gather.3
  111.6 110.5 all-gather.5
  223.9 67.1 all-gather.7
  293.2 54.8 reduce-scatter.3
  350.2 107.3 reduce-scatter.5
  459.8 77.5 reduce-scatter.7

commit v4 on v3

--- a/solution.py
+++ b/solution.py
@@ -21,49 +21,6 @@
     return pl.CostEstimate(flops=0, bytes_accessed=us * 3_400_000, transcendentals=0)
 
 
-def exchange(cid, us, arrays, outs, moves, plan):
-    def kernel(*refs):
-        ins = refs[: len(arrays)]
-        dsts = refs[len(arrays) : len(arrays) + len(outs)]
-        send, recv = refs[len(arrays) + len(outs) :]
-        me = lax.axis_index("seq")
-        peers, copies = plan(me, ins, dsts)
-        barrier = pltpu.get_barrier_semaphore()
-        for peer in peers:
-            pl.semaphore_signal(barrier, inc=1, device_id=(peer,), device_id_type=MESH)
-        pl.semaphore_wait(barrier, len(peers))
-        started = []
-        for k, (src, dst, device) in enumerate(copies):
-            if device is None:
-                copy = pltpu.make_async_copy(src, dst, send.at[k])
-            else:
-                copy = pltpu.make_async_remote_copy(
-                    src_ref=src,
-                    dst_ref=dst,
-                    send_sem=send.at[k],
-                    recv_sem=recv.at[k],
-                    device_id=(device,),
-                    device_id_type=MESH,
-                )
-            copy.start()
-            started.append(copy)
-        for copy in started:
-            copy.wait()
-
-    return pl.pallas_call(
-        kernel,
-        out_shape=[jax.ShapeDtypeStruct(s, d) for s, d in outs],
-        in_specs=[ANY] * len(arrays),
-        out_specs=[ANY] * len(outs),
-        scratch_shapes=[
-            pltpu.SemaphoreType.DMA((moves,)),
-            pltpu.SemaphoreType.DMA((moves,)),
-        ],
-        compiler_params=pltpu.CompilerParams(collective_id=cid, has_side_effects=True),
-        cost_estimate=lasting(us),
-    )(*arrays)
-
-
 def chip_of(me):
     return lax.rem(lax.div(me, 2), HEADS)
 
@@ -81,78 +38,280 @@
     return ref.at[:, pl.ds(pl.multiple_of(block * size, 128), size)]
 
 
-def first_exchange(cid, weights, output_rows):
-    rows, width = weights[0].shape
+def opening(cid, gains, codes, weights, output_rows, feed, tokens, planes):
+    strip, width = weights[0].shape
     part = width // HEADS
-
-    def plan(me, ins, outs):
+    feed_part = feed[0].shape[1] // HEADS
+    count = planes * PLANE
+    hops = planes - 1
+
+    tokens_rows = tokens.shape[0]
+
+    def kernel(g0_in, g1_in, g2_in, codes_in, q_far, k_far, v_far, o_in, gate_far, up_far, down_far, t_in,
+               g_out, c_out, line, feed_out, down_out, t_out, gain, t_mine, g_in, c_in, q_in, k_in, v_in,
+               gate_in, up_in, down_in, load, t_send, t_recv, own_sem, q_send, q_recv, side_send, side_recv, u_send, u_recv, d_send, d_recv, s_send, s_recv):
+        me = lax.axis_index("seq")
         h = chip_of(me)
-        targets = [chip_on(me, h, k) for k in (2, 1, 3)] + [(None, h)]
-        at = pl.ds(pl.multiple_of(h * rows, rows), rows)
-        moves = []
-        for device, other in targets:
-            for j in range(3):
-                dst = outs[0].at[at, pl.ds(j * part, part)]
-                moves.append((columns_at(ins[j], other, part), dst, device))
+        core = lax.rem(me, 2)
+        z = lax.div(me, PLANE)
+        sibling = me + 1 - 2 * core
+        chips = [(None, h)] + [chip_on(me, h, k) for k in (1, 2, 3)]
+        everyone = [lax.rem(me + k, count) for k in range(1, count)]
+        far = (q_far, k_far, v_far, gate_far, up_far, down_far)
+        near = (q_in, k_in, v_in, gate_in, up_in, down_in)
+        loads = [pltpu.make_async_copy(a, b, load.at[n]) for n, (a, b) in enumerate(zip(far, near))]
+        for copy in loads:
+            copy.start()
+        barrier = pltpu.get_barrier_semaphore()
+        for device in everyone:
+            pl.semaphore_signal(barrier, inc=1, device_id=(device,), device_id_type=MESH)
+        g_in[...] = jnp.zeros_like(g_in)
+        for n, ref in enumerate((g0_in, g1_in, g2_in)):
+            g_in[n : n + 1, 0:strip] = ref[...].astype(f32)
         for k in range(HEADS):
-            dst = outs[0].at[pl.ds(k * rows, rows), pl.ds(3 * part, part)]
-            moves.append((ins[3].at[:, pl.ds(k * part, part)], dst, None))
-        return [p for p, _ in targets[:3]], moves
-
-    shape = (HEADS * rows, 4 * part)
-    return exchange(cid, 18, [*weights, output_rows], [(shape, bf16)], 16, plan)[0]
-
-
-def second_exchange(cid, gains, codes, gate, up, down, count):
-    rows, width = gate.shape
-    part = width // HEADS
-
-    def plan(me, ins, outs):
-        h = chip_of(me)
-        g_in, c_in = ins[:2]
-        everyone = [lax.rem(me + k, count) for k in range(1, count)]
-        targets = [chip_on(me, h, k) for k in (1, 2, 3)] + [(None, h)]
-        at = pl.ds(pl.multiple_of(h * rows, rows), rows)
-        moves = [(g_in, outs[0].at[me], p) for p in everyone] + [(g_in, outs[0].at[me], None)]
-        for k, (device, other) in zip((1, 2, 3, 0), targets):
-            moves.append((c_in.at[other], outs[1].at[k], device))
-        for w, out, column in ((2, 2, 0), (3, 2, part), (4, 3, 0)):
-            for device, other in targets:
-                dst = outs[out].at[at, pl.ds(column, part)]
-                moves.append((columns_at(ins[w], other, part), dst, device))
-        return everyone, moves
-
-    return exchange(
-        cid,
-        36,
-        [gains, codes, gate, up, down],
-        [
-            ((count, *gains.shape), gains.dtype),
-            (codes.shape, codes.dtype),
-            ((HEADS * rows, 2 * part), bf16),
-            ((HEADS * rows, part), bf16),
+            c_in[k] = codes_in[:, pl.ds(k * SLOTS, SLOTS)]
+        for copy in loads[:3]:
+            copy.wait()
+        pl.semaphore_wait(barrier, count - 1)
+
+        def remote(src, dst, s, r, device):
+            return pltpu.make_async_remote_copy(
+                src_ref=src, dst_ref=dst, send_sem=s, recv_sem=r, device_id=(device,), device_id_type=MESH
+            )
+
+        def row(plane, chip):
+            return pl.ds(pl.multiple_of(((core * planes + plane) * HEADS + chip) * strip, strip), strip)
+
+        def unit(plane, k):
+            return line.at[row(plane, chips[k][1])]
+
+        def up(d, k):
+            n = (d - 1) * HEADS + k
+            return remote(unit(z - d + 1, k), unit(z - d + 1, k), u_send.at[n], u_recv.at[n], me + PLANE)
+
+        def down(d, k):
+            n = (d - 1) * HEADS + k
+            return remote(unit(z + d - 1, k), unit(z + d - 1, k), d_send.at[n], d_recv.at[n], me - PLANE)
+
+        def across(plane, k):
+            n = plane * HEADS + k
+            return remote(unit(plane, k), unit(plane, k), s_send.at[n], s_recv.at[n], sibling)
+
+        def pass_on(k):
+            @pl.when(z + 1 < planes)
+            def _():
+                up(1, k).start()
+
+            @pl.when(z >= 1)
+            def _():
+                down(1, k).start()
+
+            across(z, k).start()
+
+        projections = []
+        for k in (3, 1, 2):
+            device, chip = chips[k]
+            for j, w in enumerate((q_in, k_in, v_in)):
+                n = 3 * (k - 1) + j
+                dst = line.at[row(z, h), pl.ds(j * part, part)]
+                projections.append((k, remote(columns_at(w, chip, part), dst, q_send.at[n], q_recv.at[n], device)))
+        own = [
+            pltpu.make_async_copy(
+                columns_at(w, h, part), line.at[row(z, h), pl.ds(j * part, part)], own_sem.at[j]
+            )
+            for j, w in enumerate((q_in, k_in, v_in))
+        ]
+        for _, copy in projections:
+            copy.start()
+        for copy in own:
+            copy.start()
+        turned = reorder(o_in[...], planes, False)
+        for k in range(HEADS):
+            line[row(z, k), pl.ds(3 * part, part)] = turned[:, k * part : (k + 1) * part]
+        for copy in own:
+            copy.wait()
+        pass_on(0)
+
+        shared = [(g_in, g_out.at[me], device) for device in everyone]
+        sides = [(c_in.at[chip], c_out.at[k], device) for k, (device, chip) in list(enumerate(chips))[1:]]
+        at = pl.ds(pl.multiple_of(h * strip, strip), strip)
+        for src, out, column in ((gate_in, feed_out, 0), (up_in, feed_out, feed_part), (down_in, down_out, 0)):
+            for device, chip in chips[1:] + chips[:1]:
+                dst = out.at[at, pl.ds(column, feed_part)]
+                sides.append((columns_at(src, chip, feed_part), dst, device))
+        sides.append((c_in.at[h], c_out.at[0], None))
+        begun = []
+
+        def begin(listed):
+            for src, dst, device in listed:
+                n = len(begun)
+                if device is None:
+                    copy = pltpu.make_async_copy(src, dst, side_send.at[n])
+                else:
+                    copy = remote(src, dst, side_send.at[n], side_recv.at[n], device)
+                copy.start()
+                begun.append(copy)
+
+        begin(shared)
+        g_out[me] = g_in[...]
+        for k in (1, 2, 3):
+            for other, copy in projections:
+                if other == k:
+                    copy.wait_recv()
+            pass_on(k)
+        for copy in begun:
+            copy.wait()
+        shares = begun[:]
+        gain[...] = jnp.concatenate(
+            [
+                g_out[(p * PLANE + c * 2 + k), 0:1, 0:strip]
+                for k in range(2)
+                for p in range(planes)
+                for c in range(HEADS)
+            ],
+            axis=1,
+        )
+
+        def step(i, carry):
+            at = pl.ds(pl.multiple_of(i * STEP, STEP), STEP)
+            x = t_in[at, :].astype(f32)
+            t_mine[at, :] = (reorder(x * factor_of(x), planes, False) * gain[...]).astype(bf16)
+            return carry
+
+        half = tokens_rows // 2
+        low, high = pl.ds(0, half), pl.ds(half, half)
+        x_side, y_side = chips[1][0], chips[2][0]
+
+        def spread_out(mine, everything, sends, recvs):
+            def block(k, first):
+                return everything.at[pl.ds(k * tokens_rows + (0 if first else half), half)]
+
+            copies = [
+                remote(mine.at[low], block(1, True), sends.at[0], recvs.at[0], x_side),
+                remote(mine.at[high], block(2, False), sends.at[1], recvs.at[1], y_side),
+                remote(mine.at[high], block(1, False), sends.at[2], recvs.at[2], x_side),
+                remote(mine.at[low], block(2, True), sends.at[3], recvs.at[3], y_side),
+                remote(block(1, True), block(3, True), sends.at[4], recvs.at[4], y_side),
+                remote(block(2, False), block(3, False), sends.at[5], recvs.at[5], x_side),
+            ]
+            keep = pltpu.make_async_copy(mine, everything.at[pl.ds(0, tokens_rows)], sends.at[6])
+            for copy in copies[:4]:
+                copy.start()
+            keep.start()
+            return copies, keep
+
+        def relay(copies):
+            copies[0].wait_recv()
+            copies[4].start()
+            copies[1].wait_recv()
+            copies[5].start()
+
+        def finish(copies, keep):
+            for copy in copies[:2]:
+                copy.wait_send()
+            for copy in copies[2:]:
+                copy.wait()
+            keep.wait()
+
+        lax.fori_loop(0, tokens_rows // STEP, step, 0)
+        spread_t = spread_out(t_mine, t_out, t_send, t_recv)
+        for copy in loads[3:]:
+            copy.wait()
+        begin(sides)
+        for d in range(1, planes):
+            for k in range(HEADS):
+
+                @pl.when(z - d >= 0)
+                def _(d=d, k=k):
+                    up(d, k).wait_recv()
+
+                    @pl.when(z + 1 < planes)
+                    def _():
+                        up(d + 1, k).start()
+
+                    across(z - d, k).start()
+
+                @pl.when(z + d < planes)
+                def _(d=d, k=k):
+                    down(d, k).wait_recv()
+
+                    @pl.when(z >= 1)
+                    def _():
+                        down(d + 1, k).start()
+
+                    across(z + d, k).start()
+
+            if d == 1:
+                relay(spread_t[0])
+        for _, copy in projections:
+            copy.wait_send()
+        finish(*spread_t)
+        for copy in begun[len(shares) :]:
+            copy.wait()
+        for d in range(1, planes):
+            for k in range(HEADS):
+
+                @pl.when((z - d + 1 >= 0) & (z + 1 < planes))
+                def _(d=d, k=k):
+                    up(d, k).wait_send()
+
+                @pl.when((z + d - 1 < planes) & (z >= 1))
+                def _(d=d, k=k):
+                    down(d, k).wait_send()
+
+        for plane in range(planes):
+            for k in range(HEADS):
+                across(plane, k).wait()
+
+    sides = count + 4 + 12
+    vmem = pl.BlockSpec(memory_space=pltpu.VMEM)
+    sizes = (6, 7, 6, 3, 9, 9, sides, sides) + (hops * HEADS,) * 4 + (planes * HEADS,) * 2
+    shares = jax.ShapeDtypeStruct((count, 8, 128), f32)
+    logits = jax.ShapeDtypeStruct((HEADS, tokens_rows, SLOTS), codes.dtype)
+    return pl.pallas_call(
+        kernel,
+        out_shape=[
+            shares,
+            logits,
+            jax.ShapeDtypeStruct((count * strip, 4 * part), bf16),
+            jax.ShapeDtypeStruct((HEADS * strip, 2 * feed_part), bf16),
+            jax.ShapeDtypeStruct((HEADS * strip, feed_part), bf16),
+            jax.ShapeDtypeStruct((HEADS * tokens_rows, width), bf16),
         ],
-        count + 16,
-        plan,
-    )
-
-
-def return_columns(cid, x, pieces, part, planes, gains):
+        in_specs=[vmem] * 4 + [ANY] * 3 + [vmem] + [ANY] * 3 + [vmem],
+        out_specs=[vmem] * 5 + [ANY],
+        scratch_shapes=[
+            pltpu.VMEM((1, width), f32),
+            pltpu.VMEM(tokens.shape, bf16),
+            pltpu.VMEM((8, 128), f32),
+            pltpu.VMEM((HEADS, tokens_rows, SLOTS), codes.dtype),
+        ]
+        + [pltpu.VMEM(x.shape, bf16) for x in (*weights, *feed)]
+        + [pltpu.SemaphoreType.DMA((n,)) for n in sizes],
+        compiler_params=pltpu.CompilerParams(
+            collective_id=cid, has_side_effects=True, vmem_limit_bytes=58 << 20
+        ),
+        cost_estimate=lasting(85),
+    )(*(g[None] for g in gains), codes, *weights, output_rows, *feed, tokens)
+
+
+def return_columns(cid, x, pieces, part, planes, gains=None, own_rows=False):
     rows = x.shape[0] // HEADS
-    last = planes > 0
+    shared = gains is not None
     count = planes * PLANE
 
     def kernel(*refs):
         src, refs = refs[0], refs[1:]
-        shares, refs = (refs[0], refs[1:]) if last else (None, refs)
-        outs, rest = refs[:pieces], refs[pieces:]
-        extra, gain_out, rest = (rest[0], rest[1], rest[2:]) if last else (None, None, rest)
-        landed, send, recv, gain_in, gain_send, gain_recv = rest
+        shares, refs = (refs[0], refs[1:]) if shared else (None, refs)
+        outs, refs = refs[:pieces], refs[pieces:]
+        extra, refs = (refs[0], refs[1:]) if own_rows else (None, refs)
+        gain_out, refs = (refs[0], refs[1:]) if shared else (None, refs)
+        landed, send, recv, gain_in, gain_send, gain_recv = refs
         me = lax.axis_index("seq")
         h = chip_of(me)
         targets = [chip_on(me, h, k) for k in (3, 1, 2)]
         everyone = [lax.rem(me + k, count) for k in range(1, count)]
-        peers = everyone if last else [device for device, _ in targets]
+        peers = everyone if shared else [device for device, _ in targets]
         barrier = pltpu.get_barrier_semaphore()
         for device in peers:
             pl.semaphore_signal(barrier, inc=1, device_id=(device,), device_id_type=MESH)
@@ -163,6 +322,9 @@
                 src_ref=source, dst_ref=dst, send_sem=sends.at[n], recv_sem=recvs.at[n],
                 device_id=(device,), device_id_type=MESH,
             )
+
+        def place(j):
+            return landed.at[j, h] if own_rows else columns_at(outs[j], h, part)
 
         copies = []
         for k, (device, other) in enumerate(targets):
@@ -170,50 +332,78 @@
                 source = src.at[
                     pl.ds(pl.multiple_of(other * rows, rows), rows), pl.ds(j * part, part)
                 ]
-                copies.append(to(device, source, landed.at[j, h], send, recv, k * pieces + j))
-        if last:
+                copies.append(to(device, source, place(j), send, recv, k * pieces + j))
+        if shared:
             for n, device in enumerate(everyone):
                 copies.append(to(device, shares.at[device], gain_in.at[me], gain_send, gain_recv, n))
+        own = pl.ds(pl.multiple_of(h * rows, rows), rows)
+        for j in range(pieces):
+            copies.append(
+                pltpu.make_async_copy(src.at[own, pl.ds(j * part, part)], place(j), send.at[3 * pieces + j])
+            )
         for copy in copies:
             copy.start()
-        own = pl.ds(pl.multiple_of(h * rows, rows), rows)
-        for j in range(pieces):
-            landed[j, h] = src[own, pl.ds(j * part, part)]
-        if last:
+        if shared:
             gain_in[me] = shares[me]
+        if own_rows:
             blocks = [src[pl.ds(k * rows, rows), pl.ds(pieces * part, part)] for k in range(HEADS)]
             extra[...] = reorder(jnp.concatenate(blocks, axis=1).astype(f32), planes, True)
         for copy in copies:
             copy.wait()
-        for j in range(pieces):
-            for k in range(HEADS):
-                outs[j][:, pl.ds(k * part, part)] = landed[j, k].astype(f32)
-        if last:
+        if own_rows:
+            for j in range(pieces):
+                for k in range(HEADS):
+                    outs[j][:, pl.ds(k * part, part)] = landed[j, k].astype(f32)
+        if shared:
             total = gain_in[0]
             for k in range(1, count):
                 total = total + gain_in[k]
             gain_out[...] = total
 
     vmem = pl.BlockSpec(memory_space=pltpu.VMEM)
-    shapes = [(rows, HEADS * part)] * (pieces + int(last)) + [(8, 128)] * int(last)
+    kind = f32 if own_rows else bf16
+    shapes = [jax.ShapeDtypeStruct((rows, HEADS * part), kind)] * (pieces + int(own_rows))
+    shapes += [jax.ShapeDtypeStruct((8, 128), f32)] * int(shared)
     return pl.pallas_call(
         kernel,
-        out_shape=[jax.ShapeDtypeStruct(shape, f32) for shape in shapes],
-        in_specs=[vmem] * (1 + int(last)),
+        out_shape=shapes,
+        in_specs=[vmem] * (1 + int(shared)),
         out_specs=[vmem] * len(shapes),
         scratch_shapes=[
-            pltpu.VMEM((pieces, HEADS, rows, part), x.dtype),
+            pltpu.VMEM((pieces, HEADS, rows, part) if own_rows else (1, 1, 16, 128), x.dtype),
+            pltpu.SemaphoreType.DMA((4 * pieces,)),
             pltpu.SemaphoreType.DMA((3 * pieces,)),
-            pltpu.SemaphoreType.DMA((3 * pieces,)),
-            pltpu.VMEM((max(count, 1), 8, 128), f32),
-            pltpu.SemaphoreType.DMA((max(count, 2),)),
-            pltpu.SemaphoreType.DMA((max(count, 2),)),
+            pltpu.VMEM((count if shared else 1, 8, 128), f32),
+            pltpu.SemaphoreType.DMA((count if shared else 1,)),
+            pltpu.SemaphoreType.DMA((count if shared else 1,)),
         ],
         compiler_params=pltpu.CompilerParams(
             collective_id=cid, has_side_effects=True, vmem_limit_bytes=40 << 20
         ),
         cost_estimate=lasting(14),
-    )(*([x, gains] if last else [x]))
+    )(*([x, gains] if shared else [x]))
+
+
+def finished(narrow, others):
+    arrays = [*narrow, *others]
+    kinds = [f32] * len(narrow) + [x.dtype for x in others]
+
+    def kernel(*refs):
+        for src, dst in zip(refs[: len(arrays)], refs[len(arrays) :]):
+            dst[...] = src[...].astype(dst.dtype)
+
+    specs = [pl.BlockSpec((x.shape[0] // 2, x.shape[1]), lambda i: (i, 0)) for x in arrays]
+    if any(x.shape[0] % 32 for x in arrays):
+        specs = [pl.BlockSpec(x.shape, lambda i: (0, 0)) for x in arrays]
+    return pl.pallas_call(
+        kernel,
+        out_shape=[jax.ShapeDtypeStruct(x.shape, kind) for x, kind in zip(arrays, kinds)],
+        grid=(2 if specs[0].block_shape[0] < arrays[0].shape[0] else 1,),
+        in_specs=specs,
+        out_specs=specs,
+        compiler_params=pltpu.CompilerParams(vmem_limit_bytes=40 << 20),
+        cost_estimate=lasting(3),
+    )(*arrays)
 
 
 STEP = 16
@@ -436,12 +626,6 @@
     return lax.rsqrt(jnp.mean(x * x, axis=-1, keepdims=True) + epsilon)
 
 
-def norm_body(i, at, total, blocks, own, mine):
-    tokens, gain = blocks
-    x = tokens[at, :].astype(f32)
-    mine[at, :] = (x * factor_of(x) * gain[...]).astype(bf16)
-
-
 def residual_body(i, at, total, blocks, own, mine):
     tokens, gain = blocks
     x = tokens[at, :].astype(f32) + total
@@ -495,12 +679,20 @@
     return body
 
 
-def carry_states(cid, keys, values, gains, planes, reverse, rows_out=None):
-    more = int(rows_out is not None)
+def carry_states(cid, keys, values, gains, planes, reverse, rows_out=None, line=None):
+    lined = line is not None
+    more = int(rows_out is not None or lined)
     sent = bf16 if reverse else f32
     _, slots, size = keys.shape
     half = slots // 2
-    quarter, _, strip, _ = rows_out.shape if more else (1, 0, 0, 0)
+    if lined:
+        quarter, strip = planes // HEADS, line.shape[0] // (planes * PLANE)
+        landing, result = (HEADS, 2 * quarter, HEADS * strip, size), (size, HEADS * size)
+        links = 2 * quarter
+    elif more:
+        quarter, _, strip, _ = rows_out.shape
+        landing, result = (HEADS, quarter, strip, HEADS * size), (HEADS * quarter * HEADS * strip, size)
+        links = quarter
 
     def kernel(k_in, v_in, g_in, *refs):
         r_in, refs = (refs[0], refs[1:]) if more else (None, refs)
@@ -541,17 +733,26 @@
         for copy in copies:
             copy.start()
         swaps = []
+
+        def sent_rows(chip, n):
+            if not lined:
+                return r_in.at[n, chip]
+            at = ((n // quarter * planes) + chip * quarter + n % quarter) * HEADS * strip
+            return r_in.at[pl.ds(pl.multiple_of(at, HEADS * strip), HEADS * strip), pl.ds(3 * size, size)]
+
         if more:
             for n, (device, chip) in enumerate(chips):
-                for q in range(quarter):
-                    at = quarter * n + q
+                for q in range(links):
+                    at = links * n + q
                     swaps.append(
-                        remote(r_in.at[q, chip], r_all.at[h, q], r_send.at[at], r_recv.at[at], device)
+                        remote(sent_rows(chip, q), r_all.at[h, q], r_send.at[at], r_recv.at[at], device)
                     )
+            for q in range(links):
+                swaps.append(
+                    pltpu.make_async_copy(sent_rows(h, q), r_all.at[h, q], r_send.at[3 * links + q])
+                )
             for swap in swaps:
                 swap.start()
-            for q in range(quarter):
-                r_all[h, q] = r_in[q, h]
         for k in range(HEADS):
             chip = chip_on(me, h, k)[1]
             for src, dst in ((g_in, g_all), (k_in, k_all), (v_in, v_all)):
@@ -622,7 +823,13 @@
             v_out[k] = gain * v_base[...] + v_pre[chip, core]
         for swap in swaps:
             swap.wait()
-        if more:
+        if lined:
+            for c in range(HEADS):
+                for n in range(links):
+                    for b in range(HEADS):
+                        at = ((n % quarter * HEADS + c) * 2 + n // quarter) * strip
+                        r_out[pl.ds(at, strip), pl.ds(b * size, size)] = r_all[c, n, pl.ds(b * strip, strip), :]
+        elif more:
             for c in range(HEADS):
                 for q in range(quarter):
                     for b in range(HEADS):
@@ -641,14 +848,13 @@
     sends = [pltpu.VMEM((half, size), sent)] * 2
     side = []
     if more:
-        side = [pltpu.VMEM((HEADS, quarter, strip, HEADS * size), bf16)]
-        side += [pltpu.SemaphoreType.DMA((3 * quarter,))] * 2
+        side = [pltpu.VMEM(landing, bf16)] + [pltpu.SemaphoreType.DMA((4 * links,))] * 2
     semaphores = [12, 12, 3 * planes - 3, 3 * planes - 3, 2, 2]
     return pl.pallas_call(
         kernel,
         out_shape=[jax.ShapeDtypeStruct(keys.shape, f32)] * 2
-        + [jax.ShapeDtypeStruct((HEADS * quarter * HEADS * strip, size), bf16)] * more,
-        in_specs=[vmem] * (3 + more),
+        + ([jax.ShapeDtypeStruct(result, bf16)] if more else []),
+        in_specs=[vmem] * 3 + [ANY] * more,
         out_specs=[vmem] * (2 + more),
         scratch_shapes=side + wide + wide + state + far + state[:2] + sends
         + [pltpu.SemaphoreType.DMA((n,)) for n in semaphores],
@@ -656,7 +862,7 @@
             collective_id=cid, has_side_effects=True, vmem_limit_bytes=32 << 20
         ),
         cost_estimate=lasting(22),
-    )(keys, values, gains, *([rows_out] if more else []))
+    )(keys, values, gains, *([line if lined else rows_out] if more else []))
 
 
 def rms_factor(value_rows):
@@ -732,20 +938,15 @@
     def send_on(x, k):
         return lax.ppermute(x, "seq", turns[k])
 
-    def in_chip_order(parts):
-        whole = jnp.stack(parts)
-        return jnp.stack(
-            [lax.dynamic_index_in_dim(whole, j ^ h, keepdims=False) for j in range(HEADS)]
-        )
-
-    gains = jnp.stack([mixer_gain, head_gain, feed_gain]).astype(f32)
-    gains = jnp.pad(gains, ((0, 5), (0, 128 - strip)))
-    codes = gate_codes.reshape(rows, HEADS, SLOTS).swapaxes(0, 1)
-    (output_own,) = reordered([output_weight], planes)
-    mixer_rows = first_exchange(0, (query_weight, key_weight, value_weight), output_own)
-    mixer_line = gather_line(mixer_rows)
-    gains_all, codes_all, feed_rows, down_rows = second_exchange(
-        1, gains, codes, gate_weight, up_weight, down_weight, count
+    gains_all, codes_all, mixer_line, feed_rows, down_rows, h1 = opening(
+        0,
+        (mixer_gain, head_gain, feed_gain),
+        gate_codes,
+        (query_weight, key_weight, value_weight),
+        output_weight,
+        (gate_weight, up_weight, down_weight),
+        tokens,
+        planes,
     )
     feed_weight = gather_line(feed_rows)
     down_line = gather_line(down_rows)
@@ -754,10 +955,8 @@
     head_gain_f = lax.dynamic_slice(gain_of[1], (h * head_size,), (head_size,))
 
     tokens_own, cotangent_own = reordered([tokens, cotangent], planes)
-    (h1,) = plane_stage(2, None, [tokens_own, gain_one], norm_body, [], True)
-    h1, cotangent_sent = lax.optimization_barrier((h1, cotangent_own))
     h1_other = to_sibling(cut(h1, 1))
-    cotangent_parts = [cotangent_own] + [send_on(cotangent_sent, k) for k in (1, 2, 3)]
+    cotangent_parts = [cotangent_own] + [send_on(cotangent_own, k) for k in (1, 2, 3)]
 
     decay = jax.nn.log_sigmoid(codes_all.astype(f32) / 256.0)
     block = z * PLANE + 2 * ((h ^ jnp.arange(HEADS))) + core
@@ -796,13 +995,15 @@
     value = projected[:, 2 * head_size :].reshape(blocked)
     query_f = query.astype(f32)
 
-    key_state, value_state = carry_states(
+    key_state, value_state, out_weight = carry_states(
         3,
         precise("bsm,bsd->bmd", weights, key.astype(f32)),
         precise("bsm,bsd->bmd", weights, value.astype(f32)),
         carried,
         planes,
         False,
+        None,
+        mixer_line,
     )
 
     affinity = plain("btd,bsd->bts", query, key) * same
@@ -819,13 +1020,6 @@
     normed_heads = (unit_heads * head_gain_f).astype(bf16).reshape(HEADS * rows, head_size)
 
     quarter = planes // HEADS
-    output_line = mixer_line[:, 3 * head_size :].reshape(2, planes, HEADS, strip, head_size)
-    pieces = [
-        lax.dynamic_slice_in_dim(output_line, (h ^ k) * quarter, quarter, axis=1)
-        for k in range(HEADS)
-    ]
-    pieces = in_chip_order([pieces[0]] + [send_on(pieces[k], k) for k in (1, 2, 3)])
-    out_weight = pieces.transpose(2, 0, 1, 4, 3, 5).reshape(head_size, width)
     mixed = jnp.dot(normed_heads, out_weight, preferred_element_type=f32).astype(bf16)
     residual, h2 = plane_stage(
         4, mixed, [tokens_own, gain_two], residual_body, [((rows, width), f32)], True
@@ -833,13 +1027,14 @@
 
     h2, *cotangent_parts = lax.optimization_barrier((h2, *cotangent_parts))
     cotangent_all = jnp.concatenate(cotangent_parts)
+    cotangent_other = to_sibling(cut(cotangent_all, 1))
     part = down_line.shape[1]
     both = jnp.dot(h2, feed_weight, preferred_element_type=f32)
     sigma = jax.nn.sigmoid(both[:, :part])
     hidden = (both[:, :part] * sigma * both[:, part:]).astype(bf16)
     hidden, both = lax.optimization_barrier((hidden, both))
     down_part = chip_sum(
-        core, cotangent_all, hidden, to_sibling(cut(cotangent_all, 1)), to_sibling(hidden)
+        core, cotangent_all, hidden, cotangent_other, to_sibling(hidden)
     )
     down_sums = scatter_column(down_part)
     h2_other = to_sibling(cut(h2, 1))
@@ -915,7 +1110,10 @@
     )
     backs_other = to_sibling(backs)
     mixer_part = chip_sum(core, h1, backs, h1_other, backs_other, out_part)
-    mixer_part, feed_sums, backs = lax.optimization_barrier((mixer_part, feed_sums, backs))
+    (down_grad,) = return_columns(8, down_sums, 1, part, planes)
+    mixer_part, feed_sums, backs, down_grad = lax.optimization_barrier(
+        (mixer_part, feed_sums, backs, down_grad)
+    )
     mixer_sums = scatter_column(mixer_part)
     mixer_in = plain("tf,df->td", backs, mixer_weight).astype(bf16)
     input_grad, mixer_gain_part, block_out = plane_stage(
@@ -939,10 +1137,13 @@
     )
     gain_parts = gain_parts.reshape(3, count, strip).swapaxes(0, 1)
     gain_parts = jnp.pad(gain_parts, ((0, 0), (0, 5), (0, 128 - strip)))
-    (down_grad,) = return_columns(8, down_sums, 1, part, 0, None)
-    gate_grad, up_grad = return_columns(9, feed_sums, 2, part, 0, None)
-    query_grad, key_grad, value_grad, output_grad, gain_sums = return_columns(
-        10, mixer_sums, 3, head_size, planes, gain_parts
+    gate_grad, up_grad, gain_sums = return_columns(9, feed_sums, 2, part, planes, gain_parts)
+    down_grad, gate_grad, up_grad, input_grad, block_out = finished(
+        [down_grad, gate_grad, up_grad], [input_grad, block_out]
+    )
+    mixer_sums, _ = lax.optimization_barrier((mixer_sums, block_out))
+    query_grad, key_grad, value_grad, output_grad = return_columns(
+        10, mixer_sums, 3, head_size, planes, None, True
     )
     gain_sums = gain_sums[:3, :strip]
     return (

time: 583 us -> 554 us (0.950)
  Pallas kernels: 344 us -> 368 us
  local copies, waits for them, and re-layouts: 62.7 us -> 39.5 us
  waiting for transfers between devices: 54.9 us -> 37.6 us
  other arithmetic: 12.2 us -> 5.45 us
    pallas_call x5, Pallas kernels: 103 us -> 140 us  [the longest x1 89.4 us: opening(): pl.pallas_call(kernel, out_shape=[shares, logits, jax.ShapeDtypeStruct((c...]
    pallas_call x4 -> x3, Pallas kernels: 158 us -> 128 us  [plane_stage(): pl.pallas_call(kernel, out_shape=shapes, in_specs=[vmem] * (has + len(blo...]
    unnamed x163 -> x127, local copies, waits for them, and re-layouts: 47.1 us -> 28 us
    pallas_call x2, Pallas kernels: 47.4 us -> 64.3 us  [carry_states(): pl.pallas_call(kernel, out_shape=[jax.ShapeDtypeStruct(keys.shape, f32)]...]
    all_gather x3 -> x2, waiting for transfers between devices: 36.9 us -> 22.7 us  [gather_line(): return lax.all_gather(x, 'seq', axis=0, tiled=True, axis_index_groups=lines)]
  transfers between devices with their start and end apart: 23 -> 19, of which waited for: 5 -> 3; matrix products, arithmetic and copies ran while one was open for 18% -> 17% of each run, Pallas kernels for 53% -> 49%
where the time goes in v4:
time: 554 us; the launch traced here: 548 us
  Pallas kernels  368 us (66%)
  matrix products  73.5 us (13%)
  local copies, waits for them, and re-layouts  39.5 us (7%)
  waiting for transfers between devices  37.6 us (7%)
  between operations  15.5 us (3%)
  starting transfers between devices  8.74 us (2%)
    pallas_call x3, Pallas kernels, plane_stage(): pl.pallas_call(kernel, out_shape=shapes, in_specs=[vmem] * (has + len(blo...  128 us
    pallas_call x1, Pallas kernels, opening(): pl.pallas_call(kernel, out_shape=[shares, logits, jax.ShapeDtypeStruct((c...  89.4 us
    pallas_call x2, Pallas kernels, carry_states(): pl.pallas_call(kernel, out_shape=[jax.ShapeDtypeStruct(keys.shape, f32)]...  64.3 us
    pallas_call x3, Pallas kernels, return_columns(): pl.pallas_call(kernel, out_shape=shapes, in_specs=[vmem] * (1 + int(share...  48.2 us
    pallas_call x4, Pallas kernels, chip_sum(): pl.pallas_call(kernel, out_shape=jax.ShapeDtypeStruct((half, columns + mo...  30.7 us
    unnamed x127, local copies, waits for them, and re-layouts  28 us
    dot_general x9, matrix products, plain(): return jnp.einsum(form, left, right, preferred_element_type=f32)  25.7 us
    all_gather x2, waiting for transfers between devices, gather_line(): return lax.all_gather(x, 'seq', axis=0, tiled=True, axis_index_groups=lines)  22.7 us
  transfers between devices with their start and end apart: 19, of which 3 were waited for; matrix products, arithmetic and copies ran while one was open for 17% of the time, Pallas kernels for 49%

profile of v4, /device:TPU:0, one launch (start us, length us, event | category | flops | bytes accessed | tf_op | source)
XLA Modules:
  0.0 548.1 jit_solution(14665420572477215156)
XLA Ops:
  7.2 89.4 %shard_map.229 = (f32[32,8,128]{2,1,0:T(8,128)}, s32[4,160,64]{2,1,0:T(8,128)}, bf16[2048,2048]{1,0:T(8,128)(2,1)}, bf16[256,2816]{1,0:T(8,128)(2,1)}, bf16[256,...) custom-call(bf16[1,64]{1,0:T(2,128)(2,1)} %bitcast.138, bf16[1,64]{1,0:T(2,128)(2,1)} %bitcast.139, bf16[1,64]{1,0:T(2,128)(2,1)} %bitcast.140, ...), custom_call_target="tpu_custom_call" | custom-call | bytes 289000000 | tf_op jit(solution)/shard_map/pallas_call | solution.py:271
  96.8 1.7 shard_map.231
  98.5 1.5 collective-permute-start
  100.6 1.4 collective-permute-start.2
  103.9 8.8 %fusion.6 = bf16[640,1536]{1,0:T(8,128)(2,1)S(1)} fusion(bf16[640,2048]{1,0:T(8,128)(2,1)} %get-tuple-element.77.a, bf16[2048,2048]{1,0:T(8,128)(2,1)} %get-tuple-element.79.refs_0_), kind=kOutput, calls=%fused_computation.11 | convolution fusion | flops 4027514880 | bytes 10878976 | tf_op jit(solution)/shard_map/dot_general | solution.py:992
  115.0 39.0 %shard_map.230 = (f32[4,64,512]{2,1,0:T(8,128)S(1)}, f32[4,64,512]{2,1,0:T(8,128)S(1)}, bf16[512,2048]{1,0:T(8,128)(2,1)S(1)}) custom-call(f32[4,64,512]{2,1,0:T(8,128)S(1)} %fusion.29.k_in, f32[4,64,512]{2,1,0:T(8,128)S(1)} %fusion.28.v_in, f32[4,64,128]{2,1,0:T(8,128)S(1)} %broadcast_in_dim.89.g_in, bf16[2048,2048]{1,0:T(8,128)(2,1)S(1)} %bitcast.110), custom_call_target="tpu_custom_call" | custom-call | bytes 74800000 | tf_op jit(solution)/shard_map/pallas_call | solution.py:853
  157.9 1.4 multiply_reduce_fusion.2
  159.8 3.4 convolution_convert_fusion.1.refs_0_
  163.2 47.2 %shard_map.232 = (f32[160,2048]{1,0:T(8,128)S(1)}, bf16[640,2048]{1,0:T(8,128)(2,1)S(1)}) custom-call(bf16[640,2048]{1,0:T(8,128)(2,1)S(1)} %convolution_convert_fusion.1.refs_0_, bf16[160,2048]{1,0:T(8,128)(2,1)S(1)} %get-tuple-element.84.refs_1_, f32[1,2048]{1,0:T(1,128)S(1)} %broadcast_in_dim_reshape.6.refs_2_.refs_3_), custom_call_target="tpu_custom_call" | custom-call | bytes 170000000 | tf_op jit(solution)/shard_map/pallas_call | solution.py:563
  210.4 1.5 copy-done.34
  212.8 2.0 constant_dynamic-update-slice_fusion.2
  214.8 11.9 %fusion.55 = f32[640,2816]{1,0:T(8,128)S(1)} fusion(bf16[640,2048]{1,0:T(8,128)(2,1)} %copy-done.34, bf16[2048,2816]{1,0:T(8,128)(2,1)} %all-gather.3.cloned.1.call-done), kind=kOutput, calls=%fused_computation.115 | convolution fusion | flops 7381975040 | bytes 21364736 | tf_op jit(solution)/shard_map/dot_general | solution.py:1032
  227.8 1.9 copy-done.46
  229.7 2.2 constant_dynamic-update-slice_fusion.1
  231.9 2.0 constant_dynamic-update-slice_fusion.a
  233.9 2.5 constant_dynamic-slice_fusion.3
  236.7 1.2 constant_dynamic-slice_fusion.2
  238.1 2.9 shard_map.234.a
  241.9 1.7 constant_dynamic-slice_fusion.1
  243.9 7.4 %shard_map.233 = bf16[1024,1408]{1,0:T(8,128)(2,1)S(1)} custom-call(s32[1]{0:T(128)} %bitcast.which, bf16[640,2048]{1,0:T(8,128)(2,1)} %constant_dynamic-update-slice_fusion.a, bf16[640,1408]{1,0:T(8,128)(2,1)S(1)} %fusion.5.b.refs_4_, bf16[640,1024]{1,0:T(8,128)(2,1)} %collective-permute-done.3.c, bf16[640,1408]{1,0:T(8,128)(2,1)} %collective-permute-done.4.d), custom_call_target="tpu_custom_call" | custom-call | flops 3690987520 | bytes 9109504 | tf_op jit(solution)/shard_map/pallas_call | solution.py:607
  251.4 1.5 copy-done.3
  253.2 22.7 %all-gather.5.cloned.1.call-done.refs_5_ = bf16[2048,1408]{1,0:T(8,128)(2,1)} async-done(((bf16[256,1408]{1,0:T(8,128)(2,1)}), bf16[2048,1408]{1,0:T(8,128)(2,1)}) %all-gather.5.cloned.1.call-update) | async-done | bytes 5767184 | tf_op jit(solution)/shard_map/all_gather | solution.py:908
  275.9 10.6 %multiply_convert_fusion.1 = (bf16[640,1408]{1,0:T(8,128)(2,1)S(1)}, bf16[640,1408]{1,0:T(8,128)(2,1)S(1)}) fusion(f32[640,2816]{1,0:T(8,128)} %copy-done.46, bf16[640,2048]{1,0:T(8,128)(2,1)} %constant_dynamic-update-slice_fusion.a, bf16[2048,1408]{1,0:T(8,128)(2,1)} %all-gather.5.cloned.1.call-done.refs_5_), kind=kOutput, calls=%fused_computation.9 | convolution fusion | flops 3702702080 | bytes 19202048 | tf_op jit(solution)/shard_map/dot_general | solution.py:1048
  287.0 11.8 %convolution_convert_fusion.refs_0_ = bf16[640,2048]{1,0:T(8,128)(2,1)} fusion(bf16[2048,2816]{1,0:T(8,128)(2,1)} %all-gather.3.cloned.1.call-done, bf16[640,1408]{1,0:T(8,128)(2,1)S(1)} %get-tuple-element.145, bf16[640,1408]{1,0:T(8,128)(2,1)S(1)} %get-tuple-element.144), kind=kOutput, calls=%fused_computation.13 | convolution fusion | flops 7390494720 | bytes 17760256 | tf_op jit(solution)/shard_map/tf,df->td/dot_general | solution.py:877
  298.8 12.7 %shard_map.235 = bf16[1024,2816]{1,0:T(8,128)(2,1)} custom-call(s32[1]{0:T(128)} %bitcast.which, bf16[640,2048]{1,0:T(8,128)(2,1)S(1)} %copy-done.36, bf16[640,2816]{1,0:T(8,128)(2,1)S(1)} %pad_maximum_fusion.b, bf16[640,1024]{1,0:T(8,128)(2,1)} %collective-permute-done.5.c, bf16[640,2816]{1,0:T(8,128)(2,1)S(1)} %collective-permute-done.7.d), custom_call_target="tpu_custom_call" | custom-call | flops 7381975040 | bytes 15597568 | tf_op jit(solution)/shard_map/pallas_call | solution.py:607
  311.6 1.7 copy-done.9
  313.3 1.1 copy-done.11
  314.4 51.1 %shard_map.236 = (f32[160,2048]{1,0:T(8,128)S(1)}, f32[8,2048]{1,0:T(8,128)S(1)}, bf16[640,2048]{1,0:T(8,128)(2,1)}, bf16[160,2048]{1,0:T(8,128)(2,1)S(1)}, bf16...) custom-call(bf16[640,2048]{1,0:T(8,128)(2,1)S(1)} %copy-done.9, ...), custom_call_target="tpu_custom_call" | custom-call | bytes 170000000 | tf_op jit(solution)/shard_map/pallas_call | solution.py:563
  367.4 1.5 collective-permute-start.10
  368.9 1.5 collective-permute-start.11
  370.9 4.0 fusion.56
  381.7 1.2 fusion.14
  383.0 4.5 shard_map.237
  387.5 25.3 %shard_map.238 = (f32[4,64,512]{2,1,0:T(8,128)S(1)}, f32[4,64,512]{2,1,0:T(8,128)S(1)}, bf16[1024,512]{1,0:T(8,128)(2,1)S(1)}) custom-call(f32[4,64,512]{2,1,0:T(8,128)S(1)} %fusion.22.k_in, f32[4,64,512]{2,1,0:T(8,128)S(1)} %fusion.25.v_in, f32[4,64,128]{2,1,0:T(8,128)S(1)} %broadcast_in_dim.89.g_in, bf16[1,4,64,2048]{3,2,1,0:T(8,128)(2,1)S(1)} %bitcast.111), custom_call_target="tpu_custom_call" | custom-call | bytes 74800000 | tf_op jit(solution)/shard_map/pallas_call | solution.py:853
  412.8 1.3 fusion.12
  414.1 1.3 fusion.13
  415.7 2.2 copy-done.33
  418.1 11.3 %shard_map.240.refs_0_ = bf16[64,5632]{1,0:T(8,128)(2,1)S(1)} custom-call(bf16[256,1408]{1,0:T(8,128)(2,1)S(1)} %copy-done.23), custom_call_target="tpu_custom_call" | custom-call | bytes 47600000 | tf_op jit(solution)/shard_map/pallas_call | solution.py:367
  429.4 6.1 %shard_map.239 = bf16[1024,2048]{1,0:T(8,128)(2,1)S(1)} custom-call(s32[1]{0:T(128)} %bitcast.which, bf16[640,2048]{1,0:T(8,128)(2,1)S(1)} %copy-done.33, bf16[640,1536]{1,0:T(8,128)(2,1)S(1)} %pad_maximum_fusion.1.b, bf16[640,1024]{1,0:T(8,128)(2,1)S(1)} %collective-permute-done.12.c, bf16[640,1536]{1,0:T(8,128)(2,1)S(1)} %collective-permute-done.13.d, ...), custom_call_target="tpu_custom_call" | custom-call | flops 4026531840 | bytes 9699328 | tf_op jit(solution)/shard_map/pallas_call | solution.py:607
  435.5 2.0 copy-done
  437.5 5.2 reduce-scatter.6.cloned.1.call-done.refs_0_
  445.4 7.8 %fusion.9.refs_0_ = bf16[640,2048]{1,0:T(8,128)(2,1)S(1)} fusion(bf16[640,1536]{1,0:T(8,128)(2,1)} %copy-done.16, bf16[2048,2048]{1,0:T(8,128)(2,1)} %get-tuple-element.79.refs_0_), kind=kOutput, calls=%fused_computation.12 | convolution fusion | flops 4027842560 | bytes 10878976 | tf_op jit(solution)/shard_map/tf,df->td/dot_general | solution.py:877
  453.3 29.5 %shard_map.241 = (f32[160,2048]{1,0:T(8,128)S(1)}, f32[8,2048]{1,0:T(8,128)S(1)}, bf16[160,2048]{1,0:T(8,128)(2,1)S(1)}) custom-call(bf16[640,2048]{1,0:T(8,128)(2,1)S(1)} %fusion.9.refs_0_, bf16[160,2048]{1,0:T(8,128)(2,1)S(1)} %copy-done.5, f32[160,2048]{1,0:T(8,128)S(1)} %copy-done.19, f32[1,2048]{1,0:T(1,128)S(1)} %broadcast_in_dim_reshape.7.refs_3_, ...), custom_call_target="tpu_custom_call" | custom-call | bytes 85000000 | tf_op jit(solution)/shard_map/pallas_call | solution.py:563
  485.7 24.7 %shard_map.242 = (bf16[64,5632]{1,0:T(8,128)(2,1)S(1)}, bf16[64,5632]{1,0:T(8,128)(2,1)S(1)}, f32[8,128]{1,0:T(8,128)S(1)}) custom-call(bf16[256,2816]{1,0:T(8,128)(2,1)S(1)} %copy-done.17, f32[32,8,128]{2,1,0:T(8,128)S(1)} %pad.4.refs_1_), custom_call_target="tpu_custom_call" | custom-call | bytes 47600000 | tf_op jit(solution)/shard_map/pallas_call | solution.py:367
  511.5 2.9 shard_map.243
  514.9 9.6 %reduce-scatter.8.cloned.1.call-done.refs_0_ = bf16[256,2048]{1,0:T(8,128)(2,1)} async-done(((bf16[1024,2048]{1,0:T(8,128)(2,1)}), bf16[256,2048]{1,0:T(8,128)(2,1)}) %reduce-scatter.8.cloned.1.call-update) | async-done | bytes 1048592 | tf_op jit(solution)/shard_map/reduce_scatter | solution.py:913
  524.5 1.2 copy-done.22
  525.7 12.2 %shard_map.244 = (f32[64,2048]{1,0:T(8,128)S(1)}, f32[64,2048]{1,0:T(8,128)S(1)}, f32[64,2048]{1,0:T(8,128)S(1)}, f32[64,2048]{1,0:T(8,128)S(1)}) custom-call(bf16[256,2048]{1,0:T(8,128)(2,1)S(1)} %copy-done.22), custom_call_target="tpu_custom_call" | custom-call | bytes 47600000 | tf_op jit(solution)/shard_map/pallas_call | solution.py:367
  (220 shorter events, 33.2 us)
Async XLA Ops:
  7.2 207.6 %all-gather.3.cloned.1.call-start = ((), (), s32[]{:S(2)}) async-start(), calls=%async_computation.3 | async-start | bytes 12976128 | tf_op jit(solution)/shard_map/all_gather | solution.py:908
  7.2 89.5 %copy-start.6 = (bf16[160,2048]{1,0:T(8,128)(2,1)S(1)}, bf16[160,2048]{1,0:T(8,128)(2,1)}, u32[]{:S(2)}) copy-start(bf16[160,2048]{1,0:T(8,128)(2,1)} %refs_0_.1) | copy-start | bytes 1966084
  7.2 89.5 %copy-start.32 = (bf16[160,2048]{1,0:T(8,128)(2,1)S(1)}, bf16[160,2048]{1,0:T(8,128)(2,1)}, u32[]{:S(2)}) copy-start(bf16[160,2048]{1,0:T(8,128)(2,1)} %refs_1_.1) | copy-start | bytes 1966084
  96.6 5.6 %copy-start.57 = (s32[4]{0:T(128)S(1)}, s32[4]{0:T(128)}, u32[]{:S(2)}) copy-start(s32[4]{0:T(128)} %param.17) | copy-start | bytes 52
  96.7 6.2 %copy-start.55 = (s32[4,160,64]{2,1,0:T(8,128)S(1)}, s32[4,160,64]{2,1,0:T(8,128)}, u32[]{:S(2)}) copy-start(s32[4,160,64]{2,1,0:T(8,128)} %get-tuple-element.78) | copy-start | bytes 491524
  96.7 179.2 %all-gather.5.cloned.1.call-start = ((), (), s32[]{:S(2)}) async-start(), calls=%async_computation.4 | async-start | bytes 6488064 | tf_op jit(solution)/shard_map/all_gather | solution.py:908
  98.5 64.7 %copy-start.4 = (bf16[160,2048]{1,0:T(8,128)(2,1)}, bf16[160,2048]{1,0:T(8,128)(2,1)S(1)}, u32[]{:S(2)}) copy-start(bf16[160,2048]{1,0:T(8,128)(2,1)S(1)} %get-tuple-element.84.refs_1_) | copy-start | bytes 1966084
  98.5 113.4 %copy-start.10 = (bf16[160,2048]{1,0:T(8,128)(2,1)}, bf16[160,2048]{1,0:T(8,128)(2,1)S(1)}, u32[]{:S(2)}) copy-start(bf16[160,2048]{1,0:T(8,128)(2,1)S(1)} %get-tuple-element.88.refs_2_) | copy-start | bytes 1966084
  98.5 113.4 %collective-permute-start = (bf16[160,2048]{1,0:T(8,128)(2,1)S(1)}, bf16[160,2048]{1,0:T(8,128)(2,1)}, u32[]{:S(2)}, u32[]{:S(2)}) collective-permute-start(bf16[160,2048]{1,0:T(8,128)(2,1)S(1)} %get-tuple-element.88.refs_2_), channel_id=1, source_target_pairs={{0,2},{1,3},{2,0},{3,1},{4,6},{5,7},{6,4},{7,5},{8,10},{9,11},{10,... | collective-permute-start | bytes 1966088 | tf_op jit(solution)/shard_map/ppermute | solution.py:939
  100.1 111.8 %collective-permute-start.1 = (bf16[160,2048]{1,0:T(8,128)(2,1)S(1)}, bf16[160,2048]{1,0:T(8,128)(2,1)}, u32[]{:S(2)}, u32[]{:S(2)}) collective-permute-start(bf16[160,2048]{1,0:T(8,128)(2,1)S(1)} %get-tuple-element.88.refs_2_), channel_id=1, source_target_pairs={{0,4},{1,5},{2,6},{3,7},{4,0},{5,1},{6,2},{7,3},{8,12},{9,13},{10,... | collective-permute-start | bytes 1966088 | tf_op jit(solution)/shard_map/ppermute | solution.py:939
  100.6 111.3 %collective-permute-start.2 = (bf16[160,2048]{1,0:T(8,128)(2,1)S(1)}, bf16[160,2048]{1,0:T(8,128)(2,1)}, u32[]{:S(2)}, u32[]{:S(2)}) collective-permute-start(bf16[160,2048]{1,0:T(8,128)(2,1)S(1)} %get-tuple-element.88.refs_2_), channel_id=1, source_target_pairs={{0,6},{1,7},{2,4},{3,5},{4,2},{5,3},{6,0},{7,1},{8,14},{9,15},{10,... | collective-permute-start | bytes 1966088 | tf_op jit(solution)/shard_map/ppermute | solution.py:939
  102.1 268.8 %reduce-scatter.4.cloned.1.call-start = ((), (), s32[]{:S(2)}) async-start(), calls=%async_computation.5 | async-start | bytes 3604480 | tf_op jit(solution)/shard_map/reduce_scatter | solution.py:913
  103.5 54.4 %copy-start.40 = (f32[4,64,160]{2,1,0:T(8,128)}, f32[4,64,160]{2,1,0:T(8,128)S(1)}, u32[]{:S(2)}) copy-start(f32[4,64,160]{2,1,0:T(8,128)S(1)} %fusion.38) | copy-start | bytes 491524
  103.9 11.0 %slice-start = ((s8[8388608]{0:T(1024)(128)(4,1)}), s8[4194304]{0:T(1024)(128)(4,1)S(1)}, s32[]{:S(2)}) async-start(s8[8388608]{0:T(1024)(128)(4,1)} %bitcast.109), calls=%async_computation.8 | async-start | bytes 8388608
  103.9 11.0 %slice-start.1 = ((s8[8388608]{0:T(1024)(128)(4,1)}), s8[4194304]{0:T(1024)(128)(4,1)S(1)}, s32[]{:S(2)}) async-start(s8[8388608]{0:T(1024)(128)(4,1)} %bitcast.109), calls=%async_computation.9 | async-start | bytes 8388608
  113.4 43.3 %copy-start.42 = (f32[4,160,64]{2,1,0:T(8,128)}, f32[4,160,64]{2,1,0:T(8,128)S(1)}, u32[]{:S(2)}) copy-start(f32[4,160,64]{2,1,0:T(8,128)S(1)} %bitcast_multiply_fusion) | copy-start | bytes 491524
  113.5 41.4 %copy-start.44 = (bf16[640,512]{1,0:T(8,128)(2,1)}, bf16[640,512]{1,0:T(8,128)(2,1)S(1)}, u32[]{:S(2)}) copy-start(bf16[640,512]{1,0:T(8,128)(2,1)S(1)} %get-tuple-element.148) | copy-start | bytes 1966084
  113.6 41.4 %copy-start.49 = (bf16[640,512]{1,0:T(8,128)(2,1)}, bf16[640,512]{1,0:T(8,128)(2,1)S(1)}, u32[]{:S(2)}) copy-start(bf16[640,512]{1,0:T(8,128)(2,1)S(1)} %get-tuple-element.147) | copy-start | bytes 1966084
  113.6 44.0 %copy-start.51 = (bf16[640,512]{1,0:T(8,128)(2,1)}, bf16[640,512]{1,0:T(8,128)(2,1)S(1)}, u32[]{:S(2)}) copy-start(bf16[640,512]{1,0:T(8,128)(2,1)S(1)} %get-tuple-element.146) | copy-start | bytes 1966084
  115.0 39.1 %copy-start.56 = (f32[32,8,128]{2,1,0:T(8,128)S(1)}, f32[32,8,128]{2,1,0:T(8,128)}, u32[]{:S(2)}) copy-start(f32[32,8,128]{2,1,0:T(8,128)} %get-tuple-element.82) | copy-start | bytes 393220
  154.0 3.9 copy-start.14
  159.4 3.8 copy-start.38
  159.8 3.4 copy-start.7
  229.7 7.0 %copy-start.35 = (bf16[640,2048]{1,0:T(8,128)(2,1)S(1)}, bf16[640,2048]{1,0:T(8,128)(2,1)}, u32[]{:S(2)}) copy-start(bf16[640,2048]{1,0:T(8,128)(2,1)} %copy-done.34) | copy-start | bytes 7864324
  229.7 14.2 %collective-permute-start.4 = (bf16[640,1408]{1,0:T(8,128)(2,1)S(1)}, bf16[640,1408]{1,0:T(8,128)(2,1)}, u32[]{:S(2)}, u32[]{:S(2)}) collective-permute-start(bf16[640,1408]{1,0:T(8,128)(2,1)S(1)} %fusion.5.b.refs_4_), channel_id=1, source_target_pairs={{0,1},{1,0},{2,3},{3,2},{4,5},{5,4},{6,7},{7,6},{8,9},{9,8},{10,11... | collective-permute-start | bytes 5406728 | tf_op jit(solution)/shard_map/ppermute | solution.py:918
  233.9 4.2 copy-start.8
  236.4 7.5 %collective-permute-start.3 = (bf16[640,1024]{1,0:T(8,128)(2,1)}, bf16[640,1024]{1,0:T(8,128)(2,1)}, u32[]{:S(2)}, u32[]{:S(2)}) collective-permute-start(bf16[640,1024]{1,0:T(8,128)(2,1)} %constant_dynamic-slice_fusion.3), channel_id=1, source_target_pairs={{0,1},{1,0},{2,3},{3,2},{4,5},{5,4},{6,7},{7,6},{8,9},{9,8},{10,11... | collective-permute-start | bytes 3932168 | tf_op jit(solution)/shard_map/ppermute | solution.py:918
  237.9 15.2 %collective-permute-start.5 = (bf16[640,1024]{1,0:T(8,128)(2,1)}, bf16[640,1024]{1,0:T(8,128)(2,1)}, u32[]{:S(2)}, u32[]{:S(2)}) collective-permute-start(bf16[640,1024]{1,0:T(8,128)(2,1)} %constant_dynamic-slice_fusion.2), channel_id=1, source_target_pairs={{0,1},{1,0},{2,3},{3,2},{4,5},{5,4},{6,7},{7,6},{8,9},{9,8},{10,11... | collective-permute-start | bytes 3932168 | tf_op jit(solution)/shard_map/ppermute | solution.py:918
  243.6 9.6 %collective-permute-start.6 = (bf16[640,256]{1,0:T(8,128)(2,1)}, bf16[640,256]{1,0:T(8,128)(2,1)}, u32[]{:S(2)}, u32[]{:S(2)}) collective-permute-start(bf16[640,256]{1,0:T(8,128)(2,1)} %constant_dynamic-slice_fusion.1), channel_id=1, source_target_pairs={{0,1},{1,0},{2,3},{3,2},{4,5},{5,4},{6,7},{7,6},{8,9},{9,8},{10,11... | collective-permute-start | bytes 983048 | tf_op jit(solution)/shard_map/ppermute | solution.py:918
  252.9 189.7 %reduce-scatter.6.cloned.1.call-start = ((), (), s32[]{:S(2)}) async-start(), calls=%async_computation.6 | async-start | bytes 7208960 | tf_op jit(solution)/shard_map/reduce_scatter | solution.py:913
  286.7 12.1 %copy-start.36 = (bf16[640,2048]{1,0:T(8,128)(2,1)S(1)}, bf16[640,2048]{1,0:T(8,128)(2,1)}, u32[]{:S(2)}) copy-start(bf16[640,2048]{1,0:T(8,128)(2,1)} %copy-done.34) | copy-start | bytes 7864324
  286.7 12.1 %collective-permute-start.7 = (bf16[640,2816]{1,0:T(8,128)(2,1)S(1)}, bf16[640,2816]{1,0:T(8,128)(2,1)S(1)}, u32[]{:S(2)}, u32[]{:S(2)}) collective-permute-start(bf16[640,2816]{1,0:T(8,128)(2,1)S(1)} %pad_maximum_fusion.b), channel_id=1, source_target_pairs={{0,1},{1,0},{2,3},{3,2},{4,5},{5,4},{6,7},{7,6},{8,9},{9,8},{10,11... | collective-permute-start | bytes 10813448 | tf_op jit(solution)/shard_map/ppermute | solution.py:918
  311.5 212.9 %reduce-scatter.8.cloned.1.call-start = ((), (), s32[]{:S(2)}) async-start(), calls=%async_computation.7 | async-start | bytes 5242880 | tf_op jit(solution)/shard_map/reduce_scatter | solution.py:913
  367.4 15.6 %collective-permute-start.8 = (bf16[640,2048]{1,0:T(8,128)(2,1)}, bf16[640,2048]{1,0:T(8,128)(2,1)}, u32[]{:S(2)}, u32[]{:S(2)}) collective-permute-start(bf16[640,2048]{1,0:T(8,128)(2,1)} %get-tuple-element.103.b), channel_id=1, source_target_pairs={{0,1},{1,0},{2,3},{3,2},{4,5},{5,4},{6,7},{7,6},{8,9},{9,8},{10,11... | collective-permute-start | bytes 7864328 | tf_op jit(solution)/shard_map/ppermute | solution.py:918
  367.4 45.4 %collective-permute-start.10 = (bf16[160,2048]{1,0:T(8,128)(2,1)}, bf16[160,2048]{1,0:T(8,128)(2,1)S(1)}, u32[]{:S(2)}, u32[]{:S(2)}) collective-permute-start(bf16[160,2048]{1,0:T(8,128)(2,1)} %get-tuple-element.109), channel_id=1, source_target_pairs={{0,4},{1,5},{2,6},{3,7},{4,0},{5,1},{6,2},{7,3},{8,12},{9,13},{10,... | collective-permute-start | bytes 1966088 | tf_op jit(solution)/shard_map/ppermute | solution.py:939
  368.9 43.9 %collective-permute-start.11 = (bf16[160,2048]{1,0:T(8,128)(2,1)}, bf16[160,2048]{1,0:T(8,128)(2,1)S(1)}, u32[]{:S(2)}, u32[]{:S(2)}) collective-permute-start(bf16[160,2048]{1,0:T(8,128)(2,1)} %get-tuple-element.110), channel_id=1, source_target_pairs={{0,6},{1,7},{2,4},{3,5},{4,2},{5,3},{6,0},{7,1},{8,14},{9,15},{10,... | collective-permute-start | bytes 1966088 | tf_op jit(solution)/shard_map/ppermute | solution.py:939
  370.4 42.4 %collective-permute-start.9 = (bf16[160,2048]{1,0:T(8,128)(2,1)}, bf16[160,2048]{1,0:T(8,128)(2,1)}, u32[]{:S(2)}, u32[]{:S(2)}) collective-permute-start(bf16[160,2048]{1,0:T(8,128)(2,1)} %get-tuple-element.108), channel_id=1, source_target_pairs={{0,2},{1,3},{2,0},{3,1},{4,6},{5,7},{6,4},{7,5},{8,10},{9,11},{10,... | collective-permute-start | bytes 1966088 | tf_op jit(solution)/shard_map/ppermute | solution.py:939
  370.9 4.0 copy-start.39
  415.6 13.8 %copy-start.16 = (bf16[640,1536]{1,0:T(8,128)(2,1)}, bf16[640,1536]{1,0:T(8,128)(2,1)S(1)}, u32[]{:S(2)}) copy-start(bf16[640,1536]{1,0:T(8,128)(2,1)S(1)} %pad_maximum_fusion.1.b) | copy-start | bytes 5898244
  415.6 13.8 %collective-permute-start.13 = (bf16[640,1536]{1,0:T(8,128)(2,1)S(1)}, bf16[640,1536]{1,0:T(8,128)(2,1)S(1)}, u32[]{:S(2)}, u32[]{:S(2)}) collective-permute-start(bf16[640,1536]{1,0:T(8,128)(2,1)S(1)} %pad_maximum_fusion.1.b), channel_id=1, source_target_pairs={{0,1},{1,0},{2,3},{3,2},{4,5},{5,4},{6,7},{7,6},{8,9},{9,8},{10,11... | collective-permute-start | bytes 5898248 | tf_op jit(solution)/shard_map/ppermute | solution.py:918
  418.0 11.4 %collective-permute-start.12 = (bf16[640,1024]{1,0:T(8,128)(2,1)S(1)}, bf16[640,1024]{1,0:T(8,128)(2,1)S(1)}, u32[]{:S(2)}, u32[]{:S(2)}) collective-permute-start(bf16[640,1024]{1,0:T(8,128)(2,1)S(1)} %constant_dynamic-slice_fusion), channel_id=1, source_target_pairs={{0,1},{1,0},{2,3},{3,2},{4,5},{5,4},{6,7},{7,6},{8,9},{9,8},{10,11... | collective-permute-start | bytes 3932168 | tf_op jit(solution)/shard_map/ppermute | solution.py:918
  445.4 7.8 %copy-start.5 = (bf16[160,2048]{1,0:T(8,128)(2,1)S(1)}, bf16[160,2048]{1,0:T(8,128)(2,1)}, u32[]{:S(2)}) copy-start(bf16[160,2048]{1,0:T(8,128)(2,1)} %copy-done.4) | copy-start | bytes 1966084
  445.4 7.8 %copy-start.19 = (f32[160,2048]{1,0:T(8,128)S(1)}, f32[160,2048]{1,0:T(8,128)}, u32[]{:S(2)}) copy-start(f32[160,2048]{1,0:T(8,128)} %copy-done.18) | copy-start | bytes 3932164
  445.4 7.8 %copy-start.25 = (bf16[160,2048]{1,0:T(8,128)(2,1)S(1)}, bf16[160,2048]{1,0:T(8,128)(2,1)}, u32[]{:S(2)}) copy-start(bf16[160,2048]{1,0:T(8,128)(2,1)} %copy-done.24) | copy-start | bytes 1966084
  445.4 7.8 %copy-start.27 = (bf16[160,2048]{1,0:T(8,128)(2,1)S(1)}, bf16[160,2048]{1,0:T(8,128)(2,1)}, u32[]{:S(2)}) copy-start(bf16[160,2048]{1,0:T(8,128)(2,1)} %copy-done.26) | copy-start | bytes 1966084
  445.4 7.8 %copy-start.29 = (bf16[160,2048]{1,0:T(8,128)(2,1)S(1)}, bf16[160,2048]{1,0:T(8,128)(2,1)}, u32[]{:S(2)}) copy-start(bf16[160,2048]{1,0:T(8,128)(2,1)} %copy-done.28) | copy-start | bytes 1966084
  453.2 32.4 %copy-start.17 = (bf16[256,2816]{1,0:T(8,128)(2,1)S(1)}, bf16[256,2816]{1,0:T(8,128)(2,1)}, u32[]{:S(2)}) copy-start(bf16[256,2816]{1,0:T(8,128)(2,1)} %reduce-scatter.6.cloned.1.call-done.refs_0_) | copy-start | bytes 4325380
  484.6 25.7 %copy-start.21 = (f32[160,2048]{1,0:T(8,128)S(1)}, f32[160,2048]{1,0:T(8,128)}, u32[]{:S(2)}) copy-start(f32[160,2048]{1,0:T(8,128)} %copy-done.20) | copy-start | bytes 3932164
  (31 other events, 51.4 us)
Sparse Core Ops, SparseCore 0:
  96.8 110.1 all-gather.2
  208.6 67.2 all-gather.4
  278.2 54.8 reduce-scatter.3
  335.2 107.4 reduce-scatter.5
  444.8 79.6 reduce-scatter.7

commit v5 on v4

--- a/solution.py
+++ b/solution.py
@@ -83,7 +83,23 @@
             return pl.ds(pl.multiple_of(((core * planes + plane) * HEADS + chip) * strip, strip), strip)
 
         def unit(plane, k):
-            return line.at[row(plane, chips[k][1])]
+            return line.at[row(plane, chips[k][1]), pl.ds(0, 3 * part)]
+
+        def stack(plane):
+            at = pl.multiple_of((core * planes + plane) * HEADS * strip, strip)
+            return line.at[pl.ds(at, HEADS * strip), pl.ds(3 * part, part)]
+
+        def stack_up(d):
+            n = hops * HEADS + d - 1
+            return remote(stack(z - d + 1), stack(z - d + 1), u_send.at[n], u_recv.at[n], me + PLANE)
+
+        def stack_down(d):
+            n = hops * HEADS + d - 1
+            return remote(stack(z + d - 1), stack(z + d - 1), d_send.at[n], d_recv.at[n], me - PLANE)
+
+        def stack_across(plane):
+            n = planes * HEADS + plane
+            return remote(stack(plane), stack(plane), s_send.at[n], s_recv.at[n], sibling)
 
         def up(d, k):
             n = (d - 1) * HEADS + k
@@ -128,6 +144,16 @@
         turned = reorder(o_in[...], planes, False)
         for k in range(HEADS):
             line[row(z, k), pl.ds(3 * part, part)] = turned[:, k * part : (k + 1) * part]
+
+        @pl.when(z + 1 < planes)
+        def _():
+            stack_up(1).start()
+
+        @pl.when(z >= 1)
+        def _():
+            stack_down(1).start()
+
+        stack_across(z).start()
         for copy in own:
             copy.wait()
         pass_on(0)
@@ -219,6 +245,27 @@
             copy.wait()
         begin(sides)
         for d in range(1, planes):
+
+            @pl.when(z - d >= 0)
+            def _(d=d):
+                stack_up(d).wait_recv()
+
+                @pl.when(z + 1 < planes)
+                def _():
+                    stack_up(d + 1).start()
+
+                stack_across(z - d).start()
+
+            @pl.when(z + d < planes)
+            def _(d=d):
+                stack_down(d).wait_recv()
+
+                @pl.when(z >= 1)
+                def _():
+                    stack_down(d + 1).start()
+
+                stack_across(z + d).start()
+
             for k in range(HEADS):
 
                 @pl.when(z - d >= 0)
@@ -249,23 +296,27 @@
         for copy in begun[len(shares) :]:
             copy.wait()
         for d in range(1, planes):
-            for k in range(HEADS):
-
-                @pl.when((z - d + 1 >= 0) & (z + 1 < planes))
-                def _(d=d, k=k):
+
+            @pl.when((z - d + 1 >= 0) & (z + 1 < planes))
+            def _(d=d):
+                stack_up(d).wait_send()
+                for k in range(HEADS):
                     up(d, k).wait_send()
 
-                @pl.when((z + d - 1 < planes) & (z >= 1))
-                def _(d=d, k=k):
+            @pl.when((z + d - 1 < planes) & (z >= 1))
+            def _(d=d):
+                stack_down(d).wait_send()
+                for k in range(HEADS):
                     down(d, k).wait_send()
 
         for plane in range(planes):
+            stack_across(plane).wait()
             for k in range(HEADS):
                 across(plane, k).wait()
 
     sides = count + 4 + 12
     vmem = pl.BlockSpec(memory_space=pltpu.VMEM)
-    sizes = (6, 7, 6, 3, 9, 9, sides, sides) + (hops * HEADS,) * 4 + (planes * HEADS,) * 2
+    sizes = (6, 7, 6, 3, 9, 9, sides, sides) + (hops * (HEADS + 1),) * 4 + (planes * (HEADS + 1),) * 2
     shares = jax.ShapeDtypeStruct((count, 8, 128), f32)
     logits = jax.ShapeDtypeStruct((HEADS, tokens_rows, SLOTS), codes.dtype)
     return pl.pallas_call(
@@ -306,7 +357,7 @@
         outs, refs = refs[:pieces], refs[pieces:]
         extra, refs = (refs[0], refs[1:]) if own_rows else (None, refs)
         gain_out, refs = (refs[0], refs[1:]) if shared else (None, refs)
-        landed, send, recv, gain_in, gain_send, gain_recv = refs
+        send, recv, gain_in, gain_send, gain_recv = refs
         me = lax.axis_index("seq")
         h = chip_of(me)
         targets = [chip_on(me, h, k) for k in (3, 1, 2)]
@@ -324,7 +375,7 @@
             )
 
         def place(j):
-            return landed.at[j, h] if own_rows else columns_at(outs[j], h, part)
+            return columns_at(outs[j], h, part)
 
         copies = []
         for k, (device, other) in enumerate(targets):
@@ -347,13 +398,9 @@
             gain_in[me] = shares[me]
         if own_rows:
             blocks = [src[pl.ds(k * rows, rows), pl.ds(pieces * part, part)] for k in range(HEADS)]
-            extra[...] = reorder(jnp.concatenate(blocks, axis=1).astype(f32), planes, True)
+            extra[...] = reorder(jnp.concatenate(blocks, axis=1), planes, True)
         for copy in copies:
             copy.wait()
-        if own_rows:
-            for j in range(pieces):
-                for k in range(HEADS):
-                    outs[j][:, pl.ds(k * part, part)] = landed[j, k].astype(f32)
         if shared:
             total = gain_in[0]
             for k in range(1, count):
@@ -361,8 +408,7 @@
             gain_out[...] = total
 
     vmem = pl.BlockSpec(memory_space=pltpu.VMEM)
-    kind = f32 if own_rows else bf16
-    shapes = [jax.ShapeDtypeStruct((rows, HEADS * part), kind)] * (pieces + int(own_rows))
+    shapes = [jax.ShapeDtypeStruct((rows, HEADS * part), bf16)] * (pieces + int(own_rows))
     shapes += [jax.ShapeDtypeStruct((8, 128), f32)] * int(shared)
     return pl.pallas_call(
         kernel,
@@ -370,7 +416,6 @@
         in_specs=[vmem] * (1 + int(shared)),
         out_specs=[vmem] * len(shapes),
         scratch_shapes=[
-            pltpu.VMEM((pieces, HEADS, rows, part) if own_rows else (1, 1, 16, 128), x.dtype),
             pltpu.SemaphoreType.DMA((4 * pieces,)),
             pltpu.SemaphoreType.DMA((3 * pieces,)),
             pltpu.VMEM((count if shared else 1, 8, 128), f32),
@@ -1145,6 +1190,9 @@
     query_grad, key_grad, value_grad, output_grad = return_columns(
         10, mixer_sums, 3, head_size, planes, None, True
     )
+    query_grad, key_grad, value_grad, output_grad = finished(
+        [query_grad, key_grad, value_grad, output_grad], []
+    )
     gain_sums = gain_sums[:3, :strip]
     return (
         block_out,

time: 554 us -> 550 us (level)
    unnamed x127 -> x123, local copies, waits for them, and re-layouts: 28 us -> 24.9 us
  transfers between devices with their start and end apart: 19 -> 19, of which waited for: 3 -> 3; matrix products, arithmetic and copies ran while one was open for 17% -> 18% of each run, Pallas kernels for 49% -> 49%
where the time goes in v5:
time: 550 us; the launch traced here: 543 us
  Pallas kernels  366 us (67%)
  matrix products  73.2 us (13%)
  waiting for transfers between devices  38.3 us (7%)
  local copies, waits for them, and re-layouts  36.4 us (7%)
  between operations  15.5 us (3%)
  starting transfers between devices  8.75 us (2%)
    pallas_call x3, Pallas kernels, plane_stage(): pl.pallas_call(kernel, out_shape=shapes, in_specs=[vmem] * (has + len(blo...  127 us
    pallas_call x1, Pallas kernels, opening(): pl.pallas_call(kernel, out_shape=[shares, logits, jax.ShapeDtypeStruct((c...  86.8 us
    pallas_call x2, Pallas kernels, carry_states(): pl.pallas_call(kernel, out_shape=[jax.ShapeDtypeStruct(keys.shape, f32)]...  63.8 us
    pallas_call x3, Pallas kernels, return_columns(): pl.pallas_call(kernel, out_shape=shapes, in_specs=[vmem] * (1 + int(share...  48.2 us
    pallas_call x4, Pallas kernels, chip_sum(): pl.pallas_call(kernel, out_shape=jax.ShapeDtypeStruct((half, columns + mo...  30.7 us
    dot_general x9, matrix products, plain(): return jnp.einsum(form, left, right, preferred_element_type=f32)  25.7 us
    unnamed x123, local copies, waits for them, and re-layouts  24.9 us
    all_gather x2, waiting for transfers between devices, gather_line(): return lax.all_gather(x, 'seq', axis=0, tiled=True, axis_index_groups=lines)  23.4 us
  transfers between devices with their start and end apart: 19, of which 3 were waited for; matrix products, arithmetic and copies ran while one was open for 18% of the time, Pallas kernels for 49%

profile of v5, /device:TPU:0, one launch (start us, length us, event | category | flops | bytes accessed | tf_op | source)
XLA Modules:
  0.0 543.0 jit_solution(12848004346592853065)
XLA Ops:
  7.2 86.8 %shard_map.229 = (f32[32,8,128]{2,1,0:T(8,128)}, s32[4,160,64]{2,1,0:T(8,128)}, bf16[2048,2048]{1,0:T(8,128)(2,1)}, bf16[256,2816]{1,0:T(8,128)(2,1)}, bf16[256,...) custom-call(bf16[1,64]{1,0:T(2,128)(2,1)} %bitcast.138, bf16[1,64]{1,0:T(2,128)(2,1)} %bitcast.139, bf16[1,64]{1,0:T(2,128)(2,1)} %bitcast.140, ...), custom_call_target="tpu_custom_call" | custom-call | bytes 289000000 | tf_op jit(solution)/shard_map/pallas_call | solution.py:322
  94.2 1.7 shard_map.231
  97.2 2.3 collective-permute-start.2
  101.4 8.5 %fusion.6 = bf16[640,1536]{1,0:T(8,128)(2,1)S(1)} fusion(bf16[640,2048]{1,0:T(8,128)(2,1)} %get-tuple-element.81.a, bf16[2048,2048]{1,0:T(8,128)(2,1)} %get-tuple-element.83.refs_0_), kind=kOutput, calls=%fused_computation.11 | convolution fusion | flops 4027514880 | bytes 10878976 | tf_op jit(solution)/shard_map/dot_general | solution.py:1037
  112.1 38.4 %shard_map.230 = (f32[4,64,512]{2,1,0:T(8,128)S(1)}, f32[4,64,512]{2,1,0:T(8,128)S(1)}, bf16[512,2048]{1,0:T(8,128)(2,1)S(1)}) custom-call(f32[4,64,512]{2,1,0:T(8,128)S(1)} %fusion.29.k_in, f32[4,64,512]{2,1,0:T(8,128)S(1)} %fusion.28.v_in, f32[4,64,128]{2,1,0:T(8,128)S(1)} %broadcast_in_dim.89.g_in, bf16[2048,2048]{1,0:T(8,128)(2,1)S(1)} %bitcast.110), custom_call_target="tpu_custom_call" | custom-call | bytes 74800000 | tf_op jit(solution)/shard_map/pallas_call | solution.py:898
  154.5 1.4 multiply_reduce_fusion.2
  156.4 3.3 convolution_convert_fusion.1.refs_0_
  159.8 46.6 %shard_map.232 = (f32[160,2048]{1,0:T(8,128)S(1)}, bf16[640,2048]{1,0:T(8,128)(2,1)S(1)}) custom-call(bf16[640,2048]{1,0:T(8,128)(2,1)S(1)} %convolution_convert_fusion.1.refs_0_, bf16[160,2048]{1,0:T(8,128)(2,1)S(1)} %get-tuple-element.88.refs_1_, f32[1,2048]{1,0:T(1,128)S(1)} %broadcast_in_dim_reshape.6.refs_2_.refs_3_), custom_call_target="tpu_custom_call" | custom-call | bytes 170000000 | tf_op jit(solution)/shard_map/pallas_call | solution.py:608
  206.4 1.5 copy-done.34
  208.8 2.0 constant_dynamic-update-slice_fusion.2
  210.8 11.9 %fusion.55 = f32[640,2816]{1,0:T(8,128)S(1)} fusion(bf16[640,2048]{1,0:T(8,128)(2,1)} %copy-done.34, bf16[2048,2816]{1,0:T(8,128)(2,1)} %all-gather.3.cloned.1.call-done), kind=kOutput, calls=%fused_computation.115 | convolution fusion | flops 7381975040 | bytes 21364736 | tf_op jit(solution)/shard_map/dot_general | solution.py:1077
  223.8 1.9 copy-done.46
  225.7 2.2 constant_dynamic-update-slice_fusion.1
  227.9 2.0 constant_dynamic-update-slice_fusion.a
  229.9 2.6 constant_dynamic-slice_fusion.3
  232.8 1.2 constant_dynamic-slice_fusion.2
  234.1 2.9 shard_map.234.a
  237.9 1.7 constant_dynamic-slice_fusion.1
  240.0 7.4 %shard_map.233 = bf16[1024,1408]{1,0:T(8,128)(2,1)S(1)} custom-call(s32[1]{0:T(128)} %bitcast.which, bf16[640,2048]{1,0:T(8,128)(2,1)} %constant_dynamic-update-slice_fusion.a, bf16[640,1408]{1,0:T(8,128)(2,1)S(1)} %fusion.5.b.refs_4_, bf16[640,1024]{1,0:T(8,128)(2,1)} %collective-permute-done.3.c, bf16[640,1408]{1,0:T(8,128)(2,1)} %collective-permute-done.4.d), custom_call_target="tpu_custom_call" | custom-call | flops 3690987520 | bytes 9109504 | tf_op jit(solution)/shard_map/pallas_call | solution.py:652
  247.4 1.5 copy-done.3
  249.2 23.4 %all-gather.5.cloned.1.call-done.refs_5_ = bf16[2048,1408]{1,0:T(8,128)(2,1)} async-done(((bf16[256,1408]{1,0:T(8,128)(2,1)}), bf16[2048,1408]{1,0:T(8,128)(2,1)}) %all-gather.5.cloned.1.call-update) | async-done | bytes 5767184 | tf_op jit(solution)/shard_map/all_gather | solution.py:953
  272.6 10.6 %multiply_convert_fusion.1 = (bf16[640,1408]{1,0:T(8,128)(2,1)S(1)}, bf16[640,1408]{1,0:T(8,128)(2,1)S(1)}) fusion(f32[640,2816]{1,0:T(8,128)} %copy-done.46, bf16[640,2048]{1,0:T(8,128)(2,1)} %constant_dynamic-update-slice_fusion.a, bf16[2048,1408]{1,0:T(8,128)(2,1)} %all-gather.5.cloned.1.call-done.refs_5_), kind=kOutput, calls=%fused_computation.9 | convolution fusion | flops 3702702080 | bytes 19202048 | tf_op jit(solution)/shard_map/dot_general | solution.py:1093
  283.7 11.8 %convolution_convert_fusion.refs_0_ = bf16[640,2048]{1,0:T(8,128)(2,1)} fusion(bf16[2048,2816]{1,0:T(8,128)(2,1)} %all-gather.3.cloned.1.call-done, bf16[640,1408]{1,0:T(8,128)(2,1)S(1)} %get-tuple-element.153, bf16[640,1408]{1,0:T(8,128)(2,1)S(1)} %get-tuple-element.152), kind=kOutput, calls=%fused_computation.13 | convolution fusion | flops 7390494720 | bytes 17760256 | tf_op jit(solution)/shard_map/tf,df->td/dot_general | solution.py:922
  295.5 12.7 %shard_map.235 = bf16[1024,2816]{1,0:T(8,128)(2,1)} custom-call(s32[1]{0:T(128)} %bitcast.which, bf16[640,2048]{1,0:T(8,128)(2,1)S(1)} %copy-done.36, bf16[640,2816]{1,0:T(8,128)(2,1)S(1)} %pad_maximum_fusion.b, bf16[640,1024]{1,0:T(8,128)(2,1)} %collective-permute-done.5.c, bf16[640,2816]{1,0:T(8,128)(2,1)S(1)} %collective-permute-done.7.d), custom_call_target="tpu_custom_call" | custom-call | flops 7381975040 | bytes 15597568 | tf_op jit(solution)/shard_map/pallas_call | solution.py:652
  308.3 1.7 copy-done.9
  310.1 1.1 copy-done.11
  311.2 51.1 %shard_map.236 = (f32[160,2048]{1,0:T(8,128)S(1)}, f32[8,2048]{1,0:T(8,128)S(1)}, bf16[640,2048]{1,0:T(8,128)(2,1)}, bf16[160,2048]{1,0:T(8,128)(2,1)S(1)}, bf16...) custom-call(bf16[640,2048]{1,0:T(8,128)(2,1)S(1)} %copy-done.9, ...), custom_call_target="tpu_custom_call" | custom-call | bytes 170000000 | tf_op jit(solution)/shard_map/pallas_call | solution.py:608
  364.2 1.5 collective-permute-start.10
  365.7 1.5 collective-permute-start.11
  367.7 4.0 fusion.56
  378.5 1.2 fusion.14
  379.7 4.5 shard_map.237
  384.2 25.3 %shard_map.238 = (f32[4,64,512]{2,1,0:T(8,128)S(1)}, f32[4,64,512]{2,1,0:T(8,128)S(1)}, bf16[1024,512]{1,0:T(8,128)(2,1)S(1)}) custom-call(f32[4,64,512]{2,1,0:T(8,128)S(1)} %fusion.22.k_in, f32[4,64,512]{2,1,0:T(8,128)S(1)} %fusion.25.v_in, f32[4,64,128]{2,1,0:T(8,128)S(1)} %broadcast_in_dim.89.g_in, bf16[1,4,64,2048]{3,2,1,0:T(8,128)(2,1)S(1)} %bitcast.111), custom_call_target="tpu_custom_call" | custom-call | bytes 74800000 | tf_op jit(solution)/shard_map/pallas_call | solution.py:898
  409.6 1.3 fusion.12
  410.9 1.3 fusion.13
  412.4 2.2 copy-done.33
  414.8 11.4 %shard_map.240.refs_0_ = bf16[64,5632]{1,0:T(8,128)(2,1)S(1)} custom-call(bf16[256,1408]{1,0:T(8,128)(2,1)S(1)} %copy-done.23), custom_call_target="tpu_custom_call" | custom-call | bytes 47600000 | tf_op jit(solution)/shard_map/pallas_call | solution.py:413
  426.2 6.1 %shard_map.239 = bf16[1024,2048]{1,0:T(8,128)(2,1)S(1)} custom-call(s32[1]{0:T(128)} %bitcast.which, bf16[640,2048]{1,0:T(8,128)(2,1)S(1)} %copy-done.33, bf16[640,1536]{1,0:T(8,128)(2,1)S(1)} %pad_maximum_fusion.1.b, bf16[640,1024]{1,0:T(8,128)(2,1)S(1)} %collective-permute-done.12.c, bf16[640,1536]{1,0:T(8,128)(2,1)S(1)} %collective-permute-done.13.d, ...), custom_call_target="tpu_custom_call" | custom-call | flops 4026531840 | bytes 9699328 | tf_op jit(solution)/shard_map/pallas_call | solution.py:652
  432.3 2.0 copy-done
  434.3 5.1 reduce-scatter.6.cloned.1.call-done.refs_0_
  442.2 7.8 %fusion.9.refs_0_ = bf16[640,2048]{1,0:T(8,128)(2,1)S(1)} fusion(bf16[640,1536]{1,0:T(8,128)(2,1)} %copy-done.16, bf16[2048,2048]{1,0:T(8,128)(2,1)} %get-tuple-element.83.refs_0_), kind=kOutput, calls=%fused_computation.12 | convolution fusion | flops 4027842560 | bytes 10878976 | tf_op jit(solution)/shard_map/tf,df->td/dot_general | solution.py:922
  450.0 29.5 %shard_map.241 = (f32[160,2048]{1,0:T(8,128)S(1)}, f32[8,2048]{1,0:T(8,128)S(1)}, bf16[160,2048]{1,0:T(8,128)(2,1)S(1)}) custom-call(bf16[640,2048]{1,0:T(8,128)(2,1)S(1)} %fusion.9.refs_0_, bf16[160,2048]{1,0:T(8,128)(2,1)S(1)} %copy-done.5, f32[160,2048]{1,0:T(8,128)S(1)} %copy-done.19, f32[1,2048]{1,0:T(1,128)S(1)} %broadcast_in_dim_reshape.7.refs_3_, ...), custom_call_target="tpu_custom_call" | custom-call | bytes 85000000 | tf_op jit(solution)/shard_map/pallas_call | solution.py:608
  482.5 24.8 %shard_map.242 = (bf16[64,5632]{1,0:T(8,128)(2,1)S(1)}, bf16[64,5632]{1,0:T(8,128)(2,1)S(1)}, f32[8,128]{1,0:T(8,128)S(1)}) custom-call(bf16[256,2816]{1,0:T(8,128)(2,1)S(1)} %copy-done.17, f32[32,8,128]{2,1,0:T(8,128)S(1)} %pad.4.refs_1_), custom_call_target="tpu_custom_call" | custom-call | bytes 47600000 | tf_op jit(solution)/shard_map/pallas_call | solution.py:413
  508.3 2.9 shard_map.243
  511.7 9.6 %reduce-scatter.8.cloned.1.call-done.refs_0_ = bf16[256,2048]{1,0:T(8,128)(2,1)} async-done(((bf16[1024,2048]{1,0:T(8,128)(2,1)}), bf16[256,2048]{1,0:T(8,128)(2,1)}) %reduce-scatter.8.cloned.1.call-update) | async-done | bytes 1048592 | tf_op jit(solution)/shard_map/reduce_scatter | solution.py:958
  521.4 1.2 copy-done.22
  522.6 12.1 %shard_map.244 = (bf16[64,2048]{1,0:T(8,128)(2,1)S(1)}, bf16[64,2048]{1,0:T(8,128)(2,1)S(1)}, bf16[64,2048]{1,0:T(8,128)(2,1)S(1)}, bf16[64,2048]{1,0:T(8,128)(2,1)S(1)}) custom-call(bf16[256,2048]{1,0:T(8,128)(2,1)S(1)} %copy-done.22), custom_call_target="tpu_custom_call" | custom-call | bytes 47600000 | tf_op jit(solution)/shard_map/pallas_call | solution.py:413
  534.7 1.4 shard_map.245
  (217 shorter events, 30.7 us)
Async XLA Ops:
  7.2 203.6 %all-gather.3.cloned.1.call-start = ((), (), s32[]{:S(2)}) async-start(), calls=%async_computation.3 | async-start | bytes 12976128 | tf_op jit(solution)/shard_map/all_gather | solution.py:953
  7.2 87.0 %copy-start.6 = (bf16[160,2048]{1,0:T(8,128)(2,1)S(1)}, bf16[160,2048]{1,0:T(8,128)(2,1)}, u32[]{:S(2)}) copy-start(bf16[160,2048]{1,0:T(8,128)(2,1)} %refs_0_.1) | copy-start | bytes 1966084
  7.2 87.0 %copy-start.32 = (bf16[160,2048]{1,0:T(8,128)(2,1)S(1)}, bf16[160,2048]{1,0:T(8,128)(2,1)}, u32[]{:S(2)}) copy-start(bf16[160,2048]{1,0:T(8,128)(2,1)} %refs_1_.1) | copy-start | bytes 1966084
  94.1 5.6 %copy-start.57 = (s32[4]{0:T(128)S(1)}, s32[4]{0:T(128)}, u32[]{:S(2)}) copy-start(s32[4]{0:T(128)} %param.17) | copy-start | bytes 52
  94.1 6.2 %copy-start.55 = (s32[4,160,64]{2,1,0:T(8,128)S(1)}, s32[4,160,64]{2,1,0:T(8,128)}, u32[]{:S(2)}) copy-start(s32[4,160,64]{2,1,0:T(8,128)} %get-tuple-element.82) | copy-start | bytes 491524
  94.1 178.5 %all-gather.5.cloned.1.call-start = ((), (), s32[]{:S(2)}) async-start(), calls=%async_computation.4 | async-start | bytes 6488064 | tf_op jit(solution)/shard_map/all_gather | solution.py:953
  95.9 63.8 %copy-start.4 = (bf16[160,2048]{1,0:T(8,128)(2,1)}, bf16[160,2048]{1,0:T(8,128)(2,1)S(1)}, u32[]{:S(2)}) copy-start(bf16[160,2048]{1,0:T(8,128)(2,1)S(1)} %get-tuple-element.88.refs_1_) | copy-start | bytes 1966084
  95.9 111.9 %copy-start.10 = (bf16[160,2048]{1,0:T(8,128)(2,1)}, bf16[160,2048]{1,0:T(8,128)(2,1)S(1)}, u32[]{:S(2)}) copy-start(bf16[160,2048]{1,0:T(8,128)(2,1)S(1)} %get-tuple-element.92.refs_2_) | copy-start | bytes 1966084
  96.0 111.9 %collective-permute-start = (bf16[160,2048]{1,0:T(8,128)(2,1)S(1)}, bf16[160,2048]{1,0:T(8,128)(2,1)}, u32[]{:S(2)}, u32[]{:S(2)}) collective-permute-start(bf16[160,2048]{1,0:T(8,128)(2,1)S(1)} %get-tuple-element.92.refs_2_), channel_id=1, source_target_pairs={{0,2},{1,3},{2,0},{3,1},{4,6},{5,7},{6,4},{7,5},{8,10},{9,11},{10,... | collective-permute-start | bytes 1966088 | tf_op jit(solution)/shard_map/ppermute | solution.py:984
  96.6 111.2 %collective-permute-start.1 = (bf16[160,2048]{1,0:T(8,128)(2,1)S(1)}, bf16[160,2048]{1,0:T(8,128)(2,1)}, u32[]{:S(2)}, u32[]{:S(2)}) collective-permute-start(bf16[160,2048]{1,0:T(8,128)(2,1)S(1)} %get-tuple-element.92.refs_2_), channel_id=1, source_target_pairs={{0,4},{1,5},{2,6},{3,7},{4,0},{5,1},{6,2},{7,3},{8,12},{9,13},{10,... | collective-permute-start | bytes 1966088 | tf_op jit(solution)/shard_map/ppermute | solution.py:984
  97.2 110.7 %collective-permute-start.2 = (bf16[160,2048]{1,0:T(8,128)(2,1)S(1)}, bf16[160,2048]{1,0:T(8,128)(2,1)}, u32[]{:S(2)}, u32[]{:S(2)}) collective-permute-start(bf16[160,2048]{1,0:T(8,128)(2,1)S(1)} %get-tuple-element.92.refs_2_), channel_id=1, source_target_pairs={{0,6},{1,7},{2,4},{3,5},{4,2},{5,3},{6,0},{7,1},{8,14},{9,15},{10,... | collective-permute-start | bytes 1966088 | tf_op jit(solution)/shard_map/ppermute | solution.py:984
  99.5 268.1 %reduce-scatter.4.cloned.1.call-start = ((), (), s32[]{:S(2)}) async-start(), calls=%async_computation.5 | async-start | bytes 3604480 | tf_op jit(solution)/shard_map/reduce_scatter | solution.py:958
  100.9 53.5 %copy-start.40 = (f32[4,64,160]{2,1,0:T(8,128)}, f32[4,64,160]{2,1,0:T(8,128)S(1)}, u32[]{:S(2)}) copy-start(f32[4,64,160]{2,1,0:T(8,128)S(1)} %fusion.38) | copy-start | bytes 491524
  101.4 10.7 %slice-start = ((s8[8388608]{0:T(1024)(128)(4,1)}), s8[4194304]{0:T(1024)(128)(4,1)S(1)}, s32[]{:S(2)}) async-start(s8[8388608]{0:T(1024)(128)(4,1)} %bitcast.109), calls=%async_computation.8 | async-start | bytes 8388608
  101.4 10.7 %slice-start.1 = ((s8[8388608]{0:T(1024)(128)(4,1)}), s8[4194304]{0:T(1024)(128)(4,1)S(1)}, s32[]{:S(2)}) async-start(s8[8388608]{0:T(1024)(128)(4,1)} %bitcast.109), calls=%async_computation.9 | async-start | bytes 8388608
  110.5 42.7 %copy-start.42 = (f32[4,160,64]{2,1,0:T(8,128)}, f32[4,160,64]{2,1,0:T(8,128)S(1)}, u32[]{:S(2)}) copy-start(f32[4,160,64]{2,1,0:T(8,128)S(1)} %bitcast_multiply_fusion) | copy-start | bytes 491524
  110.6 40.9 %copy-start.44 = (bf16[640,512]{1,0:T(8,128)(2,1)}, bf16[640,512]{1,0:T(8,128)(2,1)S(1)}, u32[]{:S(2)}) copy-start(bf16[640,512]{1,0:T(8,128)(2,1)S(1)} %get-tuple-element.156) | copy-start | bytes 1966084
  110.6 40.8 %copy-start.49 = (bf16[640,512]{1,0:T(8,128)(2,1)}, bf16[640,512]{1,0:T(8,128)(2,1)S(1)}, u32[]{:S(2)}) copy-start(bf16[640,512]{1,0:T(8,128)(2,1)S(1)} %get-tuple-element.155) | copy-start | bytes 1966084
  110.7 43.4 %copy-start.51 = (bf16[640,512]{1,0:T(8,128)(2,1)}, bf16[640,512]{1,0:T(8,128)(2,1)S(1)}, u32[]{:S(2)}) copy-start(bf16[640,512]{1,0:T(8,128)(2,1)S(1)} %get-tuple-element.154) | copy-start | bytes 1966084
  112.1 38.5 %copy-start.56 = (f32[32,8,128]{2,1,0:T(8,128)S(1)}, f32[32,8,128]{2,1,0:T(8,128)}, u32[]{:S(2)}) copy-start(f32[32,8,128]{2,1,0:T(8,128)} %get-tuple-element.86) | copy-start | bytes 393220
  150.6 3.9 copy-start.14
  155.9 3.8 copy-start.38
  156.4 3.4 copy-start.7
  225.7 7.1 %copy-start.35 = (bf16[640,2048]{1,0:T(8,128)(2,1)S(1)}, bf16[640,2048]{1,0:T(8,128)(2,1)}, u32[]{:S(2)}) copy-start(bf16[640,2048]{1,0:T(8,128)(2,1)} %copy-done.34) | copy-start | bytes 7864324
  225.7 14.3 %collective-permute-start.4 = (bf16[640,1408]{1,0:T(8,128)(2,1)S(1)}, bf16[640,1408]{1,0:T(8,128)(2,1)}, u32[]{:S(2)}, u32[]{:S(2)}) collective-permute-start(bf16[640,1408]{1,0:T(8,128)(2,1)S(1)} %fusion.5.b.refs_4_), channel_id=1, source_target_pairs={{0,1},{1,0},{2,3},{3,2},{4,5},{5,4},{6,7},{7,6},{8,9},{9,8},{10,11... | collective-permute-start | bytes 5406728 | tf_op jit(solution)/shard_map/ppermute | solution.py:963
  229.9 4.3 copy-start.8
  232.4 7.5 %collective-permute-start.3 = (bf16[640,1024]{1,0:T(8,128)(2,1)}, bf16[640,1024]{1,0:T(8,128)(2,1)}, u32[]{:S(2)}, u32[]{:S(2)}) collective-permute-start(bf16[640,1024]{1,0:T(8,128)(2,1)} %constant_dynamic-slice_fusion.3), channel_id=1, source_target_pairs={{0,1},{1,0},{2,3},{3,2},{4,5},{5,4},{6,7},{7,6},{8,9},{9,8},{10,11... | collective-permute-start | bytes 3932168 | tf_op jit(solution)/shard_map/ppermute | solution.py:963
  234.0 15.2 %collective-permute-start.5 = (bf16[640,1024]{1,0:T(8,128)(2,1)}, bf16[640,1024]{1,0:T(8,128)(2,1)}, u32[]{:S(2)}, u32[]{:S(2)}) collective-permute-start(bf16[640,1024]{1,0:T(8,128)(2,1)} %constant_dynamic-slice_fusion.2), channel_id=1, source_target_pairs={{0,1},{1,0},{2,3},{3,2},{4,5},{5,4},{6,7},{7,6},{8,9},{9,8},{10,11... | collective-permute-start | bytes 3932168 | tf_op jit(solution)/shard_map/ppermute | solution.py:963
  239.6 9.6 %collective-permute-start.6 = (bf16[640,256]{1,0:T(8,128)(2,1)}, bf16[640,256]{1,0:T(8,128)(2,1)}, u32[]{:S(2)}, u32[]{:S(2)}) collective-permute-start(bf16[640,256]{1,0:T(8,128)(2,1)} %constant_dynamic-slice_fusion.1), channel_id=1, source_target_pairs={{0,1},{1,0},{2,3},{3,2},{4,5},{5,4},{6,7},{7,6},{8,9},{9,8},{10,11... | collective-permute-start | bytes 983048 | tf_op jit(solution)/shard_map/ppermute | solution.py:963
  249.0 190.5 %reduce-scatter.6.cloned.1.call-start = ((), (), s32[]{:S(2)}) async-start(), calls=%async_computation.6 | async-start | bytes 7208960 | tf_op jit(solution)/shard_map/reduce_scatter | solution.py:958
  283.4 12.1 %copy-start.36 = (bf16[640,2048]{1,0:T(8,128)(2,1)S(1)}, bf16[640,2048]{1,0:T(8,128)(2,1)}, u32[]{:S(2)}) copy-start(bf16[640,2048]{1,0:T(8,128)(2,1)} %copy-done.34) | copy-start | bytes 7864324
  283.4 12.1 %collective-permute-start.7 = (bf16[640,2816]{1,0:T(8,128)(2,1)S(1)}, bf16[640,2816]{1,0:T(8,128)(2,1)S(1)}, u32[]{:S(2)}, u32[]{:S(2)}) collective-permute-start(bf16[640,2816]{1,0:T(8,128)(2,1)S(1)} %pad_maximum_fusion.b), channel_id=1, source_target_pairs={{0,1},{1,0},{2,3},{3,2},{4,5},{5,4},{6,7},{7,6},{8,9},{9,8},{10,11... | collective-permute-start | bytes 10813448 | tf_op jit(solution)/shard_map/ppermute | solution.py:963
  308.3 213.1 %reduce-scatter.8.cloned.1.call-start = ((), (), s32[]{:S(2)}) async-start(), calls=%async_computation.7 | async-start | bytes 5242880 | tf_op jit(solution)/shard_map/reduce_scatter | solution.py:958
  364.2 15.6 %collective-permute-start.8 = (bf16[640,2048]{1,0:T(8,128)(2,1)}, bf16[640,2048]{1,0:T(8,128)(2,1)}, u32[]{:S(2)}, u32[]{:S(2)}) collective-permute-start(bf16[640,2048]{1,0:T(8,128)(2,1)} %get-tuple-element.107.b), channel_id=1, source_target_pairs={{0,1},{1,0},{2,3},{3,2},{4,5},{5,4},{6,7},{7,6},{8,9},{9,8},{10,11... | collective-permute-start | bytes 7864328 | tf_op jit(solution)/shard_map/ppermute | solution.py:963
  364.2 45.4 %collective-permute-start.10 = (bf16[160,2048]{1,0:T(8,128)(2,1)}, bf16[160,2048]{1,0:T(8,128)(2,1)S(1)}, u32[]{:S(2)}, u32[]{:S(2)}) collective-permute-start(bf16[160,2048]{1,0:T(8,128)(2,1)} %get-tuple-element.113), channel_id=1, source_target_pairs={{0,4},{1,5},{2,6},{3,7},{4,0},{5,1},{6,2},{7,3},{8,12},{9,13},{10,... | collective-permute-start | bytes 1966088 | tf_op jit(solution)/shard_map/ppermute | solution.py:984
  365.7 43.9 %collective-permute-start.11 = (bf16[160,2048]{1,0:T(8,128)(2,1)}, bf16[160,2048]{1,0:T(8,128)(2,1)S(1)}, u32[]{:S(2)}, u32[]{:S(2)}) collective-permute-start(bf16[160,2048]{1,0:T(8,128)(2,1)} %get-tuple-element.114), channel_id=1, source_target_pairs={{0,6},{1,7},{2,4},{3,5},{4,2},{5,3},{6,0},{7,1},{8,14},{9,15},{10,... | collective-permute-start | bytes 1966088 | tf_op jit(solution)/shard_map/ppermute | solution.py:984
  367.1 42.4 %collective-permute-start.9 = (bf16[160,2048]{1,0:T(8,128)(2,1)}, bf16[160,2048]{1,0:T(8,128)(2,1)}, u32[]{:S(2)}, u32[]{:S(2)}) collective-permute-start(bf16[160,2048]{1,0:T(8,128)(2,1)} %get-tuple-element.112), channel_id=1, source_target_pairs={{0,2},{1,3},{2,0},{3,1},{4,6},{5,7},{6,4},{7,5},{8,10},{9,11},{10,... | collective-permute-start | bytes 1966088 | tf_op jit(solution)/shard_map/ppermute | solution.py:984
  367.7 4.0 copy-start.39
  412.3 13.9 %copy-start.16 = (bf16[640,1536]{1,0:T(8,128)(2,1)}, bf16[640,1536]{1,0:T(8,128)(2,1)S(1)}, u32[]{:S(2)}) copy-start(bf16[640,1536]{1,0:T(8,128)(2,1)S(1)} %pad_maximum_fusion.1.b) | copy-start | bytes 5898244
  412.3 13.9 %collective-permute-start.13 = (bf16[640,1536]{1,0:T(8,128)(2,1)S(1)}, bf16[640,1536]{1,0:T(8,128)(2,1)S(1)}, u32[]{:S(2)}, u32[]{:S(2)}) collective-permute-start(bf16[640,1536]{1,0:T(8,128)(2,1)S(1)} %pad_maximum_fusion.1.b), channel_id=1, source_target_pairs={{0,1},{1,0},{2,3},{3,2},{4,5},{5,4},{6,7},{7,6},{8,9},{9,8},{10,11... | collective-permute-start | bytes 5898248 | tf_op jit(solution)/shard_map/ppermute | solution.py:963
  414.7 11.5 %collective-permute-start.12 = (bf16[640,1024]{1,0:T(8,128)(2,1)S(1)}, bf16[640,1024]{1,0:T(8,128)(2,1)S(1)}, u32[]{:S(2)}, u32[]{:S(2)}) collective-permute-start(bf16[640,1024]{1,0:T(8,128)(2,1)S(1)} %constant_dynamic-slice_fusion), channel_id=1, source_target_pairs={{0,1},{1,0},{2,3},{3,2},{4,5},{5,4},{6,7},{7,6},{8,9},{9,8},{10,11... | collective-permute-start | bytes 3932168 | tf_op jit(solution)/shard_map/ppermute | solution.py:963
  442.2 7.8 %copy-start.5 = (bf16[160,2048]{1,0:T(8,128)(2,1)S(1)}, bf16[160,2048]{1,0:T(8,128)(2,1)}, u32[]{:S(2)}) copy-start(bf16[160,2048]{1,0:T(8,128)(2,1)} %copy-done.4) | copy-start | bytes 1966084
  442.2 7.8 %copy-start.19 = (f32[160,2048]{1,0:T(8,128)S(1)}, f32[160,2048]{1,0:T(8,128)}, u32[]{:S(2)}) copy-start(f32[160,2048]{1,0:T(8,128)} %copy-done.18) | copy-start | bytes 3932164
  442.2 7.8 %copy-start.25 = (bf16[160,2048]{1,0:T(8,128)(2,1)S(1)}, bf16[160,2048]{1,0:T(8,128)(2,1)}, u32[]{:S(2)}) copy-start(bf16[160,2048]{1,0:T(8,128)(2,1)} %copy-done.24) | copy-start | bytes 1966084
  442.2 7.8 %copy-start.27 = (bf16[160,2048]{1,0:T(8,128)(2,1)S(1)}, bf16[160,2048]{1,0:T(8,128)(2,1)}, u32[]{:S(2)}) copy-start(bf16[160,2048]{1,0:T(8,128)(2,1)} %copy-done.26) | copy-start | bytes 1966084
  442.2 7.8 %copy-start.29 = (bf16[160,2048]{1,0:T(8,128)(2,1)S(1)}, bf16[160,2048]{1,0:T(8,128)(2,1)}, u32[]{:S(2)}) copy-start(bf16[160,2048]{1,0:T(8,128)(2,1)} %copy-done.28) | copy-start | bytes 1966084
  450.0 32.4 %copy-start.17 = (bf16[256,2816]{1,0:T(8,128)(2,1)S(1)}, bf16[256,2816]{1,0:T(8,128)(2,1)}, u32[]{:S(2)}) copy-start(bf16[256,2816]{1,0:T(8,128)(2,1)} %reduce-scatter.6.cloned.1.call-done.refs_0_) | copy-start | bytes 4325380
  481.4 25.8 %copy-start.21 = (f32[160,2048]{1,0:T(8,128)S(1)}, f32[160,2048]{1,0:T(8,128)}, u32[]{:S(2)}) copy-start(f32[160,2048]{1,0:T(8,128)} %copy-done.20) | copy-start | bytes 3932164
  (31 other events, 51.5 us)
Sparse Core Ops, SparseCore 0:
  94.2 109.4 all-gather.2
  205.3 67.2 all-gather.4
  274.9 54.8 reduce-scatter.3
  332.0 107.4 reduce-scatter.5
  441.6 79.7 reduce-scatter.7

commit v6 on v5

--- a/solution.py
+++ b/solution.py
@@ -48,8 +48,8 @@
     tokens_rows = tokens.shape[0]
 
     def kernel(g0_in, g1_in, g2_in, codes_in, q_far, k_far, v_far, o_in, gate_far, up_far, down_far, t_in,
-               g_out, c_out, line, feed_out, down_out, t_out, gain, t_mine, g_in, c_in, q_in, k_in, v_in,
-               gate_in, up_in, down_in, load, t_send, t_recv, own_sem, q_send, q_recv, side_send, side_recv, u_send, u_recv, d_send, d_recv, s_send, s_recv):
+               g_out, c_out, line_out, feed_far_out, down_far_out, t_out, gain, t_mine, g_in, c_in, q_in, k_in, v_in,
+               gate_in, up_in, down_in, line, feed_out, down_out, w_sem, load, t_send, t_recv, own_sem, q_send, q_recv, side_send, side_recv, u_send, u_recv, d_send, d_recv, s_send, s_recv):
         me = lax.axis_index("seq")
         h = chip_of(me)
         core = lax.rem(me, 2)
@@ -290,11 +290,23 @@
 
             if d == 1:
                 relay(spread_t[0])
+        def written(side, n):
+            at = pl.ds(pl.multiple_of(side * (planes * HEADS * strip), strip), planes * HEADS * strip)
+            return pltpu.make_async_copy(line.at[at], line_out.at[at], w_sem.at[n])
+
+        writes = [written(core, 0)]
+        writes[0].start()
         for _, copy in projections:
             copy.wait_send()
         finish(*spread_t)
         for copy in begun[len(shares) :]:
             copy.wait()
+        writes += [
+            pltpu.make_async_copy(feed_out, feed_far_out, w_sem.at[1]),
+            pltpu.make_async_copy(down_out, down_far_out, w_sem.at[2]),
+        ]
+        for copy in writes[1:]:
+            copy.start()
         for d in range(1, planes):
 
             @pl.when((z - d + 1 >= 0) & (z + 1 < planes))
@@ -313,6 +325,10 @@
             stack_across(plane).wait()
             for k in range(HEADS):
                 across(plane, k).wait()
+        writes.append(written(1 - core, 3))
+        writes[-1].start()
+        for copy in writes:
+            copy.wait()
 
     sides = count + 4 + 12
     vmem = pl.BlockSpec(memory_space=pltpu.VMEM)
@@ -330,7 +346,7 @@
             jax.ShapeDtypeStruct((HEADS * tokens_rows, width), bf16),
         ],
         in_specs=[vmem] * 4 + [ANY] * 3 + [vmem] + [ANY] * 3 + [vmem],
-        out_specs=[vmem] * 5 + [ANY],
+        out_specs=[vmem] * 2 + [ANY] * 4,
         scratch_shapes=[
             pltpu.VMEM((1, width), f32),
             pltpu.VMEM(tokens.shape, bf16),
@@ -338,6 +354,12 @@
             pltpu.VMEM((HEADS, tokens_rows, SLOTS), codes.dtype),
         ]
         + [pltpu.VMEM(x.shape, bf16) for x in (*weights, *feed)]
+        + [
+            pltpu.VMEM((count * strip, 4 * part), bf16),
+            pltpu.VMEM((HEADS * strip, 2 * feed_part), bf16),
+            pltpu.VMEM((HEADS * strip, feed_part), bf16),
+            pltpu.SemaphoreType.DMA((4,)),
+        ]
         + [pltpu.SemaphoreType.DMA((n,)) for n in sizes],
         compiler_params=pltpu.CompilerParams(
             collective_id=cid, has_side_effects=True, vmem_limit_bytes=58 << 20
@@ -357,7 +379,7 @@
         outs, refs = refs[:pieces], refs[pieces:]
         extra, refs = (refs[0], refs[1:]) if own_rows else (None, refs)
         gain_out, refs = (refs[0], refs[1:]) if shared else (None, refs)
-        send, recv, gain_in, gain_send, gain_recv = refs
+        send, recv, gain_in, gain_send, gain_recv, tail, tail_sem = refs
         me = lax.axis_index("seq")
         h = chip_of(me)
         targets = [chip_on(me, h, k) for k in (3, 1, 2)]
@@ -397,7 +419,10 @@
         if shared:
             gain_in[me] = shares[me]
         if own_rows:
-            blocks = [src[pl.ds(k * rows, rows), pl.ds(pieces * part, part)] for k in range(HEADS)]
+            fetch = pltpu.make_async_copy(src.at[:, pl.ds(pieces * part, part)], tail, tail_sem.at[0])
+            fetch.start()
+            fetch.wait()
+            blocks = [tail[pl.ds(k * rows, rows), :] for k in range(HEADS)]
             extra[...] = reorder(jnp.concatenate(blocks, axis=1), planes, True)
         for copy in copies:
             copy.wait()
@@ -413,7 +438,7 @@
     return pl.pallas_call(
         kernel,
         out_shape=shapes,
-        in_specs=[vmem] * (1 + int(shared)),
+        in_specs=[ANY if own_rows else vmem] + [vmem] * int(shared),
         out_specs=[vmem] * len(shapes),
         scratch_shapes=[
             pltpu.SemaphoreType.DMA((4 * pieces,)),
@@ -421,6 +446,8 @@
             pltpu.VMEM((count if shared else 1, 8, 128), f32),
             pltpu.SemaphoreType.DMA((count if shared else 1,)),
             pltpu.SemaphoreType.DMA((count if shared else 1,)),
+            pltpu.VMEM((x.shape[0], part) if own_rows else (16, 128), bf16),
+            pltpu.SemaphoreType.DMA((1,)),
         ],
         compiler_params=pltpu.CompilerParams(
             collective_id=cid, has_side_effects=True, vmem_limit_bytes=40 << 20

time: 550 us -> 549 us (level)
  no operation moved by 1% of the time
where the time goes in v6:
time: 549 us; the launch traced here: 542 us
  Pallas kernels  364 us (66%)
  matrix products  73.1 us (13%)
  waiting for transfers between devices  39.2 us (7%)
  local copies, waits for them, and re-layouts  36.3 us (7%)
  between operations  15.5 us (3%)
  starting transfers between devices  8.77 us (2%)
    pallas_call x3, Pallas kernels, plane_stage(): pl.pallas_call(kernel, out_shape=shapes, in_specs=[vmem] * (has + len(blo...  127 us
    pallas_call x1, Pallas kernels, opening(): pl.pallas_call(kernel, out_shape=[shares, logits, jax.ShapeDtypeStruct((c...  86.4 us
    pallas_call x2, Pallas kernels, carry_states(): pl.pallas_call(kernel, out_shape=[jax.ShapeDtypeStruct(keys.shape, f32)]...  63 us
    pallas_call x3, Pallas kernels, return_columns(): pl.pallas_call(kernel, out_shape=shapes, in_specs=[ANY if own_rows else v...  48.3 us
    pallas_call x4, Pallas kernels, chip_sum(): pl.pallas_call(kernel, out_shape=jax.ShapeDtypeStruct((half, columns + mo...  30.7 us
    dot_general x9, matrix products, plain(): return jnp.einsum(form, left, right, preferred_element_type=f32)  25.7 us
    unnamed x123, local copies, waits for them, and re-layouts  24.9 us
    all_gather x2, waiting for transfers between devices, gather_line(): return lax.all_gather(x, 'seq', axis=0, tiled=True, axis_index_groups=lines)  24.3 us
  transfers between devices with their start and end apart: 19, of which 3 were waited for; matrix products, arithmetic and copies ran while one was open for 18% of the time, Pallas kernels for 49%

profile of v6, /device:TPU:0, one launch (start us, length us, event | category | flops | bytes accessed | tf_op | source)
XLA Modules:
  0.0 542.4 jit_solution(6054959050145180469)
XLA Ops:
  7.2 86.4 %shard_map.229 = (f32[32,8,128]{2,1,0:T(8,128)}, s32[4,160,64]{2,1,0:T(8,128)}, bf16[2048,2048]{1,0:T(8,128)(2,1)}, bf16[256,2816]{1,0:T(8,128)(2,1)}, bf16[256,...) custom-call(bf16[1,64]{1,0:T(2,128)(2,1)} %bitcast.138, bf16[1,64]{1,0:T(2,128)(2,1)} %bitcast.139, bf16[1,64]{1,0:T(2,128)(2,1)} %bitcast.140, ...), custom_call_target="tpu_custom_call" | custom-call | bytes 289000000 | tf_op jit(solution)/shard_map/pallas_call | solution.py:338
  93.7 1.7 shard_map.231
  96.7 2.3 collective-permute-start.2
  100.9 8.4 %fusion.6 = bf16[640,1536]{1,0:T(8,128)(2,1)S(1)} fusion(bf16[640,2048]{1,0:T(8,128)(2,1)} %get-tuple-element.81.a, bf16[2048,2048]{1,0:T(8,128)(2,1)} %get-tuple-element.83.refs_0_), kind=kOutput, calls=%fused_computation.11 | convolution fusion | flops 4027514880 | bytes 10878976 | tf_op jit(solution)/shard_map/dot_general | solution.py:1064
  111.5 37.9 %shard_map.230 = (f32[4,64,512]{2,1,0:T(8,128)S(1)}, f32[4,64,512]{2,1,0:T(8,128)S(1)}, bf16[512,2048]{1,0:T(8,128)(2,1)S(1)}) custom-call(f32[4,64,512]{2,1,0:T(8,128)S(1)} %fusion.29.k_in, f32[4,64,512]{2,1,0:T(8,128)S(1)} %fusion.28.v_in, f32[4,64,128]{2,1,0:T(8,128)S(1)} %broadcast_in_dim.89.g_in, bf16[2048,2048]{1,0:T(8,128)(2,1)S(1)} %bitcast.110), custom_call_target="tpu_custom_call" | custom-call | bytes 74800000 | tf_op jit(solution)/shard_map/pallas_call | solution.py:925
  153.3 1.4 multiply_reduce_fusion.2
  155.2 3.4 convolution_convert_fusion.1.refs_0_
  158.6 46.3 %shard_map.232 = (f32[160,2048]{1,0:T(8,128)S(1)}, bf16[640,2048]{1,0:T(8,128)(2,1)S(1)}) custom-call(bf16[640,2048]{1,0:T(8,128)(2,1)S(1)} %convolution_convert_fusion.1.refs_0_, bf16[160,2048]{1,0:T(8,128)(2,1)S(1)} %get-tuple-element.88.refs_1_, f32[1,2048]{1,0:T(1,128)S(1)} %broadcast_in_dim_reshape.6.refs_2_.refs_3_), custom_call_target="tpu_custom_call" | custom-call | bytes 170000000 | tf_op jit(solution)/shard_map/pallas_call | solution.py:635
  204.9 1.5 copy-done.34
  207.3 2.0 constant_dynamic-update-slice_fusion.2
  209.3 11.9 %fusion.55 = f32[640,2816]{1,0:T(8,128)S(1)} fusion(bf16[640,2048]{1,0:T(8,128)(2,1)} %copy-done.34, bf16[2048,2816]{1,0:T(8,128)(2,1)} %all-gather.3.cloned.1.call-done), kind=kOutput, calls=%fused_computation.115 | convolution fusion | flops 7381975040 | bytes 21364736 | tf_op jit(solution)/shard_map/dot_general | solution.py:1104
  222.3 1.9 copy-done.46
  224.2 2.2 constant_dynamic-update-slice_fusion.1
  226.4 2.0 constant_dynamic-update-slice_fusion.a
  228.4 2.5 constant_dynamic-slice_fusion.3
  231.3 1.2 constant_dynamic-slice_fusion.2
  232.6 2.9 shard_map.234.a
  236.4 1.7 constant_dynamic-slice_fusion.1
  238.5 7.4 %shard_map.233 = bf16[1024,1408]{1,0:T(8,128)(2,1)S(1)} custom-call(s32[1]{0:T(128)} %bitcast.which, bf16[640,2048]{1,0:T(8,128)(2,1)} %constant_dynamic-update-slice_fusion.a, bf16[640,1408]{1,0:T(8,128)(2,1)S(1)} %fusion.5.b.refs_4_, bf16[640,1024]{1,0:T(8,128)(2,1)} %collective-permute-done.3.c, bf16[640,1408]{1,0:T(8,128)(2,1)} %collective-permute-done.4.d), custom_call_target="tpu_custom_call" | custom-call | flops 3690987520 | bytes 9109504 | tf_op jit(solution)/shard_map/pallas_call | solution.py:679
  245.9 1.5 copy-done.3
  247.7 24.3 %all-gather.5.cloned.1.call-done.refs_5_ = bf16[2048,1408]{1,0:T(8,128)(2,1)} async-done(((bf16[256,1408]{1,0:T(8,128)(2,1)}), bf16[2048,1408]{1,0:T(8,128)(2,1)}) %all-gather.5.cloned.1.call-update) | async-done | bytes 5767184 | tf_op jit(solution)/shard_map/all_gather | solution.py:980
  272.0 10.6 %multiply_convert_fusion.1 = (bf16[640,1408]{1,0:T(8,128)(2,1)S(1)}, bf16[640,1408]{1,0:T(8,128)(2,1)S(1)}) fusion(f32[640,2816]{1,0:T(8,128)} %copy-done.46, bf16[640,2048]{1,0:T(8,128)(2,1)} %constant_dynamic-update-slice_fusion.a, bf16[2048,1408]{1,0:T(8,128)(2,1)} %all-gather.5.cloned.1.call-done.refs_5_), kind=kOutput, calls=%fused_computation.9 | convolution fusion | flops 3702702080 | bytes 19202048 | tf_op jit(solution)/shard_map/dot_general | solution.py:1120
  283.2 11.8 %convolution_convert_fusion.refs_0_ = bf16[640,2048]{1,0:T(8,128)(2,1)} fusion(bf16[2048,2816]{1,0:T(8,128)(2,1)} %all-gather.3.cloned.1.call-done, bf16[640,1408]{1,0:T(8,128)(2,1)S(1)} %get-tuple-element.153, bf16[640,1408]{1,0:T(8,128)(2,1)S(1)} %get-tuple-element.152), kind=kOutput, calls=%fused_computation.13 | convolution fusion | flops 7390494720 | bytes 17760256 | tf_op jit(solution)/shard_map/tf,df->td/dot_general | solution.py:949
  294.9 12.7 %shard_map.235 = bf16[1024,2816]{1,0:T(8,128)(2,1)} custom-call(s32[1]{0:T(128)} %bitcast.which, bf16[640,2048]{1,0:T(8,128)(2,1)S(1)} %copy-done.36, bf16[640,2816]{1,0:T(8,128)(2,1)S(1)} %pad_maximum_fusion.b, bf16[640,1024]{1,0:T(8,128)(2,1)} %collective-permute-done.5.c, bf16[640,2816]{1,0:T(8,128)(2,1)S(1)} %collective-permute-done.7.d), custom_call_target="tpu_custom_call" | custom-call | flops 7381975040 | bytes 15597568 | tf_op jit(solution)/shard_map/pallas_call | solution.py:679
  307.7 1.7 copy-done.9
  309.5 1.1 copy-done.11
  310.6 51.2 %shard_map.236 = (f32[160,2048]{1,0:T(8,128)S(1)}, f32[8,2048]{1,0:T(8,128)S(1)}, bf16[640,2048]{1,0:T(8,128)(2,1)}, bf16[160,2048]{1,0:T(8,128)(2,1)S(1)}, bf16...) custom-call(bf16[640,2048]{1,0:T(8,128)(2,1)S(1)} %copy-done.9, ...), custom_call_target="tpu_custom_call" | custom-call | bytes 170000000 | tf_op jit(solution)/shard_map/pallas_call | solution.py:635
  363.6 1.4 collective-permute-start.10
  365.0 1.5 collective-permute-start.11
  367.1 4.0 fusion.56
  377.9 1.2 fusion.14
  379.2 4.5 shard_map.237
  383.7 25.2 %shard_map.238 = (f32[4,64,512]{2,1,0:T(8,128)S(1)}, f32[4,64,512]{2,1,0:T(8,128)S(1)}, bf16[1024,512]{1,0:T(8,128)(2,1)S(1)}) custom-call(f32[4,64,512]{2,1,0:T(8,128)S(1)} %fusion.22.k_in, f32[4,64,512]{2,1,0:T(8,128)S(1)} %fusion.25.v_in, f32[4,64,128]{2,1,0:T(8,128)S(1)} %broadcast_in_dim.89.g_in, bf16[1,4,64,2048]{3,2,1,0:T(8,128)(2,1)S(1)} %bitcast.111), custom_call_target="tpu_custom_call" | custom-call | bytes 74800000 | tf_op jit(solution)/shard_map/pallas_call | solution.py:925
  408.9 1.3 fusion.12
  410.2 1.3 fusion.13
  411.7 2.2 copy-done.33
  414.2 11.4 %shard_map.240.refs_0_ = bf16[64,5632]{1,0:T(8,128)(2,1)S(1)} custom-call(bf16[256,1408]{1,0:T(8,128)(2,1)S(1)} %copy-done.23), custom_call_target="tpu_custom_call" | custom-call | bytes 47600000 | tf_op jit(solution)/shard_map/pallas_call | solution.py:438
  425.6 6.1 %shard_map.239 = bf16[1024,2048]{1,0:T(8,128)(2,1)S(1)} custom-call(s32[1]{0:T(128)} %bitcast.which, bf16[640,2048]{1,0:T(8,128)(2,1)S(1)} %copy-done.33, bf16[640,1536]{1,0:T(8,128)(2,1)S(1)} %pad_maximum_fusion.1.b, bf16[640,1024]{1,0:T(8,128)(2,1)S(1)} %collective-permute-done.12.c, bf16[640,1536]{1,0:T(8,128)(2,1)S(1)} %collective-permute-done.13.d, ...), custom_call_target="tpu_custom_call" | custom-call | flops 4026531840 | bytes 9699328 | tf_op jit(solution)/shard_map/pallas_call | solution.py:679
  431.7 2.0 copy-done
  433.7 5.1 reduce-scatter.6.cloned.1.call-done.refs_0_
  441.6 7.8 %fusion.9.refs_0_ = bf16[640,2048]{1,0:T(8,128)(2,1)S(1)} fusion(bf16[640,1536]{1,0:T(8,128)(2,1)} %copy-done.16, bf16[2048,2048]{1,0:T(8,128)(2,1)} %get-tuple-element.83.refs_0_), kind=kOutput, calls=%fused_computation.12 | convolution fusion | flops 4027842560 | bytes 10878976 | tf_op jit(solution)/shard_map/tf,df->td/dot_general | solution.py:949
  449.4 29.5 %shard_map.241 = (f32[160,2048]{1,0:T(8,128)S(1)}, f32[8,2048]{1,0:T(8,128)S(1)}, bf16[160,2048]{1,0:T(8,128)(2,1)S(1)}) custom-call(bf16[640,2048]{1,0:T(8,128)(2,1)S(1)} %fusion.9.refs_0_, bf16[160,2048]{1,0:T(8,128)(2,1)S(1)} %copy-done.5, f32[160,2048]{1,0:T(8,128)S(1)} %copy-done.19, f32[1,2048]{1,0:T(1,128)S(1)} %broadcast_in_dim_reshape.7.refs_3_, ...), custom_call_target="tpu_custom_call" | custom-call | bytes 85000000 | tf_op jit(solution)/shard_map/pallas_call | solution.py:635
  481.8 24.8 %shard_map.242 = (bf16[64,5632]{1,0:T(8,128)(2,1)S(1)}, bf16[64,5632]{1,0:T(8,128)(2,1)S(1)}, f32[8,128]{1,0:T(8,128)S(1)}) custom-call(bf16[256,2816]{1,0:T(8,128)(2,1)S(1)} %copy-done.17, f32[32,8,128]{2,1,0:T(8,128)S(1)} %pad.4.refs_1_), custom_call_target="tpu_custom_call" | custom-call | bytes 47600000 | tf_op jit(solution)/shard_map/pallas_call | solution.py:438
  507.7 2.9 shard_map.243
  511.1 9.6 %reduce-scatter.8.cloned.1.call-done.refs_0_ = bf16[256,2048]{1,0:T(8,128)(2,1)} async-done(((bf16[1024,2048]{1,0:T(8,128)(2,1)}), bf16[256,2048]{1,0:T(8,128)(2,1)}) %reduce-scatter.8.cloned.1.call-update) | async-done | bytes 1048592 | tf_op jit(solution)/shard_map/reduce_scatter | solution.py:985
  520.7 1.2 copy-done.22
  522.0 12.1 %shard_map.244 = (bf16[64,2048]{1,0:T(8,128)(2,1)S(1)}, bf16[64,2048]{1,0:T(8,128)(2,1)S(1)}, bf16[64,2048]{1,0:T(8,128)(2,1)S(1)}, bf16[64,2048]{1,0:T(8,128)(2,1)S(1)}) custom-call(bf16[256,2048]{1,0:T(8,128)(2,1)S(1)} %copy-done.22), custom_call_target="tpu_custom_call" | custom-call | bytes 47600000 | tf_op jit(solution)/shard_map/pallas_call | solution.py:438
  534.0 1.4 shard_map.245
  (217 shorter events, 30.9 us)
Async XLA Ops:
  7.2 202.1 %all-gather.3.cloned.1.call-start = ((), (), s32[]{:S(2)}) async-start(), calls=%async_computation.3 | async-start | bytes 12976128 | tf_op jit(solution)/shard_map/all_gather | solution.py:980
  7.2 86.5 %copy-start.6 = (bf16[160,2048]{1,0:T(8,128)(2,1)S(1)}, bf16[160,2048]{1,0:T(8,128)(2,1)}, u32[]{:S(2)}) copy-start(bf16[160,2048]{1,0:T(8,128)(2,1)} %refs_0_.1) | copy-start | bytes 1966084
  7.2 86.5 %copy-start.32 = (bf16[160,2048]{1,0:T(8,128)(2,1)S(1)}, bf16[160,2048]{1,0:T(8,128)(2,1)}, u32[]{:S(2)}) copy-start(bf16[160,2048]{1,0:T(8,128)(2,1)} %refs_1_.1) | copy-start | bytes 1966084
  93.6 5.6 %copy-start.57 = (s32[4]{0:T(128)S(1)}, s32[4]{0:T(128)}, u32[]{:S(2)}) copy-start(s32[4]{0:T(128)} %param.17) | copy-start | bytes 52
  93.6 6.2 %copy-start.55 = (s32[4,160,64]{2,1,0:T(8,128)S(1)}, s32[4,160,64]{2,1,0:T(8,128)}, u32[]{:S(2)}) copy-start(s32[4,160,64]{2,1,0:T(8,128)} %get-tuple-element.82) | copy-start | bytes 491524
  93.7 178.3 %all-gather.5.cloned.1.call-start = ((), (), s32[]{:S(2)}) async-start(), calls=%async_computation.4 | async-start | bytes 6488064 | tf_op jit(solution)/shard_map/all_gather | solution.py:980
  95.5 63.1 %copy-start.4 = (bf16[160,2048]{1,0:T(8,128)(2,1)}, bf16[160,2048]{1,0:T(8,128)(2,1)S(1)}, u32[]{:S(2)}) copy-start(bf16[160,2048]{1,0:T(8,128)(2,1)S(1)} %get-tuple-element.88.refs_1_) | copy-start | bytes 1966084
  95.5 110.9 %copy-start.10 = (bf16[160,2048]{1,0:T(8,128)(2,1)}, bf16[160,2048]{1,0:T(8,128)(2,1)S(1)}, u32[]{:S(2)}) copy-start(bf16[160,2048]{1,0:T(8,128)(2,1)S(1)} %get-tuple-element.92.refs_2_) | copy-start | bytes 1966084
  95.5 110.9 %collective-permute-start = (bf16[160,2048]{1,0:T(8,128)(2,1)S(1)}, bf16[160,2048]{1,0:T(8,128)(2,1)}, u32[]{:S(2)}, u32[]{:S(2)}) collective-permute-start(bf16[160,2048]{1,0:T(8,128)(2,1)S(1)} %get-tuple-element.92.refs_2_), channel_id=1, source_target_pairs={{0,2},{1,3},{2,0},{3,1},{4,6},{5,7},{6,4},{7,5},{8,10},{9,11},{10,... | collective-permute-start | bytes 1966088 | tf_op jit(solution)/shard_map/ppermute | solution.py:1011
  96.1 110.3 %collective-permute-start.1 = (bf16[160,2048]{1,0:T(8,128)(2,1)S(1)}, bf16[160,2048]{1,0:T(8,128)(2,1)}, u32[]{:S(2)}, u32[]{:S(2)}) collective-permute-start(bf16[160,2048]{1,0:T(8,128)(2,1)S(1)} %get-tuple-element.92.refs_2_), channel_id=1, source_target_pairs={{0,4},{1,5},{2,6},{3,7},{4,0},{5,1},{6,2},{7,3},{8,12},{9,13},{10,... | collective-permute-start | bytes 1966088 | tf_op jit(solution)/shard_map/ppermute | solution.py:1011
  96.7 109.7 %collective-permute-start.2 = (bf16[160,2048]{1,0:T(8,128)(2,1)S(1)}, bf16[160,2048]{1,0:T(8,128)(2,1)}, u32[]{:S(2)}, u32[]{:S(2)}) collective-permute-start(bf16[160,2048]{1,0:T(8,128)(2,1)S(1)} %get-tuple-element.92.refs_2_), channel_id=1, source_target_pairs={{0,6},{1,7},{2,4},{3,5},{4,2},{5,3},{6,0},{7,1},{8,14},{9,15},{10,... | collective-permute-start | bytes 1966088 | tf_op jit(solution)/shard_map/ppermute | solution.py:1011
  99.1 268.1 %reduce-scatter.4.cloned.1.call-start = ((), (), s32[]{:S(2)}) async-start(), calls=%async_computation.5 | async-start | bytes 3604480 | tf_op jit(solution)/shard_map/reduce_scatter | solution.py:985
  100.4 52.9 %copy-start.40 = (f32[4,64,160]{2,1,0:T(8,128)}, f32[4,64,160]{2,1,0:T(8,128)S(1)}, u32[]{:S(2)}) copy-start(f32[4,64,160]{2,1,0:T(8,128)S(1)} %fusion.38) | copy-start | bytes 491524
  100.9 10.6 %slice-start = ((s8[8388608]{0:T(1024)(128)(4,1)}), s8[4194304]{0:T(1024)(128)(4,1)S(1)}, s32[]{:S(2)}) async-start(s8[8388608]{0:T(1024)(128)(4,1)} %bitcast.109), calls=%async_computation.8 | async-start | bytes 8388608
  100.9 10.6 %slice-start.1 = ((s8[8388608]{0:T(1024)(128)(4,1)}), s8[4194304]{0:T(1024)(128)(4,1)S(1)}, s32[]{:S(2)}) async-start(s8[8388608]{0:T(1024)(128)(4,1)} %bitcast.109), calls=%async_computation.9 | async-start | bytes 8388608
  109.9 42.2 %copy-start.42 = (f32[4,160,64]{2,1,0:T(8,128)}, f32[4,160,64]{2,1,0:T(8,128)S(1)}, u32[]{:S(2)}) copy-start(f32[4,160,64]{2,1,0:T(8,128)S(1)} %bitcast_multiply_fusion) | copy-start | bytes 491524
  110.1 40.3 %copy-start.44 = (bf16[640,512]{1,0:T(8,128)(2,1)}, bf16[640,512]{1,0:T(8,128)(2,1)S(1)}, u32[]{:S(2)}) copy-start(bf16[640,512]{1,0:T(8,128)(2,1)S(1)} %get-tuple-element.156) | copy-start | bytes 1966084
  110.1 40.3 %copy-start.49 = (bf16[640,512]{1,0:T(8,128)(2,1)}, bf16[640,512]{1,0:T(8,128)(2,1)S(1)}, u32[]{:S(2)}) copy-start(bf16[640,512]{1,0:T(8,128)(2,1)S(1)} %get-tuple-element.155) | copy-start | bytes 1966084
  110.1 42.9 %copy-start.51 = (bf16[640,512]{1,0:T(8,128)(2,1)}, bf16[640,512]{1,0:T(8,128)(2,1)S(1)}, u32[]{:S(2)}) copy-start(bf16[640,512]{1,0:T(8,128)(2,1)S(1)} %get-tuple-element.154) | copy-start | bytes 1966084
  111.5 37.9 %copy-start.56 = (f32[32,8,128]{2,1,0:T(8,128)S(1)}, f32[32,8,128]{2,1,0:T(8,128)}, u32[]{:S(2)}) copy-start(f32[32,8,128]{2,1,0:T(8,128)} %get-tuple-element.86) | copy-start | bytes 393220
  149.4 3.9 copy-start.14
  154.8 3.8 copy-start.38
  155.2 3.4 copy-start.7
  224.2 7.1 %copy-start.35 = (bf16[640,2048]{1,0:T(8,128)(2,1)S(1)}, bf16[640,2048]{1,0:T(8,128)(2,1)}, u32[]{:S(2)}) copy-start(bf16[640,2048]{1,0:T(8,128)(2,1)} %copy-done.34) | copy-start | bytes 7864324
  224.2 14.3 %collective-permute-start.4 = (bf16[640,1408]{1,0:T(8,128)(2,1)S(1)}, bf16[640,1408]{1,0:T(8,128)(2,1)}, u32[]{:S(2)}, u32[]{:S(2)}) collective-permute-start(bf16[640,1408]{1,0:T(8,128)(2,1)S(1)} %fusion.5.b.refs_4_), channel_id=1, source_target_pairs={{0,1},{1,0},{2,3},{3,2},{4,5},{5,4},{6,7},{7,6},{8,9},{9,8},{10,11... | collective-permute-start | bytes 5406728 | tf_op jit(solution)/shard_map/ppermute | solution.py:990
  228.4 4.2 copy-start.8
  230.9 7.6 %collective-permute-start.3 = (bf16[640,1024]{1,0:T(8,128)(2,1)}, bf16[640,1024]{1,0:T(8,128)(2,1)}, u32[]{:S(2)}, u32[]{:S(2)}) collective-permute-start(bf16[640,1024]{1,0:T(8,128)(2,1)} %constant_dynamic-slice_fusion.3), channel_id=1, source_target_pairs={{0,1},{1,0},{2,3},{3,2},{4,5},{5,4},{6,7},{7,6},{8,9},{9,8},{10,11... | collective-permute-start | bytes 3932168 | tf_op jit(solution)/shard_map/ppermute | solution.py:990
  232.5 15.2 %collective-permute-start.5 = (bf16[640,1024]{1,0:T(8,128)(2,1)}, bf16[640,1024]{1,0:T(8,128)(2,1)}, u32[]{:S(2)}, u32[]{:S(2)}) collective-permute-start(bf16[640,1024]{1,0:T(8,128)(2,1)} %constant_dynamic-slice_fusion.2), channel_id=1, source_target_pairs={{0,1},{1,0},{2,3},{3,2},{4,5},{5,4},{6,7},{7,6},{8,9},{9,8},{10,11... | collective-permute-start | bytes 3932168 | tf_op jit(solution)/shard_map/ppermute | solution.py:990
  238.1 9.6 %collective-permute-start.6 = (bf16[640,256]{1,0:T(8,128)(2,1)}, bf16[640,256]{1,0:T(8,128)(2,1)}, u32[]{:S(2)}, u32[]{:S(2)}) collective-permute-start(bf16[640,256]{1,0:T(8,128)(2,1)} %constant_dynamic-slice_fusion.1), channel_id=1, source_target_pairs={{0,1},{1,0},{2,3},{3,2},{4,5},{5,4},{6,7},{7,6},{8,9},{9,8},{10,11... | collective-permute-start | bytes 983048 | tf_op jit(solution)/shard_map/ppermute | solution.py:990
  247.5 191.4 %reduce-scatter.6.cloned.1.call-start = ((), (), s32[]{:S(2)}) async-start(), calls=%async_computation.6 | async-start | bytes 7208960 | tf_op jit(solution)/shard_map/reduce_scatter | solution.py:985
  282.8 12.1 %copy-start.36 = (bf16[640,2048]{1,0:T(8,128)(2,1)S(1)}, bf16[640,2048]{1,0:T(8,128)(2,1)}, u32[]{:S(2)}) copy-start(bf16[640,2048]{1,0:T(8,128)(2,1)} %copy-done.34) | copy-start | bytes 7864324
  282.8 12.1 %collective-permute-start.7 = (bf16[640,2816]{1,0:T(8,128)(2,1)S(1)}, bf16[640,2816]{1,0:T(8,128)(2,1)S(1)}, u32[]{:S(2)}, u32[]{:S(2)}) collective-permute-start(bf16[640,2816]{1,0:T(8,128)(2,1)S(1)} %pad_maximum_fusion.b), channel_id=1, source_target_pairs={{0,1},{1,0},{2,3},{3,2},{4,5},{5,4},{6,7},{7,6},{8,9},{9,8},{10,11... | collective-permute-start | bytes 10813448 | tf_op jit(solution)/shard_map/ppermute | solution.py:990
  307.7 213.0 %reduce-scatter.8.cloned.1.call-start = ((), (), s32[]{:S(2)}) async-start(), calls=%async_computation.7 | async-start | bytes 5242880 | tf_op jit(solution)/shard_map/reduce_scatter | solution.py:985
  363.6 15.6 %collective-permute-start.8 = (bf16[640,2048]{1,0:T(8,128)(2,1)}, bf16[640,2048]{1,0:T(8,128)(2,1)}, u32[]{:S(2)}, u32[]{:S(2)}) collective-permute-start(bf16[640,2048]{1,0:T(8,128)(2,1)} %get-tuple-element.107.b), channel_id=1, source_target_pairs={{0,1},{1,0},{2,3},{3,2},{4,5},{5,4},{6,7},{7,6},{8,9},{9,8},{10,11... | collective-permute-start | bytes 7864328 | tf_op jit(solution)/shard_map/ppermute | solution.py:990
  363.6 45.2 %collective-permute-start.10 = (bf16[160,2048]{1,0:T(8,128)(2,1)}, bf16[160,2048]{1,0:T(8,128)(2,1)S(1)}, u32[]{:S(2)}, u32[]{:S(2)}) collective-permute-start(bf16[160,2048]{1,0:T(8,128)(2,1)} %get-tuple-element.113), channel_id=1, source_target_pairs={{0,4},{1,5},{2,6},{3,7},{4,0},{5,1},{6,2},{7,3},{8,12},{9,13},{10,... | collective-permute-start | bytes 1966088 | tf_op jit(solution)/shard_map/ppermute | solution.py:1011
  365.0 43.9 %collective-permute-start.11 = (bf16[160,2048]{1,0:T(8,128)(2,1)}, bf16[160,2048]{1,0:T(8,128)(2,1)S(1)}, u32[]{:S(2)}, u32[]{:S(2)}) collective-permute-start(bf16[160,2048]{1,0:T(8,128)(2,1)} %get-tuple-element.114), channel_id=1, source_target_pairs={{0,6},{1,7},{2,4},{3,5},{4,2},{5,3},{6,0},{7,1},{8,14},{9,15},{10,... | collective-permute-start | bytes 1966088 | tf_op jit(solution)/shard_map/ppermute | solution.py:1011
  366.5 42.5 %collective-permute-start.9 = (bf16[160,2048]{1,0:T(8,128)(2,1)}, bf16[160,2048]{1,0:T(8,128)(2,1)}, u32[]{:S(2)}, u32[]{:S(2)}) collective-permute-start(bf16[160,2048]{1,0:T(8,128)(2,1)} %get-tuple-element.112), channel_id=1, source_target_pairs={{0,2},{1,3},{2,0},{3,1},{4,6},{5,7},{6,4},{7,5},{8,10},{9,11},{10,... | collective-permute-start | bytes 1966088 | tf_op jit(solution)/shard_map/ppermute | solution.py:1011
  367.1 4.0 copy-start.39
  411.7 13.9 %copy-start.16 = (bf16[640,1536]{1,0:T(8,128)(2,1)}, bf16[640,1536]{1,0:T(8,128)(2,1)S(1)}, u32[]{:S(2)}) copy-start(bf16[640,1536]{1,0:T(8,128)(2,1)S(1)} %pad_maximum_fusion.1.b) | copy-start | bytes 5898244
  411.7 13.9 %collective-permute-start.13 = (bf16[640,1536]{1,0:T(8,128)(2,1)S(1)}, bf16[640,1536]{1,0:T(8,128)(2,1)S(1)}, u32[]{:S(2)}, u32[]{:S(2)}) collective-permute-start(bf16[640,1536]{1,0:T(8,128)(2,1)S(1)} %pad_maximum_fusion.1.b), channel_id=1, source_target_pairs={{0,1},{1,0},{2,3},{3,2},{4,5},{5,4},{6,7},{7,6},{8,9},{9,8},{10,11... | collective-permute-start | bytes 5898248 | tf_op jit(solution)/shard_map/ppermute | solution.py:990
  414.1 11.5 %collective-permute-start.12 = (bf16[640,1024]{1,0:T(8,128)(2,1)S(1)}, bf16[640,1024]{1,0:T(8,128)(2,1)S(1)}, u32[]{:S(2)}, u32[]{:S(2)}) collective-permute-start(bf16[640,1024]{1,0:T(8,128)(2,1)S(1)} %constant_dynamic-slice_fusion), channel_id=1, source_target_pairs={{0,1},{1,0},{2,3},{3,2},{4,5},{5,4},{6,7},{7,6},{8,9},{9,8},{10,11... | collective-permute-start | bytes 3932168 | tf_op jit(solution)/shard_map/ppermute | solution.py:990
  441.5 7.8 %copy-start.5 = (bf16[160,2048]{1,0:T(8,128)(2,1)S(1)}, bf16[160,2048]{1,0:T(8,128)(2,1)}, u32[]{:S(2)}) copy-start(bf16[160,2048]{1,0:T(8,128)(2,1)} %copy-done.4) | copy-start | bytes 1966084
  441.5 7.8 %copy-start.19 = (f32[160,2048]{1,0:T(8,128)S(1)}, f32[160,2048]{1,0:T(8,128)}, u32[]{:S(2)}) copy-start(f32[160,2048]{1,0:T(8,128)} %copy-done.18) | copy-start | bytes 3932164
  441.5 7.8 %copy-start.25 = (bf16[160,2048]{1,0:T(8,128)(2,1)S(1)}, bf16[160,2048]{1,0:T(8,128)(2,1)}, u32[]{:S(2)}) copy-start(bf16[160,2048]{1,0:T(8,128)(2,1)} %copy-done.24) | copy-start | bytes 1966084
  441.5 7.8 %copy-start.27 = (bf16[160,2048]{1,0:T(8,128)(2,1)S(1)}, bf16[160,2048]{1,0:T(8,128)(2,1)}, u32[]{:S(2)}) copy-start(bf16[160,2048]{1,0:T(8,128)(2,1)} %copy-done.26) | copy-start | bytes 1966084
  441.6 7.8 %copy-start.29 = (bf16[160,2048]{1,0:T(8,128)(2,1)S(1)}, bf16[160,2048]{1,0:T(8,128)(2,1)}, u32[]{:S(2)}) copy-start(bf16[160,2048]{1,0:T(8,128)(2,1)} %copy-done.28) | copy-start | bytes 1966084
  449.4 32.4 %copy-start.17 = (bf16[256,2816]{1,0:T(8,128)(2,1)S(1)}, bf16[256,2816]{1,0:T(8,128)(2,1)}, u32[]{:S(2)}) copy-start(bf16[256,2816]{1,0:T(8,128)(2,1)} %reduce-scatter.6.cloned.1.call-done.refs_0_) | copy-start | bytes 4325380
  480.8 25.8 %copy-start.21 = (f32[160,2048]{1,0:T(8,128)S(1)}, f32[160,2048]{1,0:T(8,128)}, u32[]{:S(2)}) copy-start(f32[160,2048]{1,0:T(8,128)} %copy-done.20) | copy-start | bytes 3932164
  (31 other events, 51.5 us)
Sparse Core Ops, SparseCore 0:
  93.8 109.3 all-gather.2
  204.8 67.1 all-gather.4
  274.3 54.8 reduce-scatter.3
  331.4 107.4 reduce-scatter.5
  441.0 79.7 reduce-scatter.7
